TPU v7x, 32 devices: a whole 2x2x4 slice. The times are simulated.
32 devices in a mesh: dp: 4 (over z), ctx: 2 (over x), tensor: 4 (over y, core).
Axes of the slice: x: 2, y: 2, z: 4, core: 2. Of those that a mesh axis runs over, the one named last changes fastest.
Arguments:
- layer_input: bfloat16 [8, 2048, 1024], P('dp', 'ctx'), may hold values from -6 to 6
- cotangent: bfloat16 [8, 2048, 1024], P('dp', 'ctx'), may hold values from -6 to 6
- attn_gain: bfloat16 [1024], P('dp'), may hold values from 0.5 to 1.5
- query_weight: bfloat16 [1024, 1024], P('dp', 'tensor'), may hold values from -0.1875 to 0.1875
- key_weight: bfloat16 [1024, 512], P('dp', 'tensor'), may hold values from -0.1875 to 0.1875
- value_weight: bfloat16 [1024, 512], P('dp', 'tensor'), may hold values from -0.1875 to 0.1875
- query_gain: bfloat16 [64], P('dp'), may hold values from 1 to 2
- key_gain: bfloat16 [64], P('dp'), may hold values from 0.5 to 1.5
- out_weight: bfloat16 [1024, 1024], P('tensor', 'dp'), may hold values from -1.5 to 1.5
- ffn_gain: bfloat16 [1024], P('dp'), may hold values from 0.5 to 1.5
- gate_weight: bfloat16 [1024, 4608], P('dp', 'tensor'), may hold values from -0.1875 to 0.1875
- up_weight: bfloat16 [1024, 4608], P('dp', 'tensor'), may hold values from -0.1875 to 0.1875
- down_weight: bfloat16 [4608, 1024], P('tensor', 'dp'), may hold values from -0.09375 to 0.09375
Outputs:
- layer_output: bfloat16 [8, 2048, 1024], P('dp', 'ctx')
- input_grad: float32 [8, 2048, 1024], P('dp', 'ctx')
- attn_gain_grad: float32 [1024], P('dp')
- query_weight_grad: float32 [1024, 1024], P('dp', 'tensor')
- key_weight_grad: float32 [1024, 512], P('dp', 'tensor')
- value_weight_grad: float32 [1024, 512], P('dp', 'tensor')
- query_gain_grad: float32 [64], P('dp')
- key_gain_grad: float32 [64], P('dp')
- out_weight_grad: float32 [1024, 1024], P('tensor', 'dp')
- ffn_gain_grad: float32 [1024], P('dp')
- gate_weight_grad: float32 [1024, 4608], P('dp', 'tensor')
- up_weight_grad: float32 [1024, 4608], P('dp', 'tensor')
- down_weight_grad: float32 [4608, 1024], P('tensor', 'dp')
All inputs are finite; a program needn't handle non-finite values.
Results may differ from a plain program's by a relative error of at most 0.024.
Values may be sent and summed in bfloat16 or wider, within the bound.
No kernel may reach another device: no remote copies, remote signals or barrier semaphores. Data moves between devices by JAX's collectives and lax.ppermute only.
A program may use at most 320 MiB of HBM per device.

v0:
```python
import jax
import jax.numpy as jnp
from jax import lax
from jax.sharding import PartitionSpec as P

HD = 64
MICRO = 2


eps_norm = 1e-05
rope_base = 1000000.0


def rms_scale(field, norm_gain):
    return field * lax.rsqrt(jnp.mean(field * field, axis=-1, keepdims=True) + eps_norm) * norm_gain


def rope_tables(positions, head_width):
    frequency = rope_base ** (-jnp.arange(0, head_width, 2).astype(jnp.float32) / head_width)
    angles = positions.astype(jnp.float32)[:, None] * frequency[None, :]
    angles = jnp.concatenate([angles, angles], axis=-1)
    return (jnp.cos(angles), jnp.sin(angles))


def rotate(field, cosine_table, sine_table):
    half_width = field.shape[-1] // 2
    turned = jnp.concatenate([-field[..., half_width:], field[..., :half_width]], axis=-1)
    return field * cosine_table + turned * sine_table


def swiglu(gate_proj, up_proj):
    return jax.nn.silu(gate_proj) * up_proj


def reduce_first(gradients):
    return (
        lax.psum_scatter(gradients[0], ("dp", "ctx"), scatter_dimension=0, tiled=True),
        lax.psum_scatter(gradients[1], ("dp", "ctx"), scatter_dimension=0, tiled=True),
        lax.psum_scatter(gradients[2], ("dp", "ctx"), scatter_dimension=0, tiled=True),
        lax.psum_scatter(gradients[3], ("dp", "ctx"), scatter_dimension=0, tiled=True),
        lax.psum_scatter(gradients[4], ("dp", "ctx"), scatter_dimension=0, tiled=True),
        lax.psum_scatter(gradients[5], ("dp", "ctx"), scatter_dimension=0, tiled=True),
        lax.psum_scatter(gradients[6], ("dp", "ctx"), scatter_dimension=1, tiled=True),
        lax.psum_scatter(gradients[7], ("dp", "ctx"), scatter_dimension=0, tiled=True),
        lax.psum_scatter(gradients[8], ("dp", "ctx"), scatter_dimension=0, tiled=True),
        lax.psum_scatter(gradients[9], ("dp", "ctx"), scatter_dimension=0, tiled=True),
        lax.psum_scatter(gradients[10], ("dp", "ctx"), scatter_dimension=1, tiled=True),
    )


def finish_sum(gradients):
    return (
        lax.all_gather(gradients[0].astype(jnp.bfloat16), "ctx", axis=0, tiled=True).astype(
            jnp.float32
        ),
        lax.all_gather(gradients[1].astype(jnp.bfloat16), "ctx", axis=0, tiled=True).astype(
            jnp.float32
        ),
        lax.all_gather(gradients[2].astype(jnp.bfloat16), "ctx", axis=0, tiled=True).astype(
            jnp.float32
        ),
        lax.all_gather(gradients[3].astype(jnp.bfloat16), "ctx", axis=0, tiled=True).astype(
            jnp.float32
        ),
        lax.all_gather(gradients[4].astype(jnp.bfloat16), "ctx", axis=0, tiled=True).astype(
            jnp.float32
        ),
        lax.all_gather(gradients[5].astype(jnp.bfloat16), "ctx", axis=0, tiled=True).astype(
            jnp.float32
        ),
        lax.all_gather(gradients[6].astype(jnp.bfloat16), "ctx", axis=1, tiled=True).astype(
            jnp.float32
        ),
        lax.all_gather(gradients[7].astype(jnp.bfloat16), "ctx", axis=0, tiled=True).astype(
            jnp.float32
        ),
        lax.all_gather(gradients[8].astype(jnp.bfloat16), "ctx", axis=0, tiled=True).astype(
            jnp.float32
        ),
        lax.all_gather(gradients[9].astype(jnp.bfloat16), "ctx", axis=0, tiled=True).astype(
            jnp.float32
        ),
        lax.all_gather(gradients[10].astype(jnp.bfloat16), "ctx", axis=1, tiled=True).astype(
            jnp.float32
        ),
    )


def on_device(
    layer_input,
    cotangent,
    attn_gain,
    query_weight,
    key_weight,
    value_weight,
    query_gain,
    key_gain,
    out_weight,
    ffn_gain,
    gate_weight,
    up_weight,
    down_weight,
):
    seqs_dev, local_len, model_width = layer_input.shape
    per_batch = seqs_dev // MICRO
    tokens = per_batch * local_len
    local_heads = query_weight.shape[1] // HD
    local_kv = key_weight.shape[1] // HD
    group_size = local_heads // local_kv
    score_scale = HD ** (-0.5)
    ctx_place = lax.axis_index("ctx")
    positions = ctx_place * local_len + jnp.arange(local_len, dtype=jnp.int32)
    cosine_table, sine_table = rope_tables(positions, HD)
    cosine_table = cosine_table[:, None, :]
    sine_table = sine_table[:, None, :]
    stat_shape = (per_batch, local_kv, group_size, local_len)

    def norm_rope(field, norm_gain):
        return rotate(rms_scale(field, norm_gain), cosine_table, sine_table)

    outputs = []
    input_grads = []
    reduced = None
    for batch_index in range(MICRO):
        gathered = (
            lax.all_gather(attn_gain, "dp", axis=0, tiled=True),
            lax.all_gather(query_weight, "dp", axis=0, tiled=True),
            lax.all_gather(key_weight, "dp", axis=0, tiled=True),
            lax.all_gather(value_weight, "dp", axis=0, tiled=True),
            lax.all_gather(query_gain, "dp", axis=0, tiled=True),
            lax.all_gather(key_gain, "dp", axis=0, tiled=True),
            lax.all_gather(out_weight, "dp", axis=1, tiled=True),
            lax.all_gather(ffn_gain, "dp", axis=0, tiled=True),
            lax.all_gather(gate_weight, "dp", axis=0, tiled=True),
            lax.all_gather(up_weight, "dp", axis=0, tiled=True),
            lax.all_gather(down_weight, "dp", axis=1, tiled=True),
        )
        (
            full_attn_gain,
            full_query,
            full_key,
            full_value,
            full_qgain,
            full_kgain,
            full_out,
            full_ffn_gain,
            full_gate,
            full_up,
            full_down,
        ) = gathered
        first_seq = batch_index * per_batch
        inputs = layer_input[first_seq : first_seq + per_batch].astype(jnp.float32)
        flat_inputs = inputs.reshape(tokens, model_width)
        normed, attn_norm_back = jax.vjp(rms_scale, inputs, full_attn_gain.astype(jnp.float32))
        normed_low = normed.astype(jnp.bfloat16).reshape(tokens, model_width)
        query_proj = jnp.dot(normed_low, full_query, preferred_element_type=jnp.float32).reshape(
            per_batch, local_len, local_heads, HD
        )
        key_proj = jnp.dot(normed_low, full_key, preferred_element_type=jnp.float32).reshape(
            per_batch, local_len, local_kv, HD
        )
        value_low = (
            jnp.dot(normed_low, full_value, preferred_element_type=jnp.float32)
            .astype(jnp.bfloat16)
            .reshape(per_batch, local_len, local_kv * HD)
        )
        query_rot, query_back = jax.vjp(norm_rope, query_proj, full_qgain.astype(jnp.float32))
        key_rot, key_back = jax.vjp(norm_rope, key_proj, full_kgain.astype(jnp.float32))
        query_low = query_rot.astype(jnp.bfloat16).reshape(
            per_batch, local_len, local_kv, group_size, HD
        )
        key_low = key_rot.astype(jnp.bfloat16).reshape(per_batch, local_len, local_kv * HD)
        shard_piece = (
            lax.all_gather(key_low, "ctx", axis=1, tiled=True),
            lax.all_gather(value_low, "ctx", axis=1, tiled=True),
        )
        run_max = jnp.full(stat_shape, -1e30, jnp.float32)
        key_count = shard_piece[0].shape[1]
        key_rows = shard_piece[0].reshape(per_batch, key_count, local_kv, HD)
        value_rows = shard_piece[1].reshape(per_batch, key_count, local_kv, HD)
        scores = (
            jnp.einsum("sqkgd,snkd->skgqn", query_low, key_rows, preferred_element_type=jnp.float32)
            * score_scale
        )
        causal_mask = jnp.arange(key_count, dtype=jnp.int32)[None, :] <= positions[:, None]
        scores = jnp.where(causal_mask, scores, -1e30)
        new_max = jnp.maximum(run_max, jnp.max(scores, axis=-1))
        weights = jnp.where(causal_mask, jnp.exp(scores - new_max[..., None]), 0.0)
        run_sum = jnp.sum(weights, axis=-1)
        run_acc = jnp.einsum(
            "skgqn,snkd->skgqd",
            weights.astype(jnp.bfloat16),
            value_rows,
            preferred_element_type=jnp.float32,
        )
        run_max, run_sum, run_acc = (new_max, run_sum, run_acc)
        log_total = run_max + jnp.log(run_sum)
        attended_rows = (run_acc / run_sum[..., None]).transpose(0, 3, 1, 2, 4)
        attended_low = attended_rows.astype(jnp.bfloat16).reshape(tokens, local_heads * HD)
        attn_part = jnp.dot(attended_low, full_out, preferred_element_type=jnp.float32)
        attn_sum = lax.psum(attn_part.astype(jnp.bfloat16), "tensor").astype(jnp.float32)
        hidden = flat_inputs + attn_sum
        normed_ffn, ffn_norm_back = jax.vjp(rms_scale, hidden, full_ffn_gain.astype(jnp.float32))
        ffn_low = normed_ffn.astype(jnp.bfloat16)
        gate_proj = jnp.dot(ffn_low, full_gate, preferred_element_type=jnp.float32)
        up_proj = jnp.dot(ffn_low, full_up, preferred_element_type=jnp.float32)
        activated, swiglu_back = jax.vjp(swiglu, gate_proj, up_proj)
        act_low = activated.astype(jnp.bfloat16)
        ffn_part = jnp.dot(act_low, full_down, preferred_element_type=jnp.float32)
        ffn_sum = lax.psum(ffn_part.astype(jnp.bfloat16), "tensor").astype(jnp.float32)
        outputs.append(
            (hidden + ffn_sum).astype(jnp.bfloat16).reshape(per_batch, local_len, model_width)
        )
        seq_cot = cotangent[first_seq : first_seq + per_batch].reshape(tokens, model_width)
        down_wgrad = jnp.einsum("rf,rd->fd", act_low, seq_cot, preferred_element_type=jnp.float32)
        act_grad = jnp.einsum("rd,fd->rf", seq_cot, full_down, preferred_element_type=jnp.float32)
        gate_grad, up_grad = swiglu_back(act_grad)
        gate_glow = gate_grad.astype(jnp.bfloat16)
        up_glow = up_grad.astype(jnp.bfloat16)
        gate_wgrad = jnp.einsum("rd,rf->df", ffn_low, gate_glow, preferred_element_type=jnp.float32)
        up_wgrad = jnp.einsum("rd,rf->df", ffn_low, up_glow, preferred_element_type=jnp.float32)
        ffn_in_part = jnp.einsum(
            "rf,df->rd", gate_glow, full_gate, preferred_element_type=jnp.float32
        ) + jnp.einsum("rf,df->rd", up_glow, full_up, preferred_element_type=jnp.float32)
        ffn_in_grad = lax.psum(ffn_in_part.astype(jnp.bfloat16), "tensor").astype(jnp.float32)
        hidden_part, ffn_gain_grad = ffn_norm_back(ffn_in_grad)
        hidden_grad = seq_cot.astype(jnp.float32) + hidden_part
        hidden_low = hidden_grad.astype(jnp.bfloat16)
        out_wgrad = jnp.einsum(
            "rh,rd->hd", attended_low, hidden_low, preferred_element_type=jnp.float32
        )
        attended_grad = (
            jnp.einsum("rd,hd->rh", hidden_low, full_out, preferred_element_type=jnp.float32)
            .astype(jnp.bfloat16)
            .reshape(per_batch, local_len, local_kv, group_size, HD)
        )
        row_delta = jnp.sum(attended_grad.astype(jnp.float32) * attended_rows, axis=-1).transpose(
            0, 2, 3, 1
        )
        attend_shard_piece = (
            lax.all_gather(key_low, "ctx", axis=1, tiled=True),
            lax.all_gather(value_low, "ctx", axis=1, tiled=True),
        )
        attend_key_count = attend_shard_piece[0].shape[1]
        attend_key_rows = attend_shard_piece[0].reshape(per_batch, attend_key_count, local_kv, HD)
        attend_value_rows = attend_shard_piece[1].reshape(per_batch, attend_key_count, local_kv, HD)
        attend_scores = (
            jnp.einsum(
                "sqkgd,snkd->skgqn", query_low, attend_key_rows, preferred_element_type=jnp.float32
            )
            * score_scale
        )
        attend_causal_mask = (
            jnp.arange(attend_key_count, dtype=jnp.int32)[None, :] <= positions[:, None]
        )
        probabilities = jnp.where(
            attend_causal_mask,
            jnp.exp(jnp.where(attend_causal_mask, attend_scores, -1e30) - log_total[..., None]),
            0.0,
        )
        prob_grad = jnp.einsum(
            "sqkgd,snkd->skgqn",
            attended_grad,
            attend_value_rows,
            preferred_element_type=jnp.float32,
        )
        score_grad = (probabilities * (prob_grad - row_delta[..., None])).astype(jnp.bfloat16)
        query_acc = score_scale * jnp.einsum(
            "skgqn,snkd->sqkgd", score_grad, attend_key_rows, preferred_element_type=jnp.float32
        )
        key_piece = score_scale * jnp.einsum(
            "skgqn,sqkgd->snkd", score_grad, query_low, preferred_element_type=jnp.float32
        ).reshape(per_batch, attend_key_count, local_kv * HD)
        value_piece = jnp.einsum(
            "skgqn,sqkgd->snkd",
            probabilities.astype(jnp.bfloat16),
            attended_grad,
            preferred_element_type=jnp.float32,
        ).reshape(per_batch, attend_key_count, local_kv * HD)
        key_acc = key_piece
        value_acc = value_piece
        query_acc, key_acc, value_acc = (query_acc, key_acc, value_acc)
        key_grad, value_grad = (
            lax.psum_scatter(
                key_acc.astype(jnp.bfloat16), "ctx", scatter_dimension=1, tiled=True
            ).astype(jnp.float32),
            lax.psum_scatter(
                value_acc.astype(jnp.bfloat16), "ctx", scatter_dimension=1, tiled=True
            ).astype(jnp.float32),
        )
        query_raw, qgain_grad = query_back(query_acc.reshape(per_batch, local_len, local_heads, HD))
        key_raw, kgain_grad = key_back(key_grad.reshape(per_batch, local_len, local_kv, HD))
        query_glow = query_raw.astype(jnp.bfloat16).reshape(tokens, local_heads * HD)
        key_glow = key_raw.astype(jnp.bfloat16).reshape(tokens, local_kv * HD)
        value_glow = value_grad.astype(jnp.bfloat16).reshape(tokens, local_kv * HD)
        query_wgrad = jnp.einsum(
            "rd,rh->dh", normed_low, query_glow, preferred_element_type=jnp.float32
        )
        key_wgrad = jnp.einsum(
            "rd,rh->dh", normed_low, key_glow, preferred_element_type=jnp.float32
        )
        value_wgrad = jnp.einsum(
            "rd,rh->dh", normed_low, value_glow, preferred_element_type=jnp.float32
        )
        attn_in_part = (
            jnp.einsum("rh,dh->rd", query_glow, full_query, preferred_element_type=jnp.float32)
            + jnp.einsum("rh,dh->rd", key_glow, full_key, preferred_element_type=jnp.float32)
            + jnp.einsum("rh,dh->rd", value_glow, full_value, preferred_element_type=jnp.float32)
        )
        attn_in_grad, qgain_sum, kgain_sum = (
            lax.psum(attn_in_part.astype(jnp.bfloat16), "tensor").astype(jnp.float32),
            lax.psum(qgain_grad.astype(jnp.bfloat16), "tensor").astype(jnp.float32),
            lax.psum(kgain_grad.astype(jnp.bfloat16), "tensor").astype(jnp.float32),
        )
        input_part, attn_gain_grad = attn_norm_back(
            attn_in_grad.reshape(per_batch, local_len, model_width)
        )
        input_grads.append(hidden_grad.reshape(per_batch, local_len, model_width) + input_part)
        gradients = (
            attn_gain_grad,
            query_wgrad,
            key_wgrad,
            value_wgrad,
            qgain_sum,
            kgain_sum,
            out_wgrad,
            ffn_gain_grad,
            gate_wgrad,
            up_wgrad,
            down_wgrad,
        )
        shares = reduce_first(gradients)
        reduced = shares if reduced is None else jax.tree.map(jnp.add, reduced, shares)
    finals = finish_sum(reduced)
    return (
        jnp.concatenate(outputs, axis=0),
        jnp.concatenate(input_grads, axis=0),
        finals[0],
        finals[1],
        finals[2],
        finals[3],
        finals[4],
        finals[5],
        finals[6],
        finals[7],
        finals[8],
        finals[9],
        finals[10],
    )


def solution(mesh):
    placed = (
        P("dp", "ctx", None),
        P("dp", "ctx", None),
        P("dp"),
        P("dp", "tensor"),
        P("dp", "tensor"),
        P("dp", "tensor"),
        P("dp"),
        P("dp"),
        P("tensor", "dp"),
        P("dp"),
        P("dp", "tensor"),
        P("dp", "tensor"),
        P("tensor", "dp"),
    )
    return jax.shard_map(
        on_device,
        mesh=mesh,
        in_specs=placed,
        out_specs=(
            P("dp", "ctx", None),
            P("dp", "ctx", None),
            P("dp"),
            P("dp", "tensor"),
            P("dp", "tensor"),
            P("dp", "tensor"),
            P("dp"),
            P("dp"),
            P("tensor", "dp"),
            P("dp"),
            P("dp", "tensor"),
            P("dp", "tensor"),
            P("tensor", "dp"),
        ),
        check_vma=False,
    )
```

profile of v0, /device:TPU:0, one launch (start us, length us, event | category | flops | bytes accessed | tf_op | source)
XLA Modules:
  0.0 1400.1 jit_solution(7189450635703364267)
XLA Ops:
  9.0 12.7 all-gather.4
  25.4 13.9 all_gather.94
  39.3 14.3 %all_gather.99 = bf16[1024,128]{1,0:T(8,128)(2,1)S(1)} all-gather(bf16[256,128]{1,0:T(8,128)(2,1)S(1)} %copy-done.95), channel_id=1, replica_groups=mesh['dp'=4,'ctx'=2,'tensor'=4] {'dp'}, dimensions={0}, use_global_device_ids=true | all-gather | bytes 327680 | tf_op jit(solution)/shard_map/all_gather | solution.py:129
  58.2 14.9 %all_gather.97 = bf16[1024,256]{1,0:T(8,128)(2,1)S(1)} all-gather(bf16[256,256]{1,0:T(8,128)(2,1)S(1)} %copy-done.89), channel_id=1, replica_groups=mesh['dp'=4,'ctx'=2,'tensor'=4] {'dp'}, dimensions={0}, use_global_device_ids=true | all-gather | bytes 655360 | tf_op jit(solution)/shard_map/all_gather | solution.py:127
  76.8 8.6 all-reduce.21
  85.5 7.1 all-gather.3
  96.5 14.9 %all_gather.101 = bf16[256,1024]{1,0:T(8,128)(2,1)S(1)} all-gather(bf16[256,256]{1,0:T(8,128)(2,1)} %param.21), channel_id=1, replica_groups=mesh['dp'=4,'ctx'=2,'tensor'=4] {'dp'}, dimensions={1}, use_global_device_ids=true | all-gather | bytes 655360 | tf_op jit(solution)/shard_map/all_gather | solution.py:132
  114.8 10.2 all-gather.1
  130.4 7.0 all-gather
  137.4 7.3 all-gather.2
  147.0 13.7 fusion.10
  160.8 26.8 %fusion.4 = (f32[2,2,1024]{2,1,0:T(2,128)S(1)}, f32[2,2,1024]{2,1,0:T(2,128)S(1)}, f32[2,2048,1024,2]{2,1,3,0:T(8,128)}) fusion(f32[2,2048,1024,2]{2,1,3,0:T(8,128)} %get-tuple-element.115, f32[2,2,1024]{2,1,0:T(2,128)S(1)} %broadcast_maximum_fusion.1, pred[1024,2048]{0,1:T(8,128)(4,1)S(1)} %copy-done.36, bf16[2048,2,64,1]{0,2,3,1:T(8,128)(2,1)S(1)} %bitcast.519, ...), kind=kOutput, calls=%fused_computation.12 | convolution fusion | flops 1140842496 | bytes 70303744 | tf_op jit(solution)/shard_map/sqkgd,snkd->skgqn/dot_general | solution.py:182
  187.7 15.0 %fusion.6 = f32[2,2,1024]{2,1,0:T(2,128)S(1)} fusion(f32[2,2048,1024,2]{2,1,3,0:T(8,128)} %get-tuple-element.116, f32[2,2,1024]{2,1,0:T(2,128)S(1)} %broadcast_maximum_fusion, pred[1024,2048]{0,1:T(8,128)(4,1)S(1)} %copy-done.36), kind=kLoop, calls=%fused_computation.14 | loop fusion | flops 41938944 | bytes 35684352 | tf_op jit(solution)/shard_map/reduce_sum | solution.py:189
  202.7 15.7 %bitcast_convert_fusion = (bf16[1,1024,2,2,64]{1,4,3,2,0:T(8,128)(2,1)S(1)}, f32[2,2,1024,64]{2,3,1,0:T(8,128)}) fusion(f32[2,2,1024]{2,1,0:T(2,128)S(1)} %fusion.6, bf16[2048,2,64,1]{0,2,3,1:T(8,128)(2,1)S(1)} %bitcast.545, f32[2,2048,1024,2]{2,1,3,0:T(8,128)} %get-tuple-element.116, f32[2,2,1024]{2,1,0:T(2,128)S(1)} %broadcast_maximum_fusion, ...), kind=kOutput, calls=%fused_computation.177 | convolution fusion | flops 1116209152 | bytes 37781504 | tf_op jit(solution)/shard_map/skgqn,snkd->skgqd/dot_general | solution.py:190
  218.5 24.8 %bitcast_convert_fusion.1 = (bf16[1,1024,2,2,64]{1,4,3,2,0:T(8,128)(2,1)S(1)}, f32[2,2,1024,64]{2,3,1,0:T(8,128)}) fusion(f32[2,2,1024]{2,1,0:T(2,128)S(1)} %get-tuple-element.33, bf16[2048,2,64,1]{0,2,3,1:T(8,128)(2,1)S(1)} %bitcast.548, f32[2,2048,1024,2]{2,1,3,0:T(8,128)} %get-tuple-element.115, f32[2,2,1024]{2,1,0:T(2,128)S(1)} %broadcast_maximum_fusion.1, ...), kind=kOutput, calls=%fused_computation.182 | convolution fusion | flops 1116209152 | bytes 37781504 | tf_op jit(solution)/shard_map/skgqn,snkd->skgqd/dot_general | solution.py:190
  249.3 9.7 all-gather.5
  259.0 73.2 %all-reduce.31.cloned.1.call-done = (bf16[1024,1024]{1,0:T(8,128)(2,1)}, bf16[1024,1024]{1,0:T(8,128)(2,1)}) async-done(((bf16[1024,1024]{1,0:T(8,128)(2,1)}, bf16[1024,1024]{1,0:T(8,128)(2,1)}), (bf16[1024,1024]{1,0:T(8,128)(2,1)}, bf16[1024,1024]{1,0:T(8,128)(2,1)})) %all-reduce.31.cloned.1.call-update) | async-done | bytes 4194320 | tf_op jit(solution)/shard_map/psum | solution.py:201
  341.3 7.5 fusion.183
  348.8 7.5 fusion.182
  365.6 33.6 %all-gather.16.cloned.1.call-done = bf16[1152,1024]{1,0:T(8,128)(2,1)} async-done(((bf16[1152,256]{1,0:T(8,128)(2,1)}), bf16[1152,1024]{1,0:T(8,128)(2,1)}) %all-gather.16.cloned.1.call-update) | async-done | bytes 2359312 | tf_op jit(solution)/shard_map/all_gather | solution.py:136
  399.3 10.9 multiply_convert_fusion.1
  414.6 8.1 multiply_convert_fusion
  435.2 6.8 convolution_convert_fusion.1
  446.0 72.4 %all-reduce.29.cloned.1.call-done = (bf16[1024,1024]{1,0:T(8,128)(2,1)}, bf16[1024,1024]{1,0:T(8,128)(2,1)}) async-done(((bf16[1024,1024]{1,0:T(8,128)(2,1)}, bf16[1024,1024]{1,0:T(8,128)(2,1)}), (bf16[1024,1024]{1,0:T(8,128)(2,1)}, bf16[1024,1024]{1,0:T(8,128)(2,1)})) %all-reduce.29.cloned.1.call-update) | async-done | bytes 4194320 | tf_op jit(solution)/shard_map/psum | solution.py:225
  518.4 7.4 fusion.58
  535.2 17.1 %fusion.80 = bf16[2,64,2048]{2,1,0:T(8,128)(2,1)} fusion(bf16[1024,2,2,64]{0,3,2,1:T(8,128)(2,1)} %bitcast.531, f32[2,2048,1024,2]{2,1,3,0:T(8,128)} %get-tuple-element.115, f32[2,2,1024]{2,1,0:T(2,128)S(1)} %log_add_fusion.1, pred[1024,2048]{0,1:T(8,128)(4,1)S(1)} %copy-done.38), kind=kOutput, calls=%fused_computation.128 | convolution fusion | flops 1115947008 | bytes 36716544 | tf_op jit(solution)/shard_map/skgqn,sqkgd->snkd/dot_general | solution.py:274
  552.3 20.9 %fusion.16 = bf16[2,2,1024,2048]{2,3,1,0:T(8,128)(2,1)} fusion(f32[2,2048,1024,2]{2,1,3,0:T(8,128)} %get-tuple-element.115, f32[2,2,1024]{2,1,0:T(2,128)S(1)} %bitcast.564, f32[2,2,1024]{2,1,0:T(2,128)S(1)} %log_add_fusion.1, pred[1024,2048]{0,1:T(8,128)(4,1)S(1)} %copy-done.38, bf16[2048,2,64,1]{0,2,3,1:T(8,128)(2,1)} %bitcast.547, ...), kind=kOutput, calls=%fused_computation.24 | convolution fusion | flops 1132462080 | bytes 53510144 | tf_op jit(solution)/shard_map/sqkgd,snkd->skgqn/dot_general | solution.py:261
  573.3 15.9 %fusion.83 = bf16[2,64,2048]{2,1,0:T(8,128)(2,1)} fusion(bf16[1024,2,2,64]{0,3,2,1:T(8,128)(2,1)S(1)} %bitcast.527, f32[2,2048,1024,2]{2,1,3,0:T(8,128)} %get-tuple-element.116, f32[2,2,1024]{2,1,0:T(2,128)S(1)} %log_add_fusion, pred[1024,2048]{0,1:T(8,128)(4,1)S(1)} %copy-done.38), kind=kOutput, calls=%fused_computation.129 | convolution fusion | flops 1115947008 | bytes 36716544 | tf_op jit(solution)/shard_map/skgqn,sqkgd->snkd/dot_general | solution.py:274
  590.6 21.1 %fusion.17 = bf16[2,2,1024,2048]{2,3,1,0:T(8,128)(2,1)} fusion(f32[2,2048,1024,2]{2,1,3,0:T(8,128)} %get-tuple-element.116, f32[2,2,1024]{2,1,0:T(2,128)S(1)} %bitcast.563, f32[2,2,1024]{2,1,0:T(2,128)S(1)} %log_add_fusion, pred[1024,2048]{0,1:T(8,128)(4,1)S(1)} %copy-done.38, bf16[2048,2,64,1]{0,2,3,1:T(8,128)(2,1)S(1)} %bitcast.546, ...), kind=kOutput, calls=%fused_computation.25 | convolution fusion | flops 1132462080 | bytes 53510144 | tf_op jit(solution)/shard_map/sqkgd,snkd->skgqn/dot_general | solution.py:261
  611.7 11.8 fusion.79
  624.0 8.8 convolution_multiply_fusion.1
  632.9 12.3 fusion.78
  645.2 10.1 convolution_multiply_fusion
  705.1 5.5 fusion.195
  729.0 5.8 all-reduce.17
  740.9 49.0 %reduce-scatter.22.cloned.1.call-done = f32[128,128]{1,0:T(8,128)} async-done(((f32[1024,128]{1,0:T(8,128)}), f32[128,128]{1,0:T(8,128)}) %reduce-scatter.22.cloned.1.call-update) | async-done | bytes 65552 | tf_op jit(solution)/shard_map/reduce_scatter | solution.py:39
  796.0 60.2 %reduce-scatter.26.cloned.1.call-done = f32[256,128]{1,0:T(8,128)} async-done(((f32[256,1024]{1,0:T(8,128)}), f32[256,128]{1,0:T(8,128)}) %reduce-scatter.26.cloned.1.call-update) | async-done | bytes 131088 | tf_op jit(solution)/shard_map/reduce_scatter | solution.py:43
  862.8 60.1 %reduce-scatter.20.cloned.1.call-done = f32[128,256]{1,0:T(8,128)} async-done(((f32[1024,256]{1,0:T(8,128)}), f32[128,256]{1,0:T(8,128)}) %reduce-scatter.20.cloned.1.call-update) | async-done | bytes 131088 | tf_op jit(solution)/shard_map/reduce_scatter | solution.py:38
  928.8 149.8 %all-reduce.27.cloned.1.call-done = (bf16[1024,1024]{1,0:T(8,128)(2,1)}, bf16[1024,1024]{1,0:T(8,128)(2,1)}, bf16[1024,1024]{1,0:T(8,128)(2,1)}, bf16[1024,1024]{1,0:T(8,128)(2,1)}) async-done(((bf16[1024,1024]{1,0:T(8,128)(2,1)}, bf16[1024,1024]{1,0:T(8,128)(2,1)}, bf16[1024,1024]{1,0:T(8,128)(2,1)}, bf16[1024,1024]{1,0:T(8,128)(2,1)}), (bf16[1024,1024]{1,0:T(8,128)(2,1)}, bf16[1024,1024]{1,0:T(8,128)(2,1)}, ...) | async-done | bytes 8388624 | tf_op jit(solution)/shard_map/psum | solution.py:210
  1078.6 5.8 fusion.53
  1084.5 39.1 %all-reduce.16 = (bf16[1024]{0:T(1024)(128)(2,1)S(1)}, bf16[64]{0:T(256)(128)(2,1)S(1)}, bf16[64]{0:T(256)(128)(2,1)S(1)}, bf16[1024]{0:T(1024)(128)(2,1)S(1)}) all-reduce(f32[1024]{0:T(1024)S(1)} %add.368, f32[64]{0:T(128)S(1)} %get-tuple-element.124, ...), channel_id=21, replica_groups=mesh['dp'=4,'ctx'=2,'tensor'=4] {'dp','ctx'}, use_global_device_ids=true, to_apply=%region_35.36.clone | all-reduce | flops 2176 | bytes 13056
  1140.6 5.8 fusion.86
  1158.4 19.8 %reduce-scatter.28.cloned.1.call-done = f32[128,1152]{1,0:T(8,128)} async-done(((f32[1024,1152]{1,0:T(8,128)}), f32[128,1152]{1,0:T(8,128)}) %reduce-scatter.28.cloned.1.call-update) | async-done | bytes 589840 | tf_op jit(solution)/shard_map/reduce_scatter | solution.py:45
  1179.3 97.6 %reduce-scatter.30.cloned.1.call-done = f32[128,1152]{1,0:T(8,128)} async-done(((f32[1024,1152]{1,0:T(8,128)}), f32[128,1152]{1,0:T(8,128)}) %reduce-scatter.30.cloned.1.call-update) | async-done | bytes 589840 | tf_op jit(solution)/shard_map/reduce_scatter | solution.py:46
  1278.0 9.4 all_gather.117
  1287.3 14.6 %all_gather.116 = bf16[256,1152]{1,0:T(8,128)(2,1)S(1)} all-gather(bf16[128,1152]{1,0:T(8,128)(2,1)S(1)} %convert_element_type.524), channel_id=1, replica_groups=mesh['dp'=4,'ctx'=2,'tensor'=4] {'ctx'}, dimensions={0}, use_global_device_ids=true | all-gather | bytes 884736 | tf_op jit(solution)/shard_map/all_gather | solution.py:77
  1301.9 76.6 %reduce-scatter.32.cloned.1.call-done = f32[1152,128]{1,0:T(8,128)} async-done(((f32[1152,1024]{1,0:T(8,128)}), f32[1152,128]{1,0:T(8,128)}) %reduce-scatter.32.cloned.1.call-update) | async-done | bytes 589840 | tf_op jit(solution)/shard_map/reduce_scatter | solution.py:47
  1379.6 9.4 all_gather.118
  (459 shorter events, 209.0 us)
Async XLA Ops:
  8.0 17.4 %copy-start.94 = (bf16[256,128]{1,0:T(8,128)(2,1)S(1)}, bf16[256,128]{1,0:T(8,128)(2,1)}, u32[]{:S(2)}) copy-start(bf16[256,128]{1,0:T(8,128)(2,1)} %param.17) | copy-start | bytes 196612
  8.0 31.3 %copy-start.95 = (bf16[256,128]{1,0:T(8,128)(2,1)S(1)}, bf16[256,128]{1,0:T(8,128)(2,1)}, u32[]{:S(2)}) copy-start(bf16[256,128]{1,0:T(8,128)(2,1)} %param.18) | copy-start | bytes 196612
  8.0 324.1 %all-reduce.31.cloned.1.call-start = ((), (), s32[]{:S(2)}) async-start(), calls=%async_computation.27 | async-start | bytes 8388608 | tf_op jit(solution)/shard_map/psum | solution.py:201
  8.1 45.5 %copy-start = (bf16[2,1024,1024]{2,1,0:T(8,128)(2,1)S(1)}, bf16[2,1024,1024]{2,1,0:T(8,128)(2,1)}, u32[]{:S(2)}) copy-start(bf16[2,1024,1024]{2,1,0:T(8,128)(2,1)} %param.13) | copy-start | bytes 12582916
  21.7 51.4 %copy-start.98 = (f32[4,1,256]{2,1,0:T(1,128)}, f32[4,1,256]{2,1,0:T(1,128)S(1)}, u32[]{:S(2)}) copy-start(f32[4,1,256]{2,1,0:T(1,128)S(1)} %convert_element_type.532) | copy-start | bytes 12292
  24.8 29.6 %copy-start.104 = (f32[1024]{0:T(1024)}, f32[1024]{0:T(1024)S(1)}, u32[]{:S(2)}) copy-start(f32[1024]{0:T(1024)S(1)} %get-tuple-element.27) | copy-start | bytes 12292
  25.4 47.7 %copy-start.102 = (f32[1024]{0:T(1024)}, f32[1024]{0:T(1024)S(1)}, u32[]{:S(2)}) copy-start(f32[1024]{0:T(1024)S(1)} %fusion.149) | copy-start | bytes 12292
  25.4 29.9 %copy-start.100 = (f32[1024]{0:T(1024)}, f32[1024]{0:T(1024)S(1)}, u32[]{:S(2)}) copy-start(f32[1024]{0:T(1024)S(1)} %fusion.147) | copy-start | bytes 12292
  39.3 18.0 %copy-start.51 = (bf16[1024,128]{1,0:T(8,128)(2,1)}, bf16[1024,128]{1,0:T(8,128)(2,1)S(1)}, u32[]{:S(2)}) copy-start(bf16[1024,128]{1,0:T(8,128)(2,1)S(1)} %all_gather.94) | copy-start | bytes 786436
  55.3 41.1 %copy-start.25 = (f32[1024,128]{0,1:T(8,128)}, f32[1024,128]{0,1:T(8,128)S(1)}, u32[]{:S(2)}) copy-start(f32[1024,128]{0,1:T(8,128)S(1)} %fusion.172) | copy-start | bytes 1572868
  55.9 18.2 %copy-start.6 = (bf16[1024,1024]{1,0:T(8,128)(2,1)}, bf16[1024,1024]{1,0:T(8,128)(2,1)S(1)}, u32[]{:S(2)}) copy-start(bf16[1024,1024]{1,0:T(8,128)(2,1)S(1)} %fusion.88) | copy-start | bytes 6291460
  58.2 71.8 %copy-start.23 = (f32[1024,128]{0,1:T(8,128)}, f32[1024,128]{0,1:T(8,128)S(1)}, u32[]{:S(2)}) copy-start(f32[1024,128]{0,1:T(8,128)S(1)} %fusion.180) | copy-start | bytes 1572868
  74.1 71.4 %copy-start.21 = (f32[1024,256]{0,1:T(8,128)}, f32[1024,256]{0,1:T(8,128)S(1)}, u32[]{:S(2)}) copy-start(f32[1024,256]{0,1:T(8,128)S(1)} %fusion.170) | copy-start | bytes 3145732
  74.9 70.6 %copy-start.18 = (f32[1024,256]{0,1:T(8,128)}, f32[1024,256]{0,1:T(8,128)S(1)}, u32[]{:S(2)}) copy-start(f32[1024,256]{0,1:T(8,128)S(1)} %fusion.181) | copy-start | bytes 3145732
  85.4 60.1 %copy-start.110 = (f32[64]{0:T(128)}, f32[64]{0:T(128)S(1)}, u32[]{:S(2)}) copy-start(f32[64]{0:T(128)S(1)} %convert_element_type.426) | copy-start | bytes 772
  85.4 43.1 %copy-start.112 = (f32[64]{0:T(128)}, f32[64]{0:T(128)S(1)}, u32[]{:S(2)}) copy-start(f32[64]{0:T(128)S(1)} %convert_element_type.421) | copy-start | bytes 772
  96.4 49.1 %copy-start.28 = (f32[1024,64]{0,1:T(8,128)}, f32[1024,64]{0,1:T(8,128)S(1)}, u32[]{:S(2)}) copy-start(f32[1024,64]{0,1:T(8,128)S(1)} %get-tuple-element.106) | copy-start | bytes 786436
  96.5 33.5 %copy-start.81 = (f32[1024,2]{0,1:T(2,128)}, f32[1024,2]{0,1:T(2,128)S(1)}, u32[]{:S(2)}) copy-start(f32[1024,2]{0,1:T(2,128)S(1)} %fusion.146) | copy-start | bytes 24580
  111.6 16.1 %copy-start.85 = (f32[1024,4]{0,1:T(4,128)}, f32[1024,4]{0,1:T(4,128)S(1)}, u32[]{:S(2)}) copy-start(f32[1024,4]{0,1:T(4,128)S(1)} %multiply_reduce_fusion.6) | copy-start | bytes 49156
  111.6 33.1 %copy-start.76 = (f32[1024,4]{0,1:T(4,128)}, f32[1024,4]{0,1:T(4,128)S(1)}, u32[]{:S(2)}) copy-start(f32[1024,4]{0,1:T(4,128)S(1)} %fusion.144) | copy-start | bytes 49156
  128.4 16.3 %copy-start.78 = (f32[1024,4]{0,1:T(4,128)}, f32[1024,4]{0,1:T(4,128)S(1)}, u32[]{:S(2)}) copy-start(f32[1024,4]{0,1:T(4,128)S(1)} %fusion.143) | copy-start | bytes 49156
  144.7 16.0 %copy-start.46 = (bf16[2048,128]{0,1:T(8,128)(2,1)}, bf16[2048,128]{0,1:T(8,128)(2,1)S(1)}, u32[]{:S(2)}) copy-start(bf16[2048,128]{0,1:T(8,128)(2,1)S(1)} %all-gather.2) | copy-start | bytes 1572868
  160.7 26.9 %copy-start.96 = (f32[2,2,1024]{2,1,0:T(2,128)}, f32[2,2,1024]{2,1,0:T(2,128)S(1)}, u32[]{:S(2)}) copy-start(f32[2,2,1024]{2,1,0:T(2,128)S(1)} %get-tuple-element.114) | copy-start | bytes 49156
  202.7 15.8 %copy-start.75 = (bf16[2048,128]{0,1:T(8,128)(2,1)S(1)}, bf16[2048,128]{0,1:T(8,128)(2,1)}, u32[]{:S(2)}) copy-start(bf16[2048,128]{0,1:T(8,128)(2,1)} %copy.48) | copy-start | bytes 1572868
  218.5 26.9 %copy-start.65 = (bf16[1,1024,2,2,64]{1,4,3,2,0:T(8,128)(2,1)}, bf16[1,1024,2,2,64]{1,4,3,2,0:T(8,128)(2,1)S(1)}, u32[]{:S(2)}) copy-start(bf16[1,1024,2,2,64]{1,4,3,2,0:T(8,128)(2,1)S(1)} %get-tuple-element.117) | copy-start | bytes 1572868
  247.5 93.8 %all-gather.14.cloned.1.call-start = ((), (), s32[]{:S(2)}) async-start(), calls=%async_computation.12 | async-start | bytes 2949120 | tf_op jit(solution)/shard_map/all_gather | solution.py:135
  248.1 100.7 %all-gather.12.cloned.1.call-start = ((), (), s32[]{:S(2)}) async-start(), calls=%async_computation.11 | async-start | bytes 2949120 | tf_op jit(solution)/shard_map/all_gather | solution.py:134
  248.6 150.6 %all-gather.16.cloned.1.call-start = ((), (), s32[]{:S(2)}) async-start(), calls=%async_computation.13 | async-start | bytes 2949120 | tf_op jit(solution)/shard_map/all_gather | solution.py:136
  249.2 269.2 %all-reduce.29.cloned.1.call-start = ((), (), s32[]{:S(2)}) async-start(), calls=%async_computation.26 | async-start | bytes 8388608 | tf_op jit(solution)/shard_map/psum | solution.py:225
  434.4 220.9 %reduce-scatter.14.cloned.1.call-start = ((), (), s32[]{:S(2)}) async-start(), calls=%async_computation.15 | async-start | bytes 786432 | tf_op jit(solution)/shard_map/reduce_scatter | solution.py:287
  534.8 54.4 %copy-start.61 = (bf16[1024,256]{0,1:T(8,128)(2,1)}, bf16[1024,256]{0,1:T(8,128)(2,1)S(1)}, u32[]{:S(2)}) copy-start(bf16[1024,256]{0,1:T(8,128)(2,1)S(1)} %convolution_convert_fusion.4) | copy-start | bytes 1572868
  535.2 17.1 %copy-start.63 = (bf16[1024,256]{0,1:T(8,128)(2,1)S(1)}, bf16[1024,256]{0,1:T(8,128)(2,1)}, u32[]{:S(2)}) copy-start(bf16[1024,256]{0,1:T(8,128)(2,1)} %copy-done.62) | copy-start | bytes 1572868
  573.2 84.6 %reduce-scatter.18.cloned.1.call-start = ((), (), s32[]{:S(2)}) async-start(), calls=%async_computation.17 | async-start | bytes 786432 | tf_op jit(solution)/shard_map/reduce_scatter | solution.py:287
  573.3 17.4 %copy-start.74 = (bf16[2048,128]{0,1:T(8,128)(2,1)S(1)}, bf16[2048,128]{0,1:T(8,128)(2,1)}, u32[]{:S(2)}) copy-start(bf16[2048,128]{0,1:T(8,128)(2,1)} %copy.50) | copy-start | bytes 1572868
  590.6 71.2 %reduce-scatter.12.cloned.1.call-start = ((), (), s32[]{:S(2)}) async-start(), calls=%async_computation.14 | async-start | bytes 786432 | tf_op jit(solution)/shard_map/reduce_scatter | solution.py:284
  590.6 21.1 %copy-start.43 = (bf16[1024,2,2,64]{0,3,2,1:T(8,128)(2,1)S(1)}, bf16[1024,2,2,64]{0,3,2,1:T(8,128)(2,1)}, u32[]{:S(2)}) copy-start(bf16[1024,2,2,64]{0,3,2,1:T(8,128)(2,1)} %copy-done.42) | copy-start | bytes 1572868
  623.6 38.2 %reduce-scatter.16.cloned.1.call-start = ((), (), s32[]{:S(2)}) async-start(), calls=%async_computation.16 | async-start | bytes 786432 | tf_op jit(solution)/shard_map/reduce_scatter | solution.py:284
  632.9 36.4 %copy-start.20 = (f32[2,64,2,1024]{3,1,2,0:T(8,128)}, f32[2,64,2,1024]{3,1,2,0:T(8,128)S(1)}, u32[]{:S(2)}) copy-start(f32[2,64,2,1024]{3,1,2,0:T(8,128)S(1)} %convolution_multiply_fusion.1) | copy-start | bytes 3145732
  645.1 89.6 %reduce-scatter.24.cloned.1.call-start = ((), (), s32[]{:S(2)}) async-start(), calls=%async_computation.20 | async-start | bytes 589824 | tf_op jit(solution)/shard_map/reduce_scatter | solution.py:40
  661.5 128.4 %reduce-scatter.22.cloned.1.call-start = ((), (), s32[]{:S(2)}) async-start(), calls=%async_computation.19 | async-start | bytes 589824 | tf_op jit(solution)/shard_map/reduce_scatter | solution.py:39
  669.2 187.1 %reduce-scatter.26.cloned.1.call-start = ((), (), s32[]{:S(2)}) async-start(), calls=%async_computation.21 | async-start | bytes 1179648 | tf_op jit(solution)/shard_map/reduce_scatter | solution.py:43
  676.5 246.5 %reduce-scatter.20.cloned.1.call-start = ((), (), s32[]{:S(2)}) async-start(), calls=%async_computation.18 | async-start | bytes 1179648 | tf_op jit(solution)/shard_map/reduce_scatter | solution.py:38
  685.9 392.7 %all-reduce.27.cloned.1.call-start = ((), (), s32[]{:S(2)}) async-start(), calls=%async_computation.25 | async-start | bytes 16777216 | tf_op jit(solution)/shard_map/psum | solution.py:210
  694.5 483.7 %reduce-scatter.28.cloned.1.call-start = ((), (), s32[]{:S(2)}) async-start(), calls=%async_computation.22 | async-start | bytes 5308416 | tf_op jit(solution)/shard_map/reduce_scatter | solution.py:45
  705.0 571.9 %reduce-scatter.30.cloned.1.call-start = ((), (), s32[]{:S(2)}) async-start(), calls=%async_computation.23 | async-start | bytes 5308416 | tf_op jit(solution)/shard_map/reduce_scatter | solution.py:46
  715.4 663.2 %reduce-scatter.32.cloned.1.call-start = ((), (), s32[]{:S(2)}) async-start(), calls=%async_computation.24 | async-start | bytes 5308416 | tf_op jit(solution)/shard_map/reduce_scatter | solution.py:47
  725.2 353.4 %copy-start.101 = (f32[1024]{0:T(1024)S(1)}, f32[1024]{0:T(1024)}, u32[]{:S(2)}) copy-start(f32[1024]{0:T(1024)} %copy-done.100) | copy-start | bytes 12292
  1078.6 61.9 %copy-start.15 = (bf16[1024,1024]{1,0:T(8,128)(2,1)S(1)}, bf16[1024,1024]{1,0:T(8,128)(2,1)}, u32[]{:S(2)}) copy-start(bf16[1024,1024]{1,0:T(8,128)(2,1)} %get-tuple-element.55) | copy-start | bytes 6291460
  (103 other events, 486.0 us)
Sparse Core Ops, SparseCore 0:
  247.6 84.5 all-reduce.30
  434.5 83.8 all-reduce.28
  573.3 14.6 reduce-scatter.13
  590.7 14.7 reduce-scatter.17
  623.7 14.7 reduce-scatter.11
  645.3 14.7 reduce-scatter.15
  663.4 61.8 reduce-scatter.23
  729.0 60.8 reduce-scatter.21
  793.3 62.8 reduce-scatter.25
  860.5 62.4 reduce-scatter.19
  925.6 152.9 all-reduce.26
  1082.1 95.9 reduce-scatter.27
  1181.8 95.0 reduce-scatter.29
  1280.4 98.0 reduce-scatter.31
Sparse Core Ops, SparseCore 1:
  249.6 48.8 all-gather.13
  300.0 48.6 all-gather.11
  350.2 49.0 all-gather.15
where the time goes:
time: 1410 us; the launch traced here: 1400 us
  waiting for transfers between devices  694 us (49%)
  matrix products  331 us (23%)
  blocking collectives  231 us (16%)
  other arithmetic  97.9 us (7%)
  local copies, waits for them, and re-layouts  23.1 us (2%)
  between operations  20.6 us (1%)
    psum x1, waiting for transfers between devices, on_device(): lax.psum(ffn_part.astype(jnp.bfloat16), 'tensor').astype(jnp.float32)  150 us
    reduce_scatter x1, waiting for transfers between devices, reduce_first(): lax.psum_scatter(gradients[9], ('dp', 'ctx'), scatter_dimension=0, tiled=...  97.6 us
    reduce_scatter x1, waiting for transfers between devices, reduce_first(): lax.psum_scatter(gradients[10], ('dp', 'ctx'), scatter_dimension=1, tiled...  76.6 us
    psum x1, waiting for transfers between devices, on_device(): lax.psum(attn_part.astype(jnp.bfloat16), 'tensor').astype(jnp.float32)  73.2 us
    psum x1, waiting for transfers between devices, on_device(): lax.psum(ffn_in_part.astype(jnp.bfloat16), 'tensor').astype(jnp.float32)  72.4 us
    reduce_scatter x1, waiting for transfers between devices, reduce_first(): lax.psum_scatter(gradients[6], ('dp', 'ctx'), scatter_dimension=1, tiled=...  60.2 us
    reduce_scatter x1, waiting for transfers between devices, reduce_first(): lax.psum_scatter(gradients[1], ('dp', 'ctx'), scatter_dimension=0, tiled=...  60.1 us
    unnamed x3, blocking collectives  52.7 us
  transfers between devices with their start and end apart: 17, of which 10 were waited for; matrix products, arithmetic and copies ran while one was open for 16% of the time, Pallas kernels for 0%

commit v1 on v0

v1 whole, which is shorter than its diff:
```python
import functools
import math

import jax
import jax.numpy as jnp
from jax import lax
from jax.experimental import pallas as pl
from jax.experimental.pallas import tpu as pltpu
from jax.sharding import PartitionSpec as P

HD = 64
LANES = 128
EPS = 1e-05
ROPE_BASE = 1000000.0
BF = jnp.bfloat16
F32 = jnp.float32
NT = (((1,), (1,)), ((), ()))
TN = (((0,), (0,)), ((), ()))
NN = (((1,), (0,)), ((), ()))
SCALE = HD ** (-0.5)
SCORE_SCALE = SCALE * math.log2(math.e)
VMEM_LIMIT = 56 * 1024 * 1024


def mm(a, b, dims=NN):
    return lax.dot_general(a, b, dims, preferred_element_type=F32)


def low_half(shape):
    return lax.broadcasted_iota(jnp.int32, shape, 1) % HD < HD // 2


def left_head(shape):
    return lax.broadcasted_iota(jnp.int32, shape, 1) < HD


def partner(x):
    return jnp.where(low_half(x.shape), pltpu.roll(x, LANES - HD // 2, 1), pltpu.roll(x, HD // 2, 1))


def head_mean(x):
    rows = lax.broadcasted_iota(jnp.int32, (LANES, LANES), 0) // HD
    cols = lax.broadcasted_iota(jnp.int32, (LANES, LANES), 1) // HD
    ones = jnp.where(rows == cols, 1.0 / HD, 0.0).astype(BF)
    high = x.astype(BF)
    rest = (x - high.astype(F32)).astype(BF)
    return mm(high, ones) + mm(rest, ones)


def project_kernel(x_ref, gain_ref, w_ref, cos_ref, sin_ref, qg_ref, kg_ref,
                   normed_ref, z_ref, q_ref, k_ref, v_ref):
    x = x_ref[...].astype(F32)
    scale = lax.rsqrt(jnp.mean(x * x, axis=-1, keepdims=True) + EPS)
    normed = (x * scale * gain_ref[...]).astype(BF)
    normed_ref[...] = normed
    out = mm(normed, w_ref[...])
    n_q = q_ref.shape[1] // LANES
    n_k = k_ref.shape[1] // (2 * LANES)
    cos, sin = cos_ref[...], sin_ref[...]
    for block in range(n_q + n_k):
        z = out[:, block * LANES:(block + 1) * LANES]
        z_ref[:, block * LANES:(block + 1) * LANES] = z
        gain = qg_ref[...] if block < n_q else kg_ref[...]
        n = z * lax.rsqrt(head_mean(z * z) + EPS) * gain
        turned = n * cos + partner(n) * sin
        if block < n_q:
            q_ref[:, block * LANES:(block + 1) * LANES] = turned.astype(BF)
        else:
            both(turned, k_ref, block - n_q)
    for block in range(n_k):
        at = (n_q + n_k + block) * LANES
        both(out[:, at:at + LANES], v_ref, block)


def both(pair, ref, block):
    swapped = pltpu.roll(pair, HD, 1)
    left = left_head(pair.shape)
    at = 2 * block * LANES
    ref[:, at:at + LANES] = jnp.where(left, pair, swapped).astype(BF)
    ref[:, at + LANES:at + 2 * LANES] = jnp.where(left, swapped, pair).astype(BF)


def project(xs, gain, w_all, cos, sin, qgain, kgain, n_qcols, n_kcols, tb):
    tokens, width = xs.shape
    cols = w_all.shape[1]
    row = lambda b: (b, 0)
    fixed = lambda b: (0, 0)
    return pl.pallas_call(
        project_kernel,
        grid=(tokens // tb,),
        in_specs=[
            pl.BlockSpec((tb, width), row),
            pl.BlockSpec((1, width), fixed),
            pl.BlockSpec((width, cols), fixed),
            pl.BlockSpec((tb, LANES), row),
            pl.BlockSpec((tb, LANES), row),
            pl.BlockSpec((1, LANES), fixed),
            pl.BlockSpec((1, LANES), fixed),
        ],
        out_specs=[
            pl.BlockSpec((tb, width), row),
            pl.BlockSpec((tb, n_qcols + n_kcols), row),
            pl.BlockSpec((tb, n_qcols), row),
            pl.BlockSpec((tb, 2 * n_kcols), row),
            pl.BlockSpec((tb, 2 * n_kcols), row),
        ],
        out_shape=[
            jax.ShapeDtypeStruct((tokens, width), BF),
            jax.ShapeDtypeStruct((tokens, n_qcols + n_kcols), F32),
            jax.ShapeDtypeStruct((tokens, n_qcols), BF),
            jax.ShapeDtypeStruct((tokens, 2 * n_kcols), BF),
            jax.ShapeDtypeStruct((tokens, 2 * n_kcols), BF),
        ],
        cost_estimate=pl.CostEstimate(flops=2 * tokens * width * cols, bytes_accessed=tokens * 14000, transcendentals=0),
        compiler_params=pltpu.CompilerParams(vmem_limit_bytes=VMEM_LIMIT),
        name="project",
    )(xs, gain, w_all, cos, sin, qgain, kgain)


def attend_kernel(ids, q_ref, k_ref, v_ref, o_ref, lse_ref, acc_a, acc_b):
    chunk = q_ref.shape[0]
    own = ids[pl.program_id(1)]
    left = left_head(q_ref.shape)
    q = q_ref[...]
    zero = jnp.zeros_like(q)
    q_a, q_b = jnp.where(left, q, zero), jnp.where(left, zero, q)
    acc_a[...] = jnp.zeros_like(acc_a)
    acc_b[...] = jnp.zeros_like(acc_b)

    def block(at, masked):
        rows = pl.ds(pl.multiple_of(at * chunk, chunk), chunk)
        k, v = k_ref[rows, :], v_ref[rows, :]
        one = jnp.ones_like(v)
        for q_one, v_one, acc in ((q_a, jnp.where(left, v, one), acc_a), (q_b, jnp.where(left, one, v), acc_b)):
            p = jnp.exp2(mm(q_one, k, NT) * SCORE_SCALE)
            if masked:
                allowed = lax.broadcasted_iota(jnp.int32, p.shape, 1) <= lax.broadcasted_iota(jnp.int32, p.shape, 0)
                p = jnp.where(allowed, p, 0.0)
            acc[...] += mm(p.astype(BF), v_one)

    @pl.loop(0, own)
    def _(at):
        block(at, False)

    block(own, True)
    a, b = acc_a[...], acc_b[...]
    total = pltpu.roll(jnp.where(left, b, a), HD, 1)
    o_ref[...] = (jnp.where(left, a, b) / total).astype(BF)
    rows = jnp.transpose(jnp.log2(total))
    lse_ref[0:1, :] = rows[0:1, :]
    lse_ref[1:2, :] = rows[HD:HD + 1, :]


def attend(ids, q, k, v, chunk):
    tokens, cols = q.shape
    pairs = cols // LANES
    return pl.pallas_call(
        attend_kernel,
        grid_spec=pltpu.PrefetchScalarGridSpec(
            num_scalar_prefetch=1,
            grid=(pairs, 2),
            in_specs=[
                pl.BlockSpec((chunk, LANES), lambda j, c, ids: (ids[c], j)),
                pl.BlockSpec((tokens, LANES), lambda j, c, ids: (0, j)),
                pl.BlockSpec((tokens, LANES), lambda j, c, ids: (0, j)),
            ],
            out_specs=[
                pl.BlockSpec((chunk, LANES), lambda j, c, ids: (c, j)),
                pl.BlockSpec((8, chunk), lambda j, c, ids: (j, c)),
            ],
            scratch_shapes=[pltpu.VMEM((chunk, LANES), F32)] * 2,
        ),
        out_shape=[
            jax.ShapeDtypeStruct((2 * chunk, cols), BF),
            jax.ShapeDtypeStruct((8 * pairs, 2 * chunk), F32),
        ],
        cost_estimate=pl.CostEstimate(
            flops=pairs * 2 * 4 * LANES * chunk * (tokens + chunk), bytes_accessed=6 * tokens * cols,
            transcendentals=pairs * 2 * chunk * (tokens + chunk)),
        compiler_params=pltpu.CompilerParams(vmem_limit_bytes=VMEM_LIMIT),
        name="attend",
    )(ids, q, k, v)


def attend_back_kernel(ids, q_ref, k_ref, v_ref, o_ref, do_ref, lse_ref, dq_ref, dk_ref, dv_ref):
    chunk = q_ref.shape[0]
    own = ids[pl.program_id(1)]
    left = left_head(q_ref.shape)
    q, do = q_ref[...], do_ref[...]
    zero = jnp.zeros_like(q)
    q_a, q_b = jnp.where(left, q, zero), jnp.where(left, zero, q)
    do_a, do_b = jnp.where(left, do, zero), jnp.where(left, zero, do)
    prod = jnp.transpose(do.astype(F32) * o_ref[...].astype(F32))
    delta_a = jnp.sum(prod[:HD], axis=0, keepdims=True)
    delta_b = jnp.sum(prod[HD:], axis=0, keepdims=True)
    lse_a, lse_b = lse_ref[0:1, :], lse_ref[1:2, :]
    dq_ref[...] = jnp.zeros_like(dq_ref)

    @pl.when(pl.program_id(1) == 0)
    def _():
        dk_ref[...] = jnp.zeros_like(dk_ref)
        dv_ref[...] = jnp.zeros_like(dv_ref)

    def block(at, masked):
        rows = pl.ds(pl.multiple_of(at * chunk, chunk), chunk)
        k, v = k_ref[rows, :], v_ref[rows, :]
        k_a, k_b = jnp.where(left, k, zero), jnp.where(left, zero, k)
        for q_one, do_one, k_one, lse, delta in ((q_a, do_a, k_a, lse_a, delta_a), (q_b, do_b, k_b, lse_b, delta_b)):
            p = jnp.exp2(mm(k, q_one, NT) * SCORE_SCALE - lse)
            if masked:
                allowed = lax.broadcasted_iota(jnp.int32, p.shape, 0) <= lax.broadcasted_iota(jnp.int32, p.shape, 1)
                p = jnp.where(allowed, p, 0.0)
            ds = (p * (mm(v, do_one, NT) - delta)).astype(BF)
            dv_ref[rows, :] += mm(p.astype(BF), do_one)
            dk_ref[rows, :] += mm(ds, q_one)
            dq_ref[...] += mm(ds, k_one, TN)

    @pl.loop(0, own)
    def _(at):
        block(at, False)

    block(own, True)


def attend_back(ids, q, k, v, o, do, lse, chunk):
    tokens, cols = q.shape
    pairs = cols // LANES
    whole = pl.BlockSpec((tokens, LANES), lambda j, c, ids: (0, j))
    mine = pl.BlockSpec((chunk, LANES), lambda j, c, ids: (c, j))
    natural = pl.BlockSpec((chunk, LANES), lambda j, c, ids: (ids[c], j))
    return pl.pallas_call(
        attend_back_kernel,
        grid_spec=pltpu.PrefetchScalarGridSpec(
            num_scalar_prefetch=1,
            grid=(pairs, 2),
            in_specs=[natural, whole, whole, mine, mine, pl.BlockSpec((8, chunk), lambda j, c, ids: (j, c))],
            out_specs=[natural, whole, whole],
        ),
        out_shape=[jax.ShapeDtypeStruct((tokens, cols), F32)] * 3,
        cost_estimate=pl.CostEstimate(
            flops=pairs * 2 * 10 * LANES * chunk * (tokens + chunk), bytes_accessed=18 * tokens * cols,
            transcendentals=pairs * 2 * chunk * (tokens + chunk)),
        compiler_params=pltpu.CompilerParams(vmem_limit_bytes=VMEM_LIMIT),
        name="attend_back",
    )(ids, q, k, v, o, do, lse)


def turn_back_kernel(ids, z_ref, dq_ref, dk_ref, dv_ref, cos_ref, sin_ref, qg_ref, kg_ref, out_ref, gain_ref, *, per_chunk):
    step = pl.program_id(0)
    n_q = dq_ref.shape[1] // LANES
    n_k = dk_ref.shape[1] // (2 * LANES)
    cos, sin = cos_ref[...], sin_ref[...]

    @pl.when(step == 0)
    def _():
        gain_ref[...] = jnp.zeros_like(gain_ref)

    def back(block, d, gain, row):
        z = z_ref[:, block * LANES:(block + 1) * LANES]
        scale = lax.rsqrt(head_mean(z * z) + EPS)
        d = d * SCALE
        dn = d * cos - partner(d) * sin
        zr = z * scale
        gain_ref[row:row + 1, :] += jnp.sum(dn * zr, axis=0, keepdims=True)
        gdn = gain * dn
        out_ref[:, block * LANES:(block + 1) * LANES] = (scale * (gdn - zr * head_mean(zr * gdn))).astype(BF)

    own = jnp.logical_or(step // per_chunk == ids[0], step // per_chunk == ids[1])

    @pl.when(own)
    def _():
        for block in range(n_q):
            back(block, dq_ref[:, block * LANES:(block + 1) * LANES], qg_ref[...], 0)

    @pl.when(jnp.logical_not(own))
    def _():
        out_ref[:, :n_q * LANES] = jnp.zeros((out_ref.shape[0], n_q * LANES), BF)

    def folded(ref, block):
        at = 2 * block * LANES
        one, two = ref[:, at:at + LANES], ref[:, at + LANES:at + 2 * LANES]
        one, two = one + pltpu.roll(one, HD, 1), two + pltpu.roll(two, HD, 1)
        return jnp.where(left_head(one.shape), one, two)

    for block in range(n_k):
        back(n_q + block, folded(dk_ref, block), kg_ref[...], 1)
        at = (n_q + n_k + block) * LANES
        out_ref[:, at:at + LANES] = folded(dv_ref, block).astype(BF)


def turn_back(ids, z, dq, dk, dv, cos, sin, qgain, kgain, tb, chunk):
    tokens = z.shape[0]
    n_q, n_k = dq.shape[1], dk.shape[1] // 2
    row = lambda b, ids: (b, 0)
    fixed = lambda b, ids: (0, 0)
    return pl.pallas_call(
        functools.partial(turn_back_kernel, per_chunk=chunk // tb),
        grid_spec=pltpu.PrefetchScalarGridSpec(
            num_scalar_prefetch=1,
            grid=(tokens // tb,),
            in_specs=[
                pl.BlockSpec((tb, n_q + n_k), row),
                pl.BlockSpec((tb, n_q), row),
                pl.BlockSpec((tb, 2 * n_k), row),
                pl.BlockSpec((tb, 2 * n_k), row),
                pl.BlockSpec((tb, LANES), row),
                pl.BlockSpec((tb, LANES), row),
                pl.BlockSpec((1, LANES), fixed),
                pl.BlockSpec((1, LANES), fixed),
            ],
            out_specs=[pl.BlockSpec((tb, n_q + 2 * n_k), row), pl.BlockSpec((8, LANES), fixed)],
        ),
        out_shape=[
            jax.ShapeDtypeStruct((tokens, n_q + 2 * n_k), BF),
            jax.ShapeDtypeStruct((8, LANES), F32),
        ],
        cost_estimate=pl.CostEstimate(flops=tokens * 200000, bytes_accessed=tokens * 12000, transcendentals=0),
        compiler_params=pltpu.CompilerParams(vmem_limit_bytes=VMEM_LIMIT),
        name="turn_back",
    )(ids, z, dq, dk, dv, cos, sin, qgain, kgain)


def feed_kernel(hn_ref, dy_ref, wg_ref, wu_ref, wd_ref, act_ref, dg_ref, du_ref, out_ref, dhn_ref):
    hn, dy = hn_ref[...], dy_ref[...]
    parts, _, part = wd_ref.shape
    gate = mm(hn, wg_ref[...])
    up = mm(hn, wu_ref[...])
    dact = mm(dy[:, :part], wd_ref[0], NT)
    for i in range(1, parts):
        dact += mm(dy[:, i * part:(i + 1) * part], wd_ref[i], NT)
    sig = 1.0 / (1.0 + jnp.exp(-gate))
    silu = gate * sig
    act = (silu * up).astype(BF)
    dg = (dact * up * (sig + silu * (1.0 - sig))).astype(BF)
    du = (dact * silu).astype(BF)
    act_ref[...] = act
    dg_ref[...] = dg
    du_ref[...] = du
    dhn_ref[...] = (mm(dg, wg_ref[...], NT) + mm(du, wu_ref[...], NT)).astype(BF)
    for i in range(parts):
        out_ref[:, i * part:(i + 1) * part] = mm(act, wd_ref[i]).astype(BF)


def feed(hn, dy, wg, wu, wd, tb):
    tokens, width = hn.shape
    units = wg.shape[1]
    row = lambda b: (b, 0)
    fixed = lambda b: (0, 0)
    once = pl.Buffered(1)
    return pl.pallas_call(
        feed_kernel,
        grid=(tokens // tb,),
        in_specs=[
            pl.BlockSpec((tb, width), row),
            pl.BlockSpec((tb, width), row),
            pl.BlockSpec((width, units), fixed, pipeline_mode=once),
            pl.BlockSpec((width, units), fixed, pipeline_mode=once),
            pl.BlockSpec(wd.shape, lambda b: (0, 0, 0), pipeline_mode=once),
        ],
        out_specs=[pl.BlockSpec((tb, units), row)] * 3 + [pl.BlockSpec((tb, width), row)] * 2,
        out_shape=[jax.ShapeDtypeStruct((tokens, units), BF)] * 3 + [jax.ShapeDtypeStruct((tokens, width), BF)] * 2,
        cost_estimate=pl.CostEstimate(flops=12 * tokens * width * units, bytes_accessed=6 * width * units + tokens * 15000,
                                      transcendentals=tokens * units),
        compiler_params=pltpu.CompilerParams(vmem_limit_bytes=VMEM_LIMIT),
        name="feed",
    )(hn, dy, wg, wu, wd)


def rope_tables(length):
    positions = lax.optimization_barrier(jnp.arange(length, dtype=jnp.int32))
    frequency = ROPE_BASE ** (-jnp.arange(0, HD, 2).astype(F32) / HD)
    angles = positions.astype(F32)[:, None] * frequency[None, :]
    cos, sin = jnp.cos(angles), jnp.sin(angles)
    return jnp.concatenate([cos] * 4, axis=1), jnp.concatenate([-sin, sin] * 2, axis=1)


def rms(z):
    return lax.rsqrt(jnp.mean(z * z, axis=-1, keepdims=True) + EPS)


def norm_back(z, scale, gain, dn):
    zr = z * scale
    gdn = gain * dn
    dz = scale * (gdn - zr * jnp.mean(zr * gdn, axis=-1, keepdims=True))
    return dz, jnp.sum(dn * zr, axis=0)


def on_device(layer_input, cotangent, attn_gain, query_weight, key_weight, value_weight, query_gain, key_gain,
              out_weight, ffn_gain, gate_weight, up_weight, down_weight):
    n_dp, n_ctx, n_tensor = (lax.axis_size(a) for a in ("dp", "ctx", "tensor"))
    seqs, local_len, width = layer_input.shape
    assert seqs == 2 and n_tensor == 4
    chunk = local_len // 2
    length = local_len * n_ctx
    t = lax.axis_index("tensor")
    seq, core = t // 2, t % 2
    ctx = lax.axis_index("ctx")

    def own_chunk(place, which):
        return jnp.where(place % 2 == which, place, 2 * n_ctx - 1 - place)

    id_here, id_there = own_chunk(ctx, core), own_chunk(ctx, 1 - core)
    ids = jnp.stack([id_here, id_there]).astype(jnp.int32)

    def swap_core(x):
        return lax.ppermute(x, "tensor", [(i, i ^ 1) for i in range(n_tensor)])

    def swap_seq(x):
        return lax.ppermute(x, "tensor", [(i, i ^ 2) for i in range(n_tensor)])

    def swap_ctx(x):
        return lax.ppermute(x, "ctx", [(0, 1), (1, 0)])

    homes = []
    for place in range(n_ctx):
        for i in range(n_tensor):
            which = place if place % 2 == i % 2 else 2 * n_ctx - 1 - place
            homes.append((place * n_tensor + i, (which // 2) * n_tensor + i))

    def send_home(x):
        return lax.ppermute(x, ("ctx", "tensor"), homes)

    def fetch_from_home(x):
        return lax.ppermute(x, ("ctx", "tensor"), [(b, a) for a, b in homes])

    def ctx_pair(x, axis):
        if n_ctx != 2:
            return lax.all_gather(x, "ctx", axis=axis, tiled=False)
        other = swap_ctx(x)
        return jnp.where(ctx == 0, jnp.stack([x, other], axis), jnp.stack([other, x], axis))

    x_here = lax.dynamic_index_in_dim(layer_input, seq, 0, keepdims=False)
    if n_ctx == 2:
        half = lax.dynamic_slice_in_dim(x_here, core * chunk, chunk, 0)
        first = swap_ctx(half)
        second = swap_core(first)
        xs = jnp.zeros((length, width), BF)
        xs = lax.dynamic_update_slice(xs, x_here, (ctx * local_len, 0))
        xs = lax.dynamic_update_slice(xs, first, ((1 - ctx) * local_len + core * chunk, 0))
        xs = lax.dynamic_update_slice(xs, second, ((1 - ctx) * local_len + (1 - core) * chunk, 0))
    else:
        xs = lax.all_gather(x_here, "ctx", axis=0, tiled=True)

    gains = lax.all_gather(jnp.concatenate([attn_gain, ffn_gain, query_gain, key_gain]), "dp", axis=0, tiled=False)
    d_part, h_part = attn_gain.shape[0], query_gain.shape[0]
    gain_a = gains[:, :d_part].reshape(1, width).astype(F32)
    gain_f = gains[:, d_part:2 * d_part].reshape(1, width).astype(F32)
    gain_q = jnp.tile(gains[:, 2 * d_part:2 * d_part + h_part].reshape(1, HD).astype(F32), (1, 2))
    gain_k = jnp.tile(gains[:, 2 * d_part + h_part:].reshape(1, HD).astype(F32), (1, 2))

    nq, nk = query_weight.shape[1], key_weight.shape[1]
    qkv_mine = lax.all_gather(jnp.concatenate([query_weight, key_weight, value_weight], axis=1), "dp", axis=0, tiled=True)
    qkv_theirs = swap_seq(qkv_mine)

    def interleave(a, b):
        pieces = []
        for lo, hi in ((0, nq), (nq, nq + nk), (nq + nk, nq + 2 * nk)):
            pieces += [a[:, lo:hi], b[:, lo:hi]]
        return jnp.concatenate(pieces, axis=1)

    w_all = interleave(qkv_mine, qkv_theirs)
    out_mine = lax.all_gather(out_weight, "dp", axis=0, tiled=False).transpose(1, 0, 2).reshape(out_weight.shape[0], width)
    w_out = jnp.concatenate([out_mine, swap_seq(out_mine)], axis=0)

    def gather_ffn(w):
        if n_ctx != 2:
            return lax.all_gather(w, "dp", axis=0, tiled=False)
        rows = w.shape[0] // 2
        mine = lax.dynamic_slice_in_dim(w, ctx * rows, rows, 0)
        got = lax.all_gather(mine, "dp", axis=0, tiled=False)
        return ctx_pair(got, 1).reshape(n_dp, w.shape[0], w.shape[1])

    w_gate = gather_ffn(gate_weight).reshape(width, -1)
    w_up = gather_ffn(up_weight).reshape(width, -1)
    w_down = gather_ffn(down_weight)

    cot_home = lax.dynamic_slice(cotangent, (seq, core * chunk, 0), (1, chunk, width))[0]
    dy_0 = fetch_from_home(cot_home)
    dy_2 = swap_seq(dy_0)
    dy_02 = jnp.stack([dy_0, dy_2])
    dy_13 = swap_core(dy_02)
    dy_own = jnp.concatenate([dy_0, dy_13[0]], axis=0)
    dy_other = jnp.concatenate([dy_2, dy_13[1]], axis=0)

    tb = min(256, chunk)
    cos, sin = rope_tables(length)
    normed, z, q, k, v = project(xs, gain_a, w_all, cos, sin, gain_q, gain_k, 2 * nq, 2 * nk, tb)
    o, lse = attend(ids, q, k, v, chunk)
    attn = mm(o, w_out)
    got = swap_core(attn[chunk:].astype(BF))
    x_0 = lax.dynamic_slice_in_dim(xs, id_here * chunk, chunk, 0).astype(F32)
    hidden = x_0 + (attn[:chunk] + got.astype(F32))
    h_scale = rms(hidden)
    hn_0 = (hidden * h_scale * gain_f).astype(BF)
    hn_1 = swap_core(hn_0)
    hn_2 = swap_seq(hn_0)
    hn_3 = swap_core(hn_2)
    hn_own = jnp.concatenate([hn_0, hn_1], axis=0)
    hn_other = jnp.concatenate([hn_2, hn_3], axis=0)

    act_o, dg_o, du_o, y_o, dhn_o = feed(hn_own, dy_own, w_gate, w_up, w_down, tb)
    act_t, dg_t, du_t, y_t, dhn_t = feed(hn_other, dy_other, w_gate, w_up, w_down, tb)

    def sum_tensor(mine, theirs):
        for_seq = theirs[:chunk].astype(F32) + swap_core(theirs[chunk:]).astype(F32)
        here = mine[:chunk].astype(F32) + swap_core(mine[chunk:]).astype(F32)
        return here + swap_seq(for_seq.astype(BF)).astype(F32)

    dhn = sum_tensor(dhn_o, dhn_t)
    d_norm, ffn_gain_part = norm_back(hidden, h_scale, gain_f, dhn)
    dhidden = dy_0.astype(F32) + d_norm
    dhr_0 = dhidden.astype(BF)
    dhr = jnp.concatenate([dhr_0, swap_core(dhr_0)], axis=0)

    def join(piece, kind):
        p_core = swap_core(piece)
        p_seq = swap_seq(piece)
        p_both = swap_core(p_seq)
        out = jnp.zeros((2, 2, chunk, width), kind)
        for value, s, c in ((piece, seq, core), (p_core, seq, 1 - core), (p_seq, 1 - seq, core), (p_both, 1 - seq, 1 - core)):
            out = lax.dynamic_update_slice(out, value.astype(kind)[None, None], (s, c, 0, 0))
        return out.reshape(2, local_len, width)

    total = (hidden + sum_tensor(y_o, y_t)).astype(BF)
    layer_output = join(send_home(total), BF)

    def weight_sum(a_own, b_own, a_other, b_other):
        return (mm(a_own, b_own, TN) + mm(a_other, b_other, TN)).astype(BF)

    def scatter(g):
        mine = lax.psum_scatter(g, ("dp", "ctx"), scatter_dimension=0, tiled=True)
        return ctx_pair(mine, 0).reshape(g.shape[0] // n_dp, g.shape[1])

    gate_grad = scatter(weight_sum(hn_own, dg_o, hn_other, dg_t)).astype(F32)
    up_grad = scatter(weight_sum(hn_own, du_o, hn_other, du_t)).astype(F32)
    down_grad = scatter(weight_sum(dy_own, act_o, dy_other, act_t)).T.astype(F32)

    do = mm(dhr, w_out, NT).astype(BF)
    dq, dk, dv = attend_back(ids, q, k, v, o, do, lse, chunk)
    dqkv, gain_parts = turn_back(ids, z, dq, dk, dv, cos, sin, gain_q, gain_k, tb, chunk)
    dn = mm(dqkv, w_all, NT).astype(BF).reshape(n_ctx, 2, chunk, width)
    keep = lax.dynamic_index_in_dim(dn, core, 1, keepdims=False)
    give = lax.dynamic_index_in_dim(dn, 1 - core, 1, keepdims=False)
    dn = keep.astype(F32) + swap_core(give).astype(F32)
    x_kept = lax.dynamic_index_in_dim(xs.reshape(n_ctx, 2, chunk, width), core, 1, keepdims=False).astype(F32)
    dz, attn_gain_part = norm_back(x_kept, rms(x_kept), gain_a, dn.reshape(n_ctx, chunk, width))
    attn_gain_part = jnp.sum(attn_gain_part, axis=0)
    at_home = lax.dynamic_index_in_dim(dz, id_here // 2, 0, keepdims=True) + dhidden[None]
    dz = lax.dynamic_update_slice(dz, at_home, (id_here // 2, 0, 0)).astype(BF)
    if n_ctx == 2:
        mine = lax.dynamic_index_in_dim(dz, ctx, 0, keepdims=False)
        got = swap_ctx(lax.dynamic_index_in_dim(dz, 1 - ctx, 0, keepdims=False))
        dx = (mine.astype(F32) + got.astype(F32)).astype(BF)
    else:
        dx = lax.psum_scatter(dz, "ctx", scatter_dimension=0, tiled=False)
    input_grad = join(dx, F32)

    g_all = mm(normed, dqkv, TN).astype(BF)
    g_out = mm(dhr, o, TN).astype(BF)
    c1, c2 = 2 * nq, 2 * nq + 2 * nk
    h_out = out_weight.shape[0]
    g_mine = jnp.concatenate([g_all[:, :nq], g_all[:, c1:c1 + nk], g_all[:, c2:c2 + nk], g_out[:, :h_out]], axis=1)
    g_theirs = jnp.concatenate([g_all[:, nq:c1], g_all[:, c1 + nk:c2], g_all[:, c2 + nk:], g_out[:, h_out:]], axis=1)
    g = scatter((g_mine.astype(F32) + swap_seq(g_theirs).astype(F32)).astype(BF)).astype(F32)
    query_grad, key_grad, value_grad = g[:, :nq], g[:, nq:nq + nk], g[:, nq + nk:nq + 2 * nk]
    out_grad = g[:, nq + 2 * nk:].T

    fold = gain_parts[:2, :HD] + gain_parts[:2, HD:]
    small = lax.psum(jnp.concatenate([attn_gain_part, ffn_gain_part, fold.reshape(-1)]), ("dp", "ctx", "tensor"))
    dp = lax.axis_index("dp")
    attn_gain_grad = lax.dynamic_slice_in_dim(small, dp * d_part, d_part)
    ffn_gain_grad = lax.dynamic_slice_in_dim(small, width + dp * d_part, d_part)
    qgain_grad = lax.dynamic_slice_in_dim(small, 2 * width + dp * h_part, h_part)
    kgain_grad = lax.dynamic_slice_in_dim(small, 2 * width + HD + dp * h_part, h_part)

    return (layer_output, input_grad, attn_gain_grad, query_grad, key_grad, value_grad, qgain_grad, kgain_grad,
            out_grad, ffn_gain_grad, gate_grad, up_grad, down_grad)


def solution(mesh):
    token = P("dp", "ctx", None)
    into, out_of, vector = P("dp", "tensor"), P("tensor", "dp"), P("dp")
    return jax.shard_map(
        on_device,
        mesh=mesh,
        in_specs=(token, token, vector, into, into, into, vector, vector, out_of, vector, into, into, out_of),
        out_specs=(token, token, vector, into, into, into, vector, vector, out_of, vector, into, into, out_of),
        check_vma=False,
    )
```

time: 1410 us -> 635 us (0.45)
  waiting for transfers between devices: 694 us -> 164 us
  matrix products: 331 us -> 54.9 us
  blocking collectives: 231 us -> 89.3 us
  Pallas kernels: 0 us -> 132 us
  local copies, waits for them, and re-layouts: 23.1 us -> 76.4 us
  other arithmetic: 97.9 us -> 71.6 us
  starting transfers between devices: 1.92 us -> 25.2 us
    reduce_scatter x11 -> x4, waiting for transfers between devices: 363 us -> 0.03 us  [scatter(): mine = lax.psum_scatter(g, ('dp', 'ctx'), scatter_dimension=0, tiled=True)]
    psum x3 -> x0, waiting for transfers between devices: 295 us -> none  [the longest x1 150 us: on_device(): lax.psum(ffn_part.astype(jnp.bfloat16), 'tensor').astype(jnp.float32)]
    dot_general x54 -> x11, matrix products: 331 us -> 54.9 us  [mm(): return lax.dot_general(a, b, dims, preferred_element_type=F32)]
    ppermute x0 -> x35, waiting for transfers between devices: none -> 164 us  [the longest x9 92.2 us: swap_seq(): return lax.ppermute(x, 'tensor', [(i, i ^ 2) for i in range(n_tensor)])]
    all_gather x19 -> x1, blocking collectives: 173 us -> 22.7 us  [on_device(): lax.all_gather(out_weight, 'dp', axis=0, tiled=False).transpose(1, 0, 2)]
    pallas_call x0 -> x6, Pallas kernels: none -> 132 us  [the longest x2 44.1 us: feed(): pl.pallas_call(feed_kernel, grid=(tokens // tb,), in_specs=[pl.BlockSpec(...]
    psum x1, blocking collectives: 5.77 us -> 54.4 us  [on_device(): lax.psum(jnp.concatenate([attn_gain_part, ffn_gain_part, fold.reshape(-1)...]
    unnamed x3 -> x1, blocking collectives: 52.7 us -> 12.2 us
  transfers between devices with their start and end apart: 17 -> 43, of which waited for: 10 -> 9; matrix products, arithmetic and copies ran while one was open for 16% -> 28% of each run, Pallas kernels for 0% -> 17%
where the time goes in v1:
time: 635 us; the launch traced here: 629 us
  waiting for transfers between devices  164 us (26%)
  Pallas kernels  132 us (21%)
  blocking collectives  89.3 us (14%)
  local copies, waits for them, and re-layouts  76.4 us (12%)
  other arithmetic  71.6 us (11%)
  matrix products  54.9 us (9%)
  starting transfers between devices  25.2 us (4%)
  between operations  15.9 us (3%)
    ppermute x9, waiting for transfers between devices, swap_seq(): return lax.ppermute(x, 'tensor', [(i, i ^ 2) for i in range(n_tensor)])  92.2 us
    ppermute x9, waiting for transfers between devices, swap_ctx(): return lax.ppermute(x, 'ctx', [(0, 1), (1, 0)])  71.8 us
    dot_general x11, matrix products, mm(): return lax.dot_general(a, b, dims, preferred_element_type=F32)  54.9 us
    psum x1, blocking collectives, on_device(): lax.psum(jnp.concatenate([attn_gain_part, ffn_gain_part, fold.reshape(-1)...  54.4 us
    pallas_call x2, Pallas kernels, feed(): pl.pallas_call(feed_kernel, grid=(tokens // tb,), in_specs=[pl.BlockSpec(...  44.1 us
    pallas_call x1, Pallas kernels, attend_back(): pl.pallas_call(attend_back_kernel, grid_spec=pltpu.PrefetchScalarGridSpec...  37.1 us
    unnamed x126, local copies, waits for them, and re-layouts  24.7 us
    all_gather x1, blocking collectives, on_device(): lax.all_gather(out_weight, 'dp', axis=0, tiled=False).transpose(1, 0, 2)  22.7 us
  transfers between devices with their start and end apart: 43, of which 9 were waited for; matrix products, arithmetic and copies ran while one was open for 28% of the time, Pallas kernels for 17%

profile of v1, /device:TPU:0, one launch (start us, length us, event | category | flops | bytes accessed | tf_op | source)
XLA Modules:
  0.0 629.1 jit_solution(9297635153324674473)
XLA Ops:
  11.7 2.5 dynamic-slice_bitcast_fusion.3
  14.2 2.9 collective-permute-start
  17.2 22.7 %all-gather.1 = bf16[1024,256]{1,0:T(8,128)(2,1)S(1)} all-gather(bf16[256,256]{1,0:T(8,128)(2,1)S(1)} %copy-done.40), channel_id=3, replica_groups=mesh['dp'=4,'ctx'=2,'tensor'=4] {'dp'}, dimensions={0}, use_global_device_ids=true | all-gather | bytes 655360 | tf_op jit(solution)/shard_map/all_gather | solution.py:462
  46.6 5.5 fusion.13
  53.8 12.2 %all-reduce = bf16[2176]{0:T(1024)(128)(2,1)S(1)} all-reduce(bf16[2176]{0:T(1024)(128)(2,1)S(1)} %dynamic-update-slice), channel_id=2, replica_groups=mesh['dp'=4,'ctx'=2,'tensor'=4] {'dp'}, use_global_device_ids=true, to_apply=%add | all-reduce | flops 2176 | bytes 8704
  69.8 2.7 broadcast_in_dim.56
  75.8 3.0 pad_maximum_fusion.8
  86.0 9.0 %collective-permute-done.2 = bf16[1024,512]{1,0:T(8,128)(2,1)} collective-permute-done((bf16[1024,512]{1,0:T(8,128)(2,1)}, bf16[1024,512]{1,0:T(8,128)(2,1)}, u32[]{:S(2)}, u32[]{:S(2)}) %collective-permute-start.2) | collective-permute-done | bytes 1048608 | tf_op jit(solution)/shard_map/ppermute | solution.py:409
  101.9 16.1 %project.1 = (bf16[2048,1024]{1,0:T(8,128)(2,1)}, f32[2048,768]{1,0:T(8,128)}, bf16[2048,512]{1,0:T(8,128)(2,1)}, bf16[2048,512]{1,0:T(8,128)(2,1)}, bf16[2048,512]{1,0:T(8,128)(2,1)}) custom-call(bf16[2048,1024]{1,0:T(8,128)(2,1)} %constant_dynamic-update-slice_fusion.2.x_ref, f32[1,1024]{1,0:T(1,128)} %bitcast.173, ...), custom_call_target="tpu_custom_call" | custom-call | flops 4294967296 | bytes 28672000 | tf_op jit(solution)/shard_map/project/pallas_call | solution.py:88
  118.0 19.2 %attend.1 = (bf16[1024,512]{1,0:T(8,128)(2,1)}, f32[32,1024]{1,0:T(8,128)}) custom-call(s32[2]{0:T(128)} %pad_add_fusion.ids, bf16[2048,512]{1,0:T(8,128)(2,1)} %get-tuple-element.35.q_ref, bf16[2048,512]{1,0:T(8,128)(2,1)} %get-tuple-element.36.k_ref, bf16[2048,512]{1,0:T(8,128)(2,1)} %get-tuple-element.37.v_ref), custom_call_target="tpu_custom_call" | custom-call | flops 5368709120 | bytes 6291456 | tf_op jit(solution)/shard_map/attend/pallas_call | solution.py:157
  137.2 2.5 fusion.12
  147.1 4.4 maximum_select_fusion
  154.5 19.7 %collective-permute-done.10 = bf16[4,128,1152]{2,1,0:T(8,128)(2,1)} collective-permute-done((bf16[4,128,1152]{2,1,0:T(8,128)(2,1)}, bf16[4,128,1152]{2,1,0:T(8,128)(2,1)}, u32[]{:S(2)}, u32[]{:S(2)}) %collective-permute-start.10) | collective-permute-done | bytes 1179680 | tf_op jit(solution)/shard_map/ppermute | solution.py:412
  174.2 3.5 maximum_select_fusion.1
  177.8 20.8 %collective-permute-done.11 = bf16[4,576,256]{2,1,0:T(8,128)(2,1)S(1)} collective-permute-done((bf16[4,576,256]{2,1,0:T(8,128)(2,1)}, bf16[4,576,256]{2,1,0:T(8,128)(2,1)S(1)}, u32[]{:S(2)}, u32[]{:S(2)}) %collective-permute-start.11) | collective-permute-done | bytes 1179680 | tf_op jit(solution)/shard_map/ppermute | solution.py:412
  207.4 22.1 %feed.2 = (bf16[1024,1152]{1,0:T(8,128)(2,1)}, bf16[1024,1152]{1,0:T(8,128)(2,1)}, bf16[1024,1152]{1,0:T(8,128)(2,1)}, bf16[1024,1024]{1,0:T(8,128)(2,1)}, bf16[1024,1024]{1,0:T(8,128)(2,1)}) custom-call(bf16[1024,1024]{1,0:T(8,128)(2,1)} %pad_maximum_fusion.hn_ref, bf16[1024,1024]{1,0:T(8,128)(2,1)} %pad_maximum_fusion.2.dy_ref, ...), custom_call_target="tpu_custom_call" | custom-call | flops 14495514624 | bytes 22437888 | tf_op jit(solution)/shard_map/feed/pallas_call | solution.py:350
  229.4 2.4 constant_dynamic-update-slice_fusion.1
  231.8 6.6 %fusion.17 = f32[1024,1152]{1,0:T(8,128)} fusion(bf16[1024,1152]{1,0:T(8,128)(2,1)} %get-tuple-element.55, bf16[512,1024]{1,0:T(8,128)(2,1)S(1)} %copy-done.20, bf16[512,1024]{1,0:T(8,128)(2,1)S(1)} %copy-done.7), kind=kOutput, calls=%fused_computation.107 | convolution fusion | flops 2420113408 | bytes 9175040 | tf_op jit(solution)/shard_map/dot_general | solution.py:26
  240.7 22.1 %feed.3 = (bf16[1024,1152]{1,0:T(8,128)(2,1)}, bf16[1024,1152]{1,0:T(8,128)(2,1)}, bf16[1024,1152]{1,0:T(8,128)(2,1)}, bf16[1024,1024]{1,0:T(8,128)(2,1)}, bf16[1024,1024]{1,0:T(8,128)(2,1)}) custom-call(bf16[1024,1024]{1,0:T(8,128)(2,1)} %constant_dynamic-update-slice_fusion.hn_ref, bf16[1024,1024]{1,0:T(8,128)(2,1)} %pad_maximum_fusion.3.dy_ref, ...), custom_call_target="tpu_custom_call" | custom-call | flops 14495514624 | bytes 22437888 | tf_op jit(solution)/shard_map/feed/pallas_call | solution.py:350
  262.8 6.6 %add_convert_fusion = bf16[1024,1152]{1,0:T(8,128)(2,1)} fusion(f32[1024,1152]{1,0:T(8,128)} %fusion.17, bf16[1024,1152]{1,0:T(8,128)(2,1)} %get-tuple-element.56, bf16[512,1024]{1,0:T(8,128)(2,1)S(1)} %get-tuple-element.140, bf16[512,1024]{1,0:T(8,128)(2,1)S(1)} %copy-done.18), kind=kOutput, calls=%fused_computation.5 | convolution fusion | flops 2422472704 | bytes 11534336 | tf_op jit(solution)/shard_map/dot_general | solution.py:26
  269.5 5.4 fusion.18
  276.4 5.9 add_convert_fusion.1
  285.7 2.8 add_convert_fusion.4
  293.2 21.5 %collective-permute-done.23 = bf16[512,1024]{1,0:T(8,128)(2,1)} collective-permute-done((bf16[512,1024]{1,0:T(8,128)(2,1)}, bf16[512,1024]{1,0:T(8,128)(2,1)}, u32[]{:S(2)}, u32[]{:S(2)}) %collective-permute-start.23) | collective-permute-done | bytes 1048608 | tf_op jit(solution)/shard_map/ppermute | solution.py:409
  314.8 2.7 multiply_reduce_fusion
  317.5 19.3 %collective-permute-done.16 = bf16[512,1024]{1,0:T(8,128)(2,1)} collective-permute-done((bf16[512,1024]{1,0:T(8,128)(2,1)}, bf16[512,1024]{1,0:T(8,128)(2,1)}, u32[]{:S(2)}, u32[]{:S(2)}) %collective-permute-start.16) | collective-permute-done | bytes 1048608 | tf_op jit(solution)/shard_map/ppermute | solution.py:409
  336.9 4.6 fusion.21
  341.5 3.0 fusion.19
  344.5 6.1 add_convert_fusion.2
  353.8 3.9 convolution_convert_fusion.3.do_ref
  357.6 37.1 %attend_back.1 = (f32[2048,512]{1,0:T(8,128)}, f32[2048,512]{1,0:T(8,128)}, f32[2048,512]{1,0:T(8,128)}) custom-call(s32[2]{0:T(128)} %pad_add_fusion.ids, bf16[2048,512]{1,0:T(8,128)(2,1)} %get-tuple-element.35.q_ref, bf16[2048,512]{1,0:T(8,128)(2,1)} %get-tuple-element.36.k_ref, bf16[2048,512]{1,0:T(8,128)(2,1)} %get-tuple-element.37.v_ref, ...), custom_call_target="tpu_custom_call" | custom-call | flops 13421772800 | bytes 18874368 | tf_op jit(solution)/shard_map/attend_back/pallas_call | solution.py:231
  394.8 14.9 %turn_back.1 = (bf16[2048,1024]{1,0:T(8,128)(2,1)}, f32[8,128]{1,0:T(8,128)}) custom-call(s32[2]{0:T(128)} %pad_add_fusion.ids, f32[2048,768]{1,0:T(8,128)} %get-tuple-element.41.z_ref, f32[2048,512]{1,0:T(8,128)} %get-tuple-element.45.dq_ref, f32[2048,512]{1,0:T(8,128)} %get-tuple-element.46.dk_ref, f32[2048,512]{1,0:T(8,128)} %get-tuple-element.47.dv_ref, ...), custom_call_target="tpu_custom_call" | custom-call | flops 409600000 | bytes 24576000 | tf_op jit(solution)/shard_map/turn_back/pallas_call | solution.py:296
  409.7 7.0 %convolution_convert_fusion.1 = bf16[1024,1024]{0,1:T(8,128)(2,1)S(1)} fusion(bf16[2048,1024]{1,0:T(8,128)(2,1)S(1)} %copy-done.52, bf16[2048,1024]{1,0:T(8,128)(2,1)} %get-tuple-element.48), kind=kOutput, calls=%fused_computation.47 | convolution fusion | flops 4296015872 | bytes 10485760 | tf_op jit(solution)/shard_map/dot_general | solution.py:26
  418.4 2.7 convolution_convert_fusion.2
  425.0 5.2 convolution_convert_fusion
  435.2 2.5 broadcast_in_dim.55
  440.0 42.3 %collective-permute-done.19 = bf16[512,1024]{1,0:T(8,128)(2,1)} collective-permute-done((bf16[512,1024]{1,0:T(8,128)(2,1)}, bf16[512,1024]{1,0:T(8,128)(2,1)}, u32[]{:S(2)}, u32[]{:S(2)}) %collective-permute-start.19) | collective-permute-done | bytes 1048608 | tf_op jit(solution)/shard_map/ppermute | solution.py:409
  487.3 3.3 add_convert_fusion.3
  490.6 2.7 copy.86
  497.9 4.1 fusion.6
  502.1 2.7 fusion.5
  508.3 2.7 copy.84
  514.5 25.7 %collective-permute-done.26 = bf16[512,1024]{1,0:T(8,128)(2,1)} collective-permute-done((bf16[512,1024]{1,0:T(8,128)(2,1)}, bf16[512,1024]{1,0:T(8,128)(2,1)}, u32[]{:S(2)}, u32[]{:S(2)}) %collective-permute-start.26) | collective-permute-done | bytes 1048608 | tf_op jit(solution)/shard_map/ppermute | solution.py:412
  541.2 2.8 convert_dynamic-update-slice_fusion.3
  544.0 3.4 copy-done.9
  551.3 54.4 %psum.7 = f32[2176]{0:T(1024)S(1)} all-reduce(f32[2176]{0:T(1024)S(1)} %pad_maximum_fusion.14), channel_id=1, replica_groups=mesh['dp'=4,'ctx'=2,'tensor'=4] {'dp','ctx','tensor'}, use_global_device_ids=true, to_apply=%region_6.7 | all-reduce | flops 2176 | bytes 17408 | tf_op jit(solution)/shard_map/psum | solution.py:569
  612.3 4.3 collective-permute-done.31
  619.1 2.8 convert_dynamic-update-slice_fusion
  (282 shorter events, 110.6 us)
Async XLA Ops:
  7.2 61.5 %all-gather.10.cloned.1.call-start = ((), (), s32[]{:S(2)}) async-start(), calls=%async_computation.4 | async-start | bytes 1310720 | tf_op jit(solution)/shard_map/all_gather | solution.py:452
  9.0 74.6 %all-gather.12.cloned.1.call-start = ((), (), s32[]{:S(2)}) async-start(), calls=%async_computation.8 | async-start | bytes 1474560 | tf_op jit(solution)/shard_map/all_gather | solution.py:470
  9.8 135.2 %all-gather.14.cloned.1.call-start = ((), (), s32[]{:S(2)}) async-start(), calls=%async_computation.9 | async-start | bytes 1474560 | tf_op jit(solution)/shard_map/all_gather | solution.py:470
  11.6 133.5 %all-gather.16.cloned.1.call-start = ((), (), s32[]{:S(2)}) async-start(), calls=%async_computation.10 | async-start | bytes 1474560 | tf_op jit(solution)/shard_map/all_gather | solution.py:470
  14.2 52.5 %collective-permute-start = (bf16[512,1024]{1,0:T(8,128)(2,1)}, bf16[512,1024]{1,0:T(8,128)(2,1)}, u32[]{:S(2)}, u32[]{:S(2)}) collective-permute-start(bf16[512,1024]{1,0:T(8,128)(2,1)} %dynamic-slice_bitcast_fusion.3), channel_id=1, source_target_pairs={{0,4},{4,0},{1,5},{5,1},{2,6},{6,2},{3,7},{7,3},{8,12},{12,8},{9,1... | collective-permute-start | bytes 3145736 | tf_op jit(solution)/shard_map/ppermute | solution.py:412
  40.1 97.2 %collective-permute-start.3 = (bf16[256,1024]{0,1:T(8,128)(2,1)S(1)}, bf16[256,1024]{0,1:T(8,128)(2,1)S(1)}, u32[]{:S(2)}, u32[]{:S(2)}) collective-permute-start(bf16[256,1024]{0,1:T(8,128)(2,1)S(1)} %bitcast.152), channel_id=1, source_target_pairs={{0,2},{1,3},{2,0},{3,1},{4,6},{5,7},{6,4},{7,5},{8,10},{9,11},{10,... | collective-permute-start | bytes 1572872 | tf_op jit(solution)/shard_map/ppermute | solution.py:409
  43.8 35.1 %collective-permute-start.6 = (bf16[512,1024]{1,0:T(8,128)(2,1)}, bf16[512,1024]{1,0:T(8,128)(2,1)S(1)}, u32[]{:S(2)}, u32[]{:S(2)}) collective-permute-start(bf16[512,1024]{1,0:T(8,128)(2,1)} %dynamic-slice_bitcast_fusion.2), channel_id=1, source_target_pairs={{0,0},{5,1},{2,2},{7,3},{4,4},{1,5},{6,6},{3,7},{8,8},{13,9},{10,1... | collective-permute-start | bytes 3145736 | tf_op jit(solution)/shard_map/ppermute | solution.py:424
  46.6 440.3 %reduce-scatter.11.cloned.1.call-start = ((), (), s32[]{:S(2)}) async-start(), calls=%async_computation.7 | async-start | bytes 2654208 | tf_op jit(solution)/shard_map/reduce_scatter | solution.py:531
  66.7 16.9 %collective-permute-start.1 = (bf16[512,1024]{1,0:T(8,128)(2,1)}, bf16[512,1024]{1,0:T(8,128)(2,1)}, u32[]{:S(2)}, u32[]{:S(2)}) collective-permute-start(bf16[512,1024]{1,0:T(8,128)(2,1)} %collective-permute-done), channel_id=1, source_target_pairs={{0,1},{1,0},{2,3},{3,2},{4,5},{5,4},{6,7},{7,6},{8,9},{9,8},{10,11... | collective-permute-start | bytes 3145736 | tf_op jit(solution)/shard_map/ppermute | solution.py:406
  68.7 26.3 %collective-permute-start.2 = (bf16[1024,512]{1,0:T(8,128)(2,1)}, bf16[1024,512]{1,0:T(8,128)(2,1)}, u32[]{:S(2)}, u32[]{:S(2)}) collective-permute-start(bf16[1024,512]{1,0:T(8,128)(2,1)} %all-gather.10.cloned.1.call-done), channel_id=1, source_target_pairs={{0,2},{1,3},{2,0},{3,1},{4,6},{5,7},{6,4},{7,5},{8,10},{9,11},{10,... | collective-permute-start | bytes 3145736 | tf_op jit(solution)/shard_map/ppermute | solution.py:409
  78.8 64.1 %copy-start.6 = (bf16[512,1024]{1,0:T(8,128)(2,1)}, bf16[512,1024]{1,0:T(8,128)(2,1)S(1)}, u32[]{:S(2)}) copy-start(bf16[512,1024]{1,0:T(8,128)(2,1)S(1)} %collective-permute-done.6) | copy-start | bytes 3145732
  78.8 64.1 %collective-permute-start.7 = (bf16[512,1024]{1,0:T(8,128)(2,1)S(1)}, bf16[512,1024]{1,0:T(8,128)(2,1)S(1)}, u32[]{:S(2)}, u32[]{:S(2)}) collective-permute-start(bf16[512,1024]{1,0:T(8,128)(2,1)S(1)} %collective-permute-done.6), channel_id=1, source_target_pairs={{0,2},{1,3},{2,0},{3,1},{4,6},{5,7},{6,4},{7,5},{8,10},{9,11},{10,... | collective-permute-start | bytes 3145736 | tf_op jit(solution)/shard_map/ppermute | solution.py:409
  83.6 63.5 %collective-permute-start.9 = (bf16[4,128,1152]{2,1,0:T(8,128)(2,1)}, bf16[4,128,1152]{2,1,0:T(8,128)(2,1)}, u32[]{:S(2)}, u32[]{:S(2)}) collective-permute-start(bf16[4,128,1152]{2,1,0:T(8,128)(2,1)} %bitcast.157), channel_id=1, source_target_pairs={{0,4},{4,0},{1,5},{5,1},{2,6},{6,2},{3,7},{7,3},{8,12},{12,8},{9,1... | collective-permute-start | bytes 3538952 | tf_op jit(solution)/shard_map/ppermute | solution.py:412
  143.0 8.6 %collective-permute-start.4 = (bf16[512,1024]{1,0:T(8,128)(2,1)}, bf16[512,1024]{1,0:T(8,128)(2,1)}, u32[]{:S(2)}, u32[]{:S(2)}) collective-permute-start(bf16[512,1024]{1,0:T(8,128)(2,1)} %slice.201), channel_id=1, source_target_pairs={{0,1},{1,0},{2,3},{3,2},{4,5},{5,4},{6,7},{7,6},{8,9},{9,8},{10,11... | collective-permute-start | bytes 3145736 | tf_op jit(solution)/shard_map/ppermute | solution.py:406
  144.6 55.7 %collective-permute-start.8 = (bf16[2,512,1024]{2,1,0:T(8,128)(2,1)}, bf16[2,512,1024]{2,1,0:T(8,128)(2,1)}, u32[]{:S(2)}, u32[]{:S(2)}) collective-permute-start(bf16[2,512,1024]{2,1,0:T(8,128)(2,1)} %pad_maximum_fusion.1), channel_id=1, source_target_pairs={{0,1},{1,0},{2,3},{3,2},{4,5},{5,4},{6,7},{7,6},{8,9},{9,8},{10,11... | collective-permute-start | bytes 6291464 | tf_op jit(solution)/shard_map/ppermute | solution.py:406
  145.1 29.1 %collective-permute-start.10 = (bf16[4,128,1152]{2,1,0:T(8,128)(2,1)}, bf16[4,128,1152]{2,1,0:T(8,128)(2,1)}, u32[]{:S(2)}, u32[]{:S(2)}) collective-permute-start(bf16[4,128,1152]{2,1,0:T(8,128)(2,1)} %bitcast.155), channel_id=1, source_target_pairs={{0,4},{4,0},{1,5},{5,1},{2,6},{6,2},{3,7},{7,3},{8,12},{12,8},{9,1... | collective-permute-start | bytes 3538952 | tf_op jit(solution)/shard_map/ppermute | solution.py:412
  145.1 53.4 %collective-permute-start.11 = (bf16[4,576,256]{2,1,0:T(8,128)(2,1)}, bf16[4,576,256]{2,1,0:T(8,128)(2,1)S(1)}, u32[]{:S(2)}, u32[]{:S(2)}) collective-permute-start(bf16[4,576,256]{2,1,0:T(8,128)(2,1)} %bitcast.159), channel_id=1, source_target_pairs={{0,4},{4,0},{1,5},{5,1},{2,6},{6,2},{3,7},{7,3},{8,12},{12,8},{9,1... | collective-permute-start | bytes 3538952 | tf_op jit(solution)/shard_map/ppermute | solution.py:412
  153.9 51.8 %copy-start.15 = (bf16[512,1024]{1,0:T(8,128)(2,1)}, bf16[512,1024]{1,0:T(8,128)(2,1)S(1)}, u32[]{:S(2)}) copy-start(bf16[512,1024]{1,0:T(8,128)(2,1)S(1)} %multiply_convert_fusion) | copy-start | bytes 3145732
  153.9 51.8 %collective-permute-start.5 = (bf16[512,1024]{1,0:T(8,128)(2,1)S(1)}, bf16[512,1024]{1,0:T(8,128)(2,1)S(1)}, u32[]{:S(2)}, u32[]{:S(2)}) collective-permute-start(bf16[512,1024]{1,0:T(8,128)(2,1)S(1)} %multiply_convert_fusion), channel_id=1, source_target_pairs={{0,1},{1,0},{2,3},{3,2},{4,5},{5,4},{6,7},{7,6},{8,9},{9,8},{10,11... | collective-permute-start | bytes 3145736 | tf_op jit(solution)/shard_map/ppermute | solution.py:406
  154.0 53.4 %collective-permute-start.13 = (bf16[512,1024]{1,0:T(8,128)(2,1)S(1)}, bf16[512,1024]{1,0:T(8,128)(2,1)}, u32[]{:S(2)}, u32[]{:S(2)}) collective-permute-start(bf16[512,1024]{1,0:T(8,128)(2,1)S(1)} %multiply_convert_fusion), channel_id=1, source_target_pairs={{0,2},{1,3},{2,0},{3,1},{4,6},{5,7},{6,4},{7,5},{8,10},{9,11},{10,... | collective-permute-start | bytes 3145736 | tf_op jit(solution)/shard_map/ppermute | solution.py:409
  207.4 31.1 %collective-permute-start.14 = (bf16[512,1024]{1,0:T(8,128)(2,1)}, bf16[512,1024]{1,0:T(8,128)(2,1)}, u32[]{:S(2)}, u32[]{:S(2)}) collective-permute-start(bf16[512,1024]{1,0:T(8,128)(2,1)} %collective-permute-done.13), channel_id=1, source_target_pairs={{0,1},{1,0},{2,3},{3,2},{4,5},{5,4},{6,7},{7,6},{8,9},{9,8},{10,11... | collective-permute-start | bytes 3145736 | tf_op jit(solution)/shard_map/ppermute | solution.py:406
  269.4 224.0 %reduce-scatter.9.cloned.1.call-start = ((), (), s32[]{:S(2)}) async-start(), calls=%async_computation.6 | async-start | bytes 2654208 | tf_op jit(solution)/shard_map/reduce_scatter | solution.py:531
  275.9 9.8 %collective-permute-start.22 = (bf16[512,1024]{1,0:T(8,128)(2,1)}, bf16[512,1024]{1,0:T(8,128)(2,1)}, u32[]{:S(2)}, u32[]{:S(2)}) collective-permute-start(bf16[512,1024]{1,0:T(8,128)(2,1)} %slice.130), channel_id=1, source_target_pairs={{0,1},{1,0},{2,3},{3,2},{4,5},{5,4},{6,7},{7,6},{8,9},{9,8},{10,11... | collective-permute-start | bytes 3145736 | tf_op jit(solution)/shard_map/ppermute | solution.py:406
  282.4 212.6 %reduce-scatter.7.cloned.1.call-start = ((), (), s32[]{:S(2)}) async-start(), calls=%async_computation.5 | async-start | bytes 2654208 | tf_op jit(solution)/shard_map/reduce_scatter | solution.py:531
  284.1 6.1 collective-permute-start.15
  285.6 7.6 %collective-permute-start.21 = (bf16[512,1024]{1,0:T(8,128)(2,1)}, bf16[512,1024]{1,0:T(8,128)(2,1)}, u32[]{:S(2)}, u32[]{:S(2)}) collective-permute-start(bf16[512,1024]{1,0:T(8,128)(2,1)} %slice.128), channel_id=1, source_target_pairs={{0,1},{1,0},{2,3},{3,2},{4,5},{5,4},{6,7},{7,6},{8,9},{9,8},{10,11... | collective-permute-start | bytes 3145736 | tf_op jit(solution)/shard_map/ppermute | solution.py:406
  288.5 26.3 %collective-permute-start.23 = (bf16[512,1024]{1,0:T(8,128)(2,1)}, bf16[512,1024]{1,0:T(8,128)(2,1)}, u32[]{:S(2)}, u32[]{:S(2)}) collective-permute-start(bf16[512,1024]{1,0:T(8,128)(2,1)} %add_convert_fusion.4), channel_id=1, source_target_pairs={{0,2},{1,3},{2,0},{3,1},{4,6},{5,7},{6,4},{7,5},{8,10},{9,11},{10,... | collective-permute-start | bytes 3145736 | tf_op jit(solution)/shard_map/ppermute | solution.py:409
  290.0 27.5 %collective-permute-start.12 = (bf16[512,1024]{1,0:T(8,128)(2,1)}, bf16[512,1024]{1,0:T(8,128)(2,1)}, u32[]{:S(2)}, u32[]{:S(2)}) collective-permute-start(bf16[512,1024]{1,0:T(8,128)(2,1)} %slice.123), channel_id=1, source_target_pairs={{0,1},{1,0},{2,3},{3,2},{4,5},{5,4},{6,7},{7,6},{8,9},{9,8},{10,11... | collective-permute-start | bytes 3145736 | tf_op jit(solution)/shard_map/ppermute | solution.py:406
  291.6 45.2 %collective-permute-start.16 = (bf16[512,1024]{1,0:T(8,128)(2,1)}, bf16[512,1024]{1,0:T(8,128)(2,1)}, u32[]{:S(2)}, u32[]{:S(2)}) collective-permute-start(bf16[512,1024]{1,0:T(8,128)(2,1)} %add_convert_fusion.6), channel_id=1, source_target_pairs={{0,2},{1,3},{2,0},{3,1},{4,6},{5,7},{6,4},{7,5},{8,10},{9,11},{10,... | collective-permute-start | bytes 3145736 | tf_op jit(solution)/shard_map/ppermute | solution.py:409
  293.2 43.7 %copy-start.8 = (bf16[512,1024]{1,0:T(8,128)(2,1)S(1)}, bf16[512,1024]{1,0:T(8,128)(2,1)}, u32[]{:S(2)}) copy-start(bf16[512,1024]{1,0:T(8,128)(2,1)} %copy-done.6) | copy-start | bytes 3145732
  293.2 43.7 %copy-start.12 = (bf16[1024,1024]{1,0:T(8,128)(2,1)S(1)}, bf16[1024,1024]{1,0:T(8,128)(2,1)}, u32[]{:S(2)}) copy-start(bf16[1024,1024]{1,0:T(8,128)(2,1)} %get-tuple-element.42) | copy-start | bytes 6291460
  293.2 43.7 %copy-start.23 = (bf16[1024,1024]{1,0:T(8,128)(2,1)S(1)}, bf16[1024,1024]{1,0:T(8,128)(2,1)}, u32[]{:S(2)}) copy-start(bf16[1024,1024]{1,0:T(8,128)(2,1)} %get-tuple-element.39) | copy-start | bytes 6291460
  341.5 12.3 %collective-permute-start.24 = (bf16[512,1024]{1,0:T(8,128)(2,1)}, bf16[512,1024]{1,0:T(8,128)(2,1)S(1)}, u32[]{:S(2)}, u32[]{:S(2)}) collective-permute-start(bf16[512,1024]{1,0:T(8,128)(2,1)} %get-tuple-element.128), channel_id=1, source_target_pairs={{0,1},{1,0},{2,3},{3,2},{4,5},{5,4},{6,7},{7,6},{8,9},{9,8},{10,11... | collective-permute-start | bytes 3145736 | tf_op jit(solution)/shard_map/ppermute | solution.py:406
  350.7 257.8 %reduce-scatter.13.cloned.1.call-start = ((), (), s32[]{:S(2)}) async-start(), calls=%async_computation.11 | async-start | bytes 1769472 | tf_op jit(solution)/shard_map/reduce_scatter | solution.py:531
  351.9 71.2 %collective-permute-start.17 = (bf16[512,1024]{1,0:T(8,128)(2,1)S(1)}, bf16[512,1024]{1,0:T(8,128)(2,1)}, u32[]{:S(2)}, u32[]{:S(2)}) collective-permute-start(bf16[512,1024]{1,0:T(8,128)(2,1)S(1)} %copy-done.30), channel_id=1, source_target_pairs={{0,0},{1,5},{2,2},{3,7},{4,4},{5,1},{6,6},{7,3},{8,8},{9,13},{10,1... | collective-permute-start | bytes 3145736 | tf_op jit(solution)/shard_map/ppermute | solution.py:421
  422.4 64.9 %collective-permute-start.30 = (bf16[1024,768]{0,1:T(8,128)(2,1)}, bf16[1024,768]{0,1:T(8,128)(2,1)}, u32[]{:S(2)}, u32[]{:S(2)}) collective-permute-start(bf16[1024,768]{0,1:T(8,128)(2,1)} %pad_maximum_fusion.5), channel_id=1, source_target_pairs={{0,2},{1,3},{2,0},{3,1},{4,6},{5,7},{6,4},{7,5},{8,10},{9,11},{10,... | collective-permute-start | bytes 4718600 | tf_op jit(solution)/shard_map/ppermute | solution.py:409
  423.1 59.3 %collective-permute-start.18 = (bf16[512,1024]{1,0:T(8,128)(2,1)}, bf16[512,1024]{1,0:T(8,128)(2,1)}, u32[]{:S(2)}, u32[]{:S(2)}) collective-permute-start(bf16[512,1024]{1,0:T(8,128)(2,1)} %collective-permute-done.17), channel_id=1, source_target_pairs={{0,1},{1,0},{2,3},{3,2},{4,5},{5,4},{6,7},{7,6},{8,9},{9,8},{10,11... | collective-permute-start | bytes 3145736 | tf_op jit(solution)/shard_map/ppermute | solution.py:406
  423.5 58.9 %collective-permute-start.19 = (bf16[512,1024]{1,0:T(8,128)(2,1)}, bf16[512,1024]{1,0:T(8,128)(2,1)}, u32[]{:S(2)}, u32[]{:S(2)}) collective-permute-start(bf16[512,1024]{1,0:T(8,128)(2,1)} %collective-permute-done.17), channel_id=1, source_target_pairs={{0,2},{1,3},{2,0},{3,1},{4,6},{5,7},{6,4},{7,5},{8,10},{9,11},{10,... | collective-permute-start | bytes 3145736 | tf_op jit(solution)/shard_map/ppermute | solution.py:409
  432.9 65.0 %collective-permute-start.25 = (bf16[2,512,1024]{2,1,0:T(8,128)(2,1)}, bf16[2,512,1024]{2,1,0:T(8,128)(2,1)S(1)}, u32[]{:S(2)}, u32[]{:S(2)}) collective-permute-start(bf16[2,512,1024]{2,1,0:T(8,128)(2,1)} %dynamic-slice_bitcast_fusion), channel_id=1, source_target_pairs={{0,1},{1,0},{2,3},{3,2},{4,5},{5,4},{6,7},{7,6},{8,9},{9,8},{10,11... | collective-permute-start | bytes 6291464 | tf_op jit(solution)/shard_map/ppermute | solution.py:406
  482.3 66.7 %collective-permute-start.20 = (bf16[512,1024]{1,0:T(8,128)(2,1)}, bf16[512,1024]{1,0:T(8,128)(2,1)}, u32[]{:S(2)}, u32[]{:S(2)}) collective-permute-start(bf16[512,1024]{1,0:T(8,128)(2,1)} %collective-permute-done.19), channel_id=1, source_target_pairs={{0,1},{1,0},{2,3},{3,2},{4,5},{5,4},{6,7},{7,6},{8,9},{9,8},{10,11... | collective-permute-start | bytes 3145736 | tf_op jit(solution)/shard_map/ppermute | solution.py:406
  486.9 9.9 %collective-permute-start.34 = (bf16[128,1152]{1,0:T(8,128)(2,1)}, bf16[128,1152]{1,0:T(8,128)(2,1)}, u32[]{:S(2)}, u32[]{:S(2)}) collective-permute-start(bf16[128,1152]{1,0:T(8,128)(2,1)} %reduce-scatter.11.cloned.1.call-done), channel_id=1, source_target_pairs={{0,4},{4,0},{1,5},{5,1},{2,6},{6,2},{3,7},{7,3},{8,12},{12,8},{9,1... | collective-permute-start | bytes 884744 | tf_op jit(solution)/shard_map/ppermute | solution.py:412
  493.3 17.6 %collective-permute-start.33 = (bf16[128,1152]{1,0:T(8,128)(2,1)}, bf16[128,1152]{1,0:T(8,128)(2,1)}, u32[]{:S(2)}, u32[]{:S(2)}) collective-permute-start(bf16[128,1152]{1,0:T(8,128)(2,1)} %reduce-scatter.9.cloned.1.call-done), channel_id=1, source_target_pairs={{0,4},{4,0},{1,5},{5,1},{2,6},{6,2},{3,7},{7,3},{8,12},{12,8},{9,1... | collective-permute-start | bytes 884744 | tf_op jit(solution)/shard_map/ppermute | solution.py:412
  495.0 18.3 %collective-permute-start.32 = (bf16[128,1152]{1,0:T(8,128)(2,1)}, bf16[128,1152]{1,0:T(8,128)(2,1)}, u32[]{:S(2)}, u32[]{:S(2)}) collective-permute-start(bf16[128,1152]{1,0:T(8,128)(2,1)} %reduce-scatter.7.cloned.1.call-done), channel_id=1, source_target_pairs={{0,4},{4,0},{1,5},{5,1},{2,6},{6,2},{3,7},{7,3},{8,12},{12,8},{9,1... | collective-permute-start | bytes 884744 | tf_op jit(solution)/shard_map/ppermute | solution.py:412
  506.7 33.5 %collective-permute-start.26 = (bf16[512,1024]{1,0:T(8,128)(2,1)}, bf16[512,1024]{1,0:T(8,128)(2,1)}, u32[]{:S(2)}, u32[]{:S(2)}) collective-permute-start(bf16[512,1024]{1,0:T(8,128)(2,1)} %dynamic-slice_bitcast_fusion.1), channel_id=1, source_target_pairs={{0,4},{4,0},{1,5},{5,1},{2,6},{6,2},{3,7},{7,3},{8,12},{12,8},{9,1... | collective-permute-start | bytes 3145736 | tf_op jit(solution)/shard_map/ppermute | solution.py:412
  547.4 59.5 %collective-permute-start.27 = (bf16[512,1024]{1,0:T(8,128)(2,1)}, bf16[512,1024]{1,0:T(8,128)(2,1)S(1)}, u32[]{:S(2)}, u32[]{:S(2)}) collective-permute-start(bf16[512,1024]{1,0:T(8,128)(2,1)} %get-tuple-element.127), channel_id=1, source_target_pairs={{0,1},{1,0},{2,3},{3,2},{4,5},{5,4},{6,7},{7,6},{8,9},{9,8},{10,11... | collective-permute-start | bytes 3145736 | tf_op jit(solution)/shard_map/ppermute | solution.py:406
  547.4 59.5 %collective-permute-start.28 = (bf16[512,1024]{1,0:T(8,128)(2,1)}, bf16[512,1024]{1,0:T(8,128)(2,1)S(1)}, u32[]{:S(2)}, u32[]{:S(2)}) collective-permute-start(bf16[512,1024]{1,0:T(8,128)(2,1)} %get-tuple-element.127), channel_id=1, source_target_pairs={{0,2},{1,3},{2,0},{3,1},{4,6},{5,7},{6,4},{7,5},{8,10},{9,11},{10,... | collective-permute-start | bytes 3145736 | tf_op jit(solution)/shard_map/ppermute | solution.py:409
  606.9 12.1 %collective-permute-start.29 = (bf16[512,1024]{1,0:T(8,128)(2,1)S(1)}, bf16[512,1024]{1,0:T(8,128)(2,1)}, u32[]{:S(2)}, u32[]{:S(2)}) collective-permute-start(bf16[512,1024]{1,0:T(8,128)(2,1)S(1)} %collective-permute-done.28), channel_id=1, source_target_pairs={{0,1},{1,0},{2,3},{3,2},{4,5},{5,4},{6,7},{7,6},{8,9},{9,8},{10,11... | collective-permute-start | bytes 3145736 | tf_op jit(solution)/shard_map/ppermute | solution.py:406
  608.5 8.1 %collective-permute-start.31 = (bf16[128,768]{1,0:T(8,128)(2,1)}, bf16[128,768]{1,0:T(8,128)(2,1)S(1)}, u32[]{:S(2)}, u32[]{:S(2)}) collective-permute-start(bf16[128,768]{1,0:T(8,128)(2,1)} %reduce-scatter.13.cloned.1.call-done), channel_id=1, source_target_pairs={{0,4},{4,0},{1,5},{5,1},{2,6},{6,2},{3,7},{7,3},{8,12},{12,8},{9,1... | collective-permute-start | bytes 589832 | tf_op jit(solution)/shard_map/ppermute | solution.py:412
  (51 other events, 351.0 us)
Sparse Core Ops, SparseCore 0:
  10.2 37.0 all-gather.9
  49.4 30.3 all-gather.11
  81.4 29.1 all-gather.13
  112.0 29.5 all-gather.15
  269.5 65.3 reduce-scatter.10
  338.2 68.2 reduce-scatter.8
  410.1 68.3 reduce-scatter.6
  493.4 65.6 reduce-scatter.12

commit v2 on v1

v2 whole, which is shorter than its diff:
```python
import functools
import math

import jax
import jax.numpy as jnp
from jax import lax
from jax.experimental import pallas as pl
from jax.experimental.pallas import tpu as pltpu
from jax.sharding import PartitionSpec as P

HD = 64
LANES = 128
EPS = 1e-05
ROPE_BASE = 1000000.0
BF = jnp.bfloat16
F32 = jnp.float32
NT = (((1,), (1,)), ((), ()))
TN = (((0,), (0,)), ((), ()))
NN = (((1,), (0,)), ((), ()))
SCALE = HD ** (-0.5)
SCORE_SCALE = SCALE * math.log2(math.e)
VMEM_LIMIT = 56 * 1024 * 1024
COST_PART = 1000


def cost(flops, bytes_accessed, transcendentals):
    return pl.CostEstimate(flops=flops // COST_PART, bytes_accessed=bytes_accessed // COST_PART,
                           transcendentals=transcendentals // COST_PART)


def mm(a, b, dims=NN):
    return lax.dot_general(a, b, dims, preferred_element_type=F32)


def low_half(shape):
    return lax.broadcasted_iota(jnp.int32, shape, 1) % HD < HD // 2


def left_head(shape):
    return lax.broadcasted_iota(jnp.int32, shape, 1) < HD


def partner(x):
    return jnp.where(low_half(x.shape), pltpu.roll(x, LANES - HD // 2, 1), pltpu.roll(x, HD // 2, 1))


def head_mean(x):
    rows = lax.broadcasted_iota(jnp.int32, (LANES, LANES), 0) // HD
    cols = lax.broadcasted_iota(jnp.int32, (LANES, LANES), 1) // HD
    ones = jnp.where(rows == cols, 1.0 / HD, 0.0).astype(BF)
    high = x.astype(BF)
    rest = (x - high.astype(F32)).astype(BF)
    return mm(high, ones) + mm(rest, ones)


def project_kernel(x_ref, gain_ref, w_ref, cos_ref, sin_ref, qg_ref, kg_ref,
                   normed_ref, z_ref, q_ref, k_ref, v_ref):
    x = x_ref[...].astype(F32)
    scale = lax.rsqrt(jnp.mean(x * x, axis=-1, keepdims=True) + EPS)
    normed = (x * scale * gain_ref[...]).astype(BF)
    normed_ref[...] = normed
    out = mm(normed, w_ref[...])
    cos, sin = cos_ref[...], sin_ref[...]
    for kind, block, at in column_blocks(q_ref.shape[1], k_ref.shape[1]):
        z = out[:, at * LANES:(at + 1) * LANES]
        if kind == "v":
            both(z, v_ref, block)
            continue
        z_ref[:, at * LANES:(at + 1) * LANES] = z
        gain = qg_ref[...] if kind == "q" else kg_ref[...]
        n = z * lax.rsqrt(head_mean(z * z) + EPS) * gain
        turned = n * cos + partner(n) * sin
        if kind == "q":
            q_ref[:, block * LANES:(block + 1) * LANES] = turned.astype(BF)
        else:
            both(turned, k_ref, block)


def column_blocks(n_q, n_k_twice):
    n_q, n_k = n_q // (2 * LANES), n_k_twice // (4 * LANES)
    blocks, at = [], 0
    for shard in range(2):
        for kind, count in (("q", n_q), ("k", n_k), ("v", n_k)):
            for i in range(count):
                blocks.append((kind, shard * count + i, at))
                at += 1
    return blocks


def both(pair, ref, block):
    swapped = pltpu.roll(pair, HD, 1)
    left = left_head(pair.shape)
    at = 2 * block * LANES
    ref[:, at:at + LANES] = jnp.where(left, pair, swapped).astype(BF)
    ref[:, at + LANES:at + 2 * LANES] = jnp.where(left, swapped, pair).astype(BF)


def project(xs, gain, w_all, cos, sin, qgain, kgain, n_qcols, n_kcols, tb):
    tokens, width = xs.shape
    cols = w_all.shape[1]
    row = lambda b: (b, 0)
    fixed = lambda b: (0, 0)
    return pl.pallas_call(
        project_kernel,
        grid=(tokens // tb,),
        in_specs=[
            pl.BlockSpec((tb, width), row),
            pl.BlockSpec((1, width), fixed),
            pl.BlockSpec((width, cols), fixed),
            pl.BlockSpec((tb, LANES), row),
            pl.BlockSpec((tb, LANES), row),
            pl.BlockSpec((1, LANES), fixed),
            pl.BlockSpec((1, LANES), fixed),
        ],
        out_specs=[
            pl.BlockSpec((tb, width), row),
            pl.BlockSpec((tb, cols), row),
            pl.BlockSpec((tb, n_qcols), row),
            pl.BlockSpec((tb, 2 * n_kcols), row),
            pl.BlockSpec((tb, 2 * n_kcols), row),
        ],
        out_shape=[
            jax.ShapeDtypeStruct((tokens, width), BF),
            jax.ShapeDtypeStruct((tokens, cols), F32),
            jax.ShapeDtypeStruct((tokens, n_qcols), BF),
            jax.ShapeDtypeStruct((tokens, 2 * n_kcols), BF),
            jax.ShapeDtypeStruct((tokens, 2 * n_kcols), BF),
        ],
        cost_estimate=cost(flops=2 * tokens * width * cols, bytes_accessed=tokens * 14000, transcendentals=0),
        compiler_params=pltpu.CompilerParams(vmem_limit_bytes=VMEM_LIMIT),
        name="project",
    )(xs, gain, w_all, cos, sin, qgain, kgain)


def attend_kernel(ids, q_ref, k_ref, v_ref, o_ref, lse_ref, acc_a, acc_b):
    chunk = q_ref.shape[0]
    own = ids[pl.program_id(1)]
    left = left_head(q_ref.shape)
    q = q_ref[...]
    zero = jnp.zeros_like(q)
    q_a, q_b = jnp.where(left, q, zero), jnp.where(left, zero, q)
    acc_a[...] = jnp.zeros_like(acc_a)
    acc_b[...] = jnp.zeros_like(acc_b)

    def block(at, masked):
        rows = pl.ds(pl.multiple_of(at * chunk, chunk), chunk)
        k, v = k_ref[rows, :], v_ref[rows, :]
        one = jnp.ones_like(v)
        for q_one, v_one, acc in ((q_a, jnp.where(left, v, one), acc_a), (q_b, jnp.where(left, one, v), acc_b)):
            p = jnp.exp2(mm(q_one, k, NT) * SCORE_SCALE)
            if masked:
                allowed = lax.broadcasted_iota(jnp.int32, p.shape, 1) <= lax.broadcasted_iota(jnp.int32, p.shape, 0)
                p = jnp.where(allowed, p, 0.0)
            acc[...] += mm(p.astype(BF), v_one)

    @pl.loop(0, own)
    def _(at):
        block(at, False)

    block(own, True)
    a, b = acc_a[...], acc_b[...]
    total = pltpu.roll(jnp.where(left, b, a), HD, 1)
    o_ref[...] = (jnp.where(left, a, b) / total).astype(BF)
    rows = jnp.transpose(jnp.log2(total))
    lse_ref[0:1, :] = rows[0:1, :]
    lse_ref[1:2, :] = rows[HD:HD + 1, :]


def attend(ids, q, k, v, chunk):
    tokens, cols = q.shape
    pairs = cols // LANES
    return pl.pallas_call(
        attend_kernel,
        grid_spec=pltpu.PrefetchScalarGridSpec(
            num_scalar_prefetch=1,
            grid=(pairs, 2),
            in_specs=[
                pl.BlockSpec((chunk, LANES), lambda j, c, ids: (ids[c], j)),
                pl.BlockSpec((tokens, LANES), lambda j, c, ids: (0, j)),
                pl.BlockSpec((tokens, LANES), lambda j, c, ids: (0, j)),
            ],
            out_specs=[
                pl.BlockSpec((chunk, LANES), lambda j, c, ids: (c, j)),
                pl.BlockSpec((8, chunk), lambda j, c, ids: (j, c)),
            ],
            scratch_shapes=[pltpu.VMEM((chunk, LANES), F32)] * 2,
        ),
        out_shape=[
            jax.ShapeDtypeStruct((2 * chunk, cols), BF),
            jax.ShapeDtypeStruct((8 * pairs, 2 * chunk), F32),
        ],
        cost_estimate=cost(
            flops=pairs * 2 * 4 * LANES * chunk * (tokens + chunk), bytes_accessed=6 * tokens * cols,
            transcendentals=pairs * 2 * chunk * (tokens + chunk)),
        compiler_params=pltpu.CompilerParams(vmem_limit_bytes=VMEM_LIMIT),
        name="attend",
    )(ids, q, k, v)


def attend_back_kernel(ids, q_ref, k_ref, v_ref, o_ref, do_ref, lse_ref, dq_ref, dk_ref, dv_ref):
    chunk = q_ref.shape[0]
    own = ids[pl.program_id(1)]
    left = left_head(q_ref.shape)
    q, do = q_ref[...], do_ref[...]
    zero = jnp.zeros_like(q)
    q_a, q_b = jnp.where(left, q, zero), jnp.where(left, zero, q)
    do_a, do_b = jnp.where(left, do, zero), jnp.where(left, zero, do)
    prod = jnp.transpose(do.astype(F32) * o_ref[...].astype(F32))
    delta_a = jnp.sum(prod[:HD], axis=0, keepdims=True)
    delta_b = jnp.sum(prod[HD:], axis=0, keepdims=True)
    lse_a, lse_b = lse_ref[0:1, :], lse_ref[1:2, :]
    dq_ref[...] = jnp.zeros_like(dq_ref)

    @pl.when(pl.program_id(1) == 0)
    def _():
        dk_ref[...] = jnp.zeros_like(dk_ref)
        dv_ref[...] = jnp.zeros_like(dv_ref)

    def block(at, masked):
        rows = pl.ds(pl.multiple_of(at * chunk, chunk), chunk)
        k, v = k_ref[rows, :], v_ref[rows, :]
        k_a, k_b = jnp.where(left, k, zero), jnp.where(left, zero, k)
        for q_one, do_one, k_one, lse, delta in ((q_a, do_a, k_a, lse_a, delta_a), (q_b, do_b, k_b, lse_b, delta_b)):
            p = jnp.exp2(mm(k, q_one, NT) * SCORE_SCALE - lse)
            if masked:
                allowed = lax.broadcasted_iota(jnp.int32, p.shape, 0) <= lax.broadcasted_iota(jnp.int32, p.shape, 1)
                p = jnp.where(allowed, p, 0.0)
            ds = (p * (mm(v, do_one, NT) - delta)).astype(BF)
            dv_ref[rows, :] += mm(p.astype(BF), do_one)
            dk_ref[rows, :] += mm(ds, q_one)
            dq_ref[...] += mm(ds, k_one, TN)

    @pl.loop(0, own)
    def _(at):
        block(at, False)

    block(own, True)


def attend_back(ids, q, k, v, o, do, lse, chunk, group):
    tokens, cols = q.shape
    pairs = cols // LANES // 2
    first = group * pairs
    whole = pl.BlockSpec((tokens, LANES), lambda j, c, ids: (0, first + j))
    mine = pl.BlockSpec((chunk, LANES), lambda j, c, ids: (c, first + j))
    natural = pl.BlockSpec((chunk, LANES), lambda j, c, ids: (ids[c], first + j))
    total = pl.BlockSpec((tokens, LANES), lambda j, c, ids: (0, j))
    return pl.pallas_call(
        attend_back_kernel,
        grid_spec=pltpu.PrefetchScalarGridSpec(
            num_scalar_prefetch=1,
            grid=(pairs, 2),
            in_specs=[natural, whole, whole, mine, mine, pl.BlockSpec((8, chunk), lambda j, c, ids: (first + j, c))],
            out_specs=[pl.BlockSpec((chunk, LANES), lambda j, c, ids: (ids[c], j)), total, total],
        ),
        out_shape=[jax.ShapeDtypeStruct((tokens, cols // 2), F32)] * 3,
        cost_estimate=cost(
            flops=pairs * 2 * 10 * LANES * chunk * (tokens + chunk), bytes_accessed=9 * tokens * cols,
            transcendentals=pairs * 2 * chunk * (tokens + chunk)),
        compiler_params=pltpu.CompilerParams(vmem_limit_bytes=VMEM_LIMIT),
        name="attend_back",
    )(ids, q, k, v, o, do, lse)


def turn_back_kernel(ids, z_ref, dq_ref, dk_ref, dv_ref, cos_ref, sin_ref, qg_ref, kg_ref, out_ref, gain_ref, *, per_chunk):
    step = pl.program_id(0)
    blocks = column_blocks(2 * dq_ref.shape[1], 2 * dk_ref.shape[1])
    blocks = blocks[:len(blocks) // 2]
    cos, sin = cos_ref[...], sin_ref[...]

    @pl.when(step == 0)
    def _():
        gain_ref[...] = jnp.zeros_like(gain_ref)

    def back(block, d, gain, row):
        z = z_ref[:, block * LANES:(block + 1) * LANES]
        scale = lax.rsqrt(head_mean(z * z) + EPS)
        d = d * SCALE
        dn = d * cos - partner(d) * sin
        zr = z * scale
        gain_ref[row:row + 1, :] += jnp.sum(dn * zr, axis=0, keepdims=True)
        gdn = gain * dn
        out_ref[:, block * LANES:(block + 1) * LANES] = (scale * (gdn - zr * head_mean(zr * gdn))).astype(BF)

    own = jnp.logical_or(step // per_chunk == ids[0], step // per_chunk == ids[1])

    @pl.when(own)
    def _():
        for kind, block, at in blocks:
            if kind == "q":
                back(at, dq_ref[:, block * LANES:(block + 1) * LANES], qg_ref[...], 0)

    @pl.when(jnp.logical_not(own))
    def _():
        for kind, _, at in blocks:
            if kind == "q":
                out_ref[:, at * LANES:(at + 1) * LANES] = jnp.zeros((out_ref.shape[0], LANES), BF)

    def folded(ref, block):
        at = 2 * block * LANES
        one, two = ref[:, at:at + LANES], ref[:, at + LANES:at + 2 * LANES]
        one, two = one + pltpu.roll(one, HD, 1), two + pltpu.roll(two, HD, 1)
        return jnp.where(left_head(one.shape), one, two)

    for kind, block, at in blocks:
        if kind == "k":
            back(at, folded(dk_ref, block), kg_ref[...], 1)
        if kind == "v":
            out_ref[:, at * LANES:(at + 1) * LANES] = folded(dv_ref, block).astype(BF)


def turn_back(ids, z, dq, dk, dv, cos, sin, qgain, kgain, tb, chunk, group):
    tokens = z.shape[0]
    n_q, n_k = dq.shape[1], dk.shape[1] // 2
    row = lambda b, ids: (b, 0)
    fixed = lambda b, ids: (0, 0)
    return pl.pallas_call(
        functools.partial(turn_back_kernel, per_chunk=chunk // tb),
        grid_spec=pltpu.PrefetchScalarGridSpec(
            num_scalar_prefetch=1,
            grid=(tokens // tb,),
            in_specs=[
                pl.BlockSpec((tb, n_q + 2 * n_k), lambda b, ids: (b, group)),
                pl.BlockSpec((tb, n_q), row),
                pl.BlockSpec((tb, 2 * n_k), row),
                pl.BlockSpec((tb, 2 * n_k), row),
                pl.BlockSpec((tb, LANES), row),
                pl.BlockSpec((tb, LANES), row),
                pl.BlockSpec((1, LANES), fixed),
                pl.BlockSpec((1, LANES), fixed),
            ],
            out_specs=[pl.BlockSpec((tb, n_q + 2 * n_k), row), pl.BlockSpec((8, LANES), fixed)],
        ),
        out_shape=[
            jax.ShapeDtypeStruct((tokens, n_q + 2 * n_k), BF),
            jax.ShapeDtypeStruct((8, LANES), F32),
        ],
        cost_estimate=cost(flops=tokens * 200000, bytes_accessed=tokens * 12000, transcendentals=0),
        compiler_params=pltpu.CompilerParams(vmem_limit_bytes=VMEM_LIMIT),
        name="turn_back",
    )(ids, z, dq, dk, dv, cos, sin, qgain, kgain)


def feed_kernel(place, *refs, n_pieces):
    hn_a, hn_b, dy_a, dy_b = refs[:4]
    pieces, rest = [], refs[4:]
    for count in n_pieces:
        pieces.append(rest[:count])
        rest = rest[count:]
    act_ref, dg_ref, du_ref, out_a, out_b, dhn_a, dhn_b, wg_ref, wu_ref, wd_ref, sems = rest
    step, steps = pl.program_id(0), pl.num_programs(0)
    early = step < steps // 2
    n_dp = wd_ref.shape[0]
    part = wd_ref.shape[2]

    def copies(weight):
        made = []
        for half, source in enumerate(pieces[weight]):
            rows = source.shape[1]
            offset = (place[0] if half == 0 else 1 - place[0]) * rows if n_pieces[weight] == 2 else 0
            for i in range(n_dp):
                if weight < 2:
                    target = (wg_ref, wu_ref)[weight]
                    window = target.at[pl.ds(pl.multiple_of(i * n_pieces[weight] * rows + offset, rows), rows), :]
                else:
                    window = wd_ref.at[i, pl.ds(pl.multiple_of(offset, rows), rows), :]
                made.append(pltpu.make_async_copy(source.at[i], window, sems.at[weight, half, i]))
        return made

    @pl.when(step == 0)
    def _():
        for weight in range(3):
            for copy in copies(weight):
                copy.start()
        for weight in range(3):
            for copy in copies(weight):
                copy.wait()

    hn = jnp.where(early, hn_a[...], hn_b[...])
    dy = jnp.where(early, dy_a[...], dy_b[...])
    gate = mm(hn, wg_ref[...])
    up = mm(hn, wu_ref[...])
    dact = mm(dy[:, :part], wd_ref[0], NT)
    for i in range(1, n_dp):
        dact += mm(dy[:, i * part:(i + 1) * part], wd_ref[i], NT)
    sig = 1.0 / (1.0 + jnp.exp(-gate))
    silu = gate * sig
    act = (silu * up).astype(BF)
    dg = (dact * up * (sig + silu * (1.0 - sig))).astype(BF)
    du = (dact * silu).astype(BF)
    act_ref[...] = act
    dg_ref[...] = dg
    du_ref[...] = du
    dhn = (mm(dg, wg_ref[...], NT) + mm(du, wu_ref[...], NT)).astype(BF)
    out = [mm(act, wd_ref[i]).astype(BF) for i in range(n_dp)]

    def store(dhn_ref, out_ref):
        dhn_ref[...] = dhn
        for i in range(n_dp):
            out_ref[:, i * part:(i + 1) * part] = out[i]

    @pl.when(early)
    def _():
        store(dhn_a, out_a)

    @pl.when(jnp.logical_not(early))
    def _():
        store(dhn_b, out_b)


def feed(place, hn, dy, gate, up, down, tb):
    chunk, width = hn[0].shape
    n_dp, _, units = gate[0].shape
    n_pieces = (len(gate), len(up), len(down))
    steps = 2 * chunk // tb
    row = lambda b, p: (b, 0)
    a = pl.BlockSpec((tb, width), lambda b, p: (jnp.minimum(b, steps // 2 - 1), 0))
    b = pl.BlockSpec((tb, width), lambda b, p: (jnp.maximum(b - steps // 2, 0), 0))
    anywhere = pl.BlockSpec(memory_space=pl.ANY)
    return pl.pallas_call(
        functools.partial(feed_kernel, n_pieces=n_pieces),
        grid_spec=pltpu.PrefetchScalarGridSpec(
            num_scalar_prefetch=1,
            grid=(steps,),
            in_specs=[a, b, a, b] + [anywhere] * sum(n_pieces),
            out_specs=[pl.BlockSpec((tb, units), row)] * 3 + [a, b, a, b],
            scratch_shapes=[
                pltpu.VMEM((width, units), BF),
                pltpu.VMEM((width, units), BF),
                pltpu.VMEM((n_dp, units, width // n_dp), BF),
                pltpu.SemaphoreType.DMA((3, 2, n_dp)),
            ],
        ),
        out_shape=[jax.ShapeDtypeStruct((2 * chunk, units), BF)] * 3 + [jax.ShapeDtypeStruct((chunk, width), BF)] * 4,
        cost_estimate=cost(flops=24 * chunk * width * units, bytes_accessed=6 * width * units + chunk * 30000,
                           transcendentals=2 * chunk * units),
        compiler_params=pltpu.CompilerParams(vmem_limit_bytes=VMEM_LIMIT),
        name="feed",
    )(place, *hn, *dy, *gate, *up, *down)


def weight_grad_kernel(place, *refs, n_left, n_right, n_dp):
    lefts, rights, give_ref, keep_ref = refs[:n_left * n_dp], refs[n_left * n_dp:-2], refs[-2], refs[-1]
    total, right, at = None, 0, 0
    for i in range(n_left):
        tall = jnp.concatenate([lefts[i * n_dp + j][...] for j in range(n_dp)], axis=1)
        tokens = tall.shape[0]
        term = mm(tall, rights[right][at:at + tokens, :], TN)
        total = term if total is None else total + term
        at += tokens
        if at == rights[right].shape[0]:
            right, at = right + 1, 0
    total = total.astype(BF).reshape(give_ref.shape)

    @pl.when(pl.program_id(0) == 0)
    def _():
        give_ref[...] = total

    @pl.when(pl.program_id(0) == 1)
    def _():
        keep_ref[...] = total


def weight_grad(place, lefts, rights, n_dp):
    width, units = lefts[0].shape[1], rights[0].shape[1]
    rows = width // (2 * n_dp)
    tokens = sum(left.shape[0] for left in lefts)

    def column(left, i):
        return pl.BlockSpec((left.shape[0], rows), lambda h, p: (0, 2 * i + jnp.where(h == 0, 1 - p[0], p[0])))

    return pl.pallas_call(
        functools.partial(weight_grad_kernel, n_left=len(lefts), n_right=len(rights), n_dp=n_dp),
        grid_spec=pltpu.PrefetchScalarGridSpec(
            num_scalar_prefetch=1,
            grid=(2,),
            in_specs=[column(left, i) for left in lefts for i in range(n_dp)]
            + [pl.BlockSpec(right.shape, lambda h, p: (0, 0), pipeline_mode=pl.Buffered(1)) for right in rights],
            out_specs=[pl.BlockSpec((n_dp, rows, units), lambda h, p: (0, 0, 0))] * 2,
        ),
        out_shape=[jax.ShapeDtypeStruct((n_dp, rows, units), BF)] * 2,
        cost_estimate=cost(flops=2 * tokens * width * units, bytes_accessed=2 * tokens * (width + units), transcendentals=0),
        compiler_params=pltpu.CompilerParams(vmem_limit_bytes=VMEM_LIMIT),
        name="weight_grad",
    )(place, *[left for left in lefts for _ in range(n_dp)], *rights)


def put_kernel(where, a_ref, b_ref, *refs):
    out_ref = refs[-1]

    @pl.when(pl.program_id(0) == 0)
    def _():
        out_ref[...] = a_ref[...].astype(out_ref.dtype)

    @pl.when(pl.program_id(0) == 1)
    def _():
        out_ref[...] = b_ref[...].astype(out_ref.dtype)


def put(where, a, b, into, kind):
    chunk, width = a.shape
    tb = min(256, chunk)
    per = chunk // tb
    more = () if into is None else (into,)
    return pl.pallas_call(
        put_kernel,
        grid_spec=pltpu.PrefetchScalarGridSpec(
            num_scalar_prefetch=1,
            grid=(2, per),
            in_specs=[
                pl.BlockSpec((tb, width), lambda i, r, w: (jnp.where(i == 0, r, per - 1), 0)),
                pl.BlockSpec((tb, width), lambda i, r, w: (jnp.where(i == 1, r, 0), 0)),
            ] + [pl.BlockSpec(memory_space=pl.ANY)] * len(more),
            out_specs=pl.BlockSpec((tb, width), lambda i, r, w: (jnp.where(i == 0, w[0], w[1]) * per + r, 0)),
        ),
        out_shape=jax.ShapeDtypeStruct((4 * chunk, width), kind),
        input_output_aliases={3: 0} if more else {},
        cost_estimate=cost(flops=chunk, bytes_accessed=12 * chunk * width, transcendentals=0),
        compiler_params=pltpu.CompilerParams(vmem_limit_bytes=VMEM_LIMIT),
        name="put",
    )(where, a, b, *more)


def unproject_kernel(parity, a_ref, b_ref, w_ref, out_ref):
    half = a_ref.shape[1]
    out = mm(a_ref[...], w_ref[:, :half], NT) + mm(b_ref[...], w_ref[:, half:], NT)
    out_ref[...] = out.astype(BF)


def unproject(parity, a, b, w, tb, chunk):
    tokens, half = a.shape
    width = w.shape[0]
    per = chunk // tb
    natural = lambda r, p: ((2 * (r // per) + p[0]) * per + r % per, 0)
    return pl.pallas_call(
        unproject_kernel,
        grid_spec=pltpu.PrefetchScalarGridSpec(
            num_scalar_prefetch=1,
            grid=(tokens // 2 // tb,),
            in_specs=[pl.BlockSpec((tb, half), natural), pl.BlockSpec((tb, half), natural),
                      pl.BlockSpec(w.shape, lambda r, p: (0, 0))],
            out_specs=pl.BlockSpec((tb, width), lambda r, p: (r, 0)),
        ),
        out_shape=jax.ShapeDtypeStruct((tokens // 2, width), BF),
        cost_estimate=cost(flops=2 * tokens * width * half, bytes_accessed=4 * tokens * width, transcendentals=0),
        compiler_params=pltpu.CompilerParams(vmem_limit_bytes=VMEM_LIMIT),
        name="unproject",
    )(parity, a, b, w)


def close_kernel(where, a_ref, b_ref, w_ref, got_ref, x_ref, gain_ref, dhidden_ref, dz_ref, *, per):
    step = pl.program_id(0)
    half = a_ref.shape[1]
    dn = mm(a_ref[...], w_ref[:, :half], NT) + mm(b_ref[...], w_ref[:, half:], NT) + got_ref[...].astype(F32)
    x = x_ref[...].astype(F32)
    scale = lax.rsqrt(jnp.mean(x * x, axis=-1, keepdims=True) + EPS)
    zr = x * scale
    gdn = gain_ref[...] * dn
    dz = scale * (gdn - zr * jnp.mean(zr * gdn, axis=-1, keepdims=True))
    dz += jnp.where(step // per == where[1], dhidden_ref[...], 0.0)
    dz_ref[...] = dz.astype(BF)


def close(where, a, b, w, got, xs, gain, dhidden, tb, chunk):
    tokens, width = got.shape
    half = a.shape[1]
    per = chunk // tb
    row = lambda r, p: (r, 0)
    fixed = lambda r, p: (0, 0)
    natural = lambda r, p: ((2 * (r // per) + p[0]) * per + r % per, 0)
    return pl.pallas_call(
        functools.partial(close_kernel, per=per),
        grid_spec=pltpu.PrefetchScalarGridSpec(
            num_scalar_prefetch=1,
            grid=(tokens // tb,),
            in_specs=[
                pl.BlockSpec((tb, half), natural),
                pl.BlockSpec((tb, half), natural),
                pl.BlockSpec(w.shape, fixed),
                pl.BlockSpec((tb, width), row),
                pl.BlockSpec((tb, width), natural),
                pl.BlockSpec((1, width), fixed),
                pl.BlockSpec((tb, width), lambda r, p: (r % per, 0)),
            ],
            out_specs=pl.BlockSpec((tb, width), row),
        ),
        out_shape=jax.ShapeDtypeStruct((tokens, width), BF),
        cost_estimate=cost(flops=4 * tokens * width * half, bytes_accessed=10 * tokens * width, transcendentals=0),
        compiler_params=pltpu.CompilerParams(vmem_limit_bytes=VMEM_LIMIT),
        name="close",
    )(where, a, b, w, got, xs, gain, dhidden)


def rope_tables(length):
    positions = lax.optimization_barrier(jnp.arange(length, dtype=jnp.int32))
    frequency = ROPE_BASE ** (-jnp.arange(0, HD, 2).astype(F32) / HD)
    angles = positions.astype(F32)[:, None] * frequency[None, :]
    cos, sin = jnp.cos(angles), jnp.sin(angles)
    return jnp.concatenate([cos] * 4, axis=1), jnp.concatenate([-sin, sin] * 2, axis=1)


def tie(*values):
    return lax.optimization_barrier(values)


def rms(z):
    return lax.rsqrt(jnp.mean(z * z, axis=-1, keepdims=True) + EPS)


def norm_back(z, scale, gain, dn):
    zr = z * scale
    gdn = gain * dn
    return scale * (gdn - zr * jnp.mean(zr * gdn, axis=-1, keepdims=True))


def on_device(layer_input, cotangent, attn_gain, query_weight, key_weight, value_weight, query_gain, key_gain,
              out_weight, ffn_gain, gate_weight, up_weight, down_weight):
    n_dp, n_ctx, n_tensor = (lax.axis_size(a) for a in ("dp", "ctx", "tensor"))
    seqs, local_len, width = layer_input.shape
    assert seqs == 2 and n_tensor == 4
    chunk = local_len // 2
    length = local_len * n_ctx
    t = lax.axis_index("tensor")
    seq, core = t // 2, t % 2
    ctx = lax.axis_index("ctx")

    def own_chunk(place, which):
        return jnp.where(place % 2 == which, place, 2 * n_ctx - 1 - place)

    id_here, id_there = own_chunk(ctx, core), own_chunk(ctx, 1 - core)
    ids = jnp.stack([id_here, id_there]).astype(jnp.int32)

    def swap_core(x):
        return lax.ppermute(x, "tensor", [(i, i ^ 1) for i in range(n_tensor)])

    def swap_seq(x):
        return lax.ppermute(x, "tensor", [(i, i ^ 2) for i in range(n_tensor)])

    def swap_ctx(x):
        return lax.ppermute(x, "ctx", [(0, 1), (1, 0)])

    homes = []
    for place in range(n_ctx):
        for i in range(n_tensor):
            which = place if place % 2 == i % 2 else 2 * n_ctx - 1 - place
            homes.append((place * n_tensor + i, (which // 2) * n_tensor + i))

    def send_home(x):
        return lax.ppermute(x, ("ctx", "tensor"), homes)

    def fetch_from_home(x):
        return lax.ppermute(x, ("ctx", "tensor"), [(b, a) for a, b in homes])

    def ctx_pair(x, axis):
        if n_ctx != 2:
            return lax.all_gather(x, "ctx", axis=axis, tiled=False)
        other = swap_ctx(x)
        return jnp.where(ctx == 0, jnp.stack([x, other], axis), jnp.stack([other, x], axis))

    x_here = lax.dynamic_index_in_dim(layer_input, seq, 0, keepdims=False)
    if n_ctx == 2:
        first = swap_ctx(lax.dynamic_slice(layer_input, (seq, core * chunk, 0), (1, chunk, width))[0])
        second = swap_core(first)
        xs = jnp.zeros((length, width), BF)
        xs = lax.dynamic_update_slice(xs, x_here, (ctx * local_len, 0))
        xs = lax.dynamic_update_slice(xs, first, ((1 - ctx) * local_len + core * chunk, 0))
        xs = lax.dynamic_update_slice(xs, second, ((1 - ctx) * local_len + (1 - core) * chunk, 0))
    else:
        xs = lax.all_gather(x_here, "ctx", axis=0, tiled=True)

    d_part, h_part = attn_gain.shape[0], query_gain.shape[0]
    nq, nk = query_weight.shape[1], key_weight.shape[1]
    n_qkv = nq + 2 * nk
    gains = jnp.concatenate([attn_gain, ffn_gain, query_gain, key_gain])
    gain_rows = -(-gains.shape[0] // LANES)
    gains = jnp.pad(gains, (0, gain_rows * LANES - gains.shape[0])).reshape(gain_rows, LANES)
    gains = jnp.pad(gains, ((0, d_part - gain_rows), (0, 0)))
    piece = jnp.concatenate([query_weight, key_weight, value_weight, gains], axis=1)
    dp = lax.axis_index("dp")
    w_all = jnp.zeros((width, 2 * n_qkv), BF)
    gains = jnp.zeros((n_dp, gain_rows, LANES), BF)
    for hop in range(n_dp):
        owner = (dp + n_dp - hop) % n_dp
        w_all = lax.dynamic_update_slice(w_all, piece[:, :n_qkv], (owner * d_part, 0))
        w_all = lax.dynamic_update_slice(w_all, swap_seq(piece[:, :n_qkv]), (owner * d_part, n_qkv))
        gains = lax.dynamic_update_slice(gains, piece[None, :gain_rows, n_qkv:], (owner, 0, 0))
        if hop < n_dp - 1:
            piece = lax.ppermute(piece, "dp", [(i, (i + 1) % n_dp) for i in range(n_dp)])
    gains = gains.reshape(n_dp, gain_rows * LANES)
    gain_a = gains[:, :d_part].reshape(1, width).astype(F32)
    gain_f = gains[:, d_part:2 * d_part].reshape(1, width).astype(F32)
    gain_q = jnp.tile(gains[:, 2 * d_part:2 * d_part + h_part].reshape(1, HD).astype(F32), (1, 2))
    gain_k = jnp.tile(gains[:, 2 * d_part + h_part:2 * d_part + 2 * h_part].reshape(1, HD).astype(F32), (1, 2))

    def half_rows(w):
        rows = w.shape[0] // 2
        return lax.dynamic_slice_in_dim(w, ctx * rows, rows, 0) if n_ctx == 2 else w

    def gather_dp(w):
        return lax.all_gather(w, "dp", axis=0, tiled=False)

    h_out = out_weight.shape[0]
    got = gather_dp(jnp.concatenate([out_weight, half_rows(down_weight)], axis=0))
    out_mine = got[:, :h_out].transpose(1, 0, 2).reshape(h_out, width)
    out_theirs = swap_seq(out_mine)
    down = [got[:, h_out:]]
    gate = [gather_dp(half_rows(gate_weight))]
    up = [gather_dp(up_weight)]
    if n_ctx == 2:
        down.append(swap_ctx(down[0]))

    cot_home = lax.dynamic_slice(cotangent, (seq, core * chunk, 0), (1, chunk, width))[0]
    dy_0 = fetch_from_home(cot_home)
    dy_2 = swap_seq(dy_0)
    dy_02 = jnp.stack([dy_0, dy_2])
    dy_13 = swap_core(dy_02)
    dy_own, dy_other = [dy_0, dy_13[0]], [dy_2, dy_13[1]]

    tb = min(256, chunk)
    cos, sin = rope_tables(length)
    normed, z, q, k, v = project(xs, gain_a, w_all, cos, sin, gain_q, gain_k, 2 * nq, 2 * nk, tb)
    if n_ctx == 2:
        q, down[1], gate[0] = tie(q, down[1], gate[0])
        gate.append(swap_ctx(gate[0]))
    o, lse = attend(ids, q, k, v, chunk)
    if n_ctx == 2:
        o, gate[1] = tie(o, gate[1])
    w_out = jnp.concatenate([out_mine, out_theirs], axis=0)
    attn = mm(o, w_out)
    got = swap_core(attn[chunk:].astype(BF))
    x_0 = lax.dynamic_slice_in_dim(xs, id_here * chunk, chunk, 0).astype(F32)
    hidden = x_0 + (attn[:chunk] + got.astype(F32))
    h_scale = rms(hidden)
    hn_0 = (hidden * h_scale * gain_f).astype(BF)
    hn_1 = swap_core(hn_0)
    hn_2 = swap_seq(hn_0)

    place = jnp.reshape(ctx, (1,)).astype(jnp.int32)

    def added(a, b):
        return (a.astype(F32) + b.astype(F32)).astype(BF)

    act_o, dg_o, du_o, y_0, y_1, dhn_0, dhn_1 = feed(place, [hn_0, hn_1], dy_own, gate, up, down, tb)
    act_o, hn_2 = tie(act_o, hn_2)
    hn_3 = swap_core(hn_2)
    act_t, dg_t, du_t, y_2, y_3, dhn_2, dhn_3 = feed(place, [hn_2, hn_3], dy_other, gate, up, down, tb)
    dhn_send = added(dhn_2, swap_core(dhn_3))
    dhn_got = swap_seq(dhn_send)

    def weight_sum(lefts, rights):
        if n_ctx == 2:
            return weight_grad(place, lefts, rights, n_dp)
        return None, mm(jnp.concatenate(lefts, axis=0), jnp.concatenate(rights, axis=0), TN).astype(BF)

    def to_ctx(give, keep):
        return swap_ctx(give) if n_ctx == 2 else keep[:1]

    def ctx_sum(keep, got):
        return added(keep, got) if n_ctx == 2 else keep

    def scatter(half):
        if n_ctx == 2:
            return lax.psum_scatter(half, "dp", scatter_dimension=0, tiled=False)
        return lax.psum_scatter(half, ("dp", "ctx"), scatter_dimension=0, tiled=True)

    def gather_rows(mine):
        return ctx_pair(mine, 0).reshape(width // n_dp, mine.shape[1])

    hn_all, dy_all = [hn_0, hn_1, hn_2, hn_3], dy_own + dy_other
    act_t, dg_t, du_t, dhn_send = tie(act_t, dg_t, du_t, dhn_send)
    give, g_gate = weight_sum(hn_all, [dg_o, dg_t])
    gate_got = to_ctx(give, g_gate)
    du_o, g_gate = tie(du_o, g_gate)
    give, g_up = weight_sum(hn_all, [du_o, du_t])
    up_got = to_ctx(give, g_up)
    act_o, g_up = tie(act_o, g_up)
    give, g_down = weight_sum(dy_all, [act_o, act_t])
    dhn_got, g_down, gate_got = tie(dhn_got, g_down, gate_got)
    down_got = to_ctx(give, g_down)

    y_send, dhn_got = tie(added(y_2, swap_core(y_3)), dhn_got)
    y_got = swap_seq(y_send)
    dhn = dhn_0.astype(F32) + swap_core(dhn_1).astype(F32) + dhn_got.astype(F32)
    dhidden = dy_0.astype(F32) + norm_back(hidden, h_scale, gain_f, dhn)
    dhr_0 = dhidden.astype(BF)
    dhr_1 = swap_core(dhr_0)
    do = mm(jnp.concatenate([dhr_0, dhr_1], axis=0), w_out, NT).astype(BF)

    def ordinal(s, c):
        return 2 * s + c

    blocks = jnp.stack([ordinal(seq, core), ordinal(seq, 1 - core), ordinal(1 - seq, core), ordinal(1 - seq, 1 - core)])
    blocks = blocks.astype(jnp.int32)

    out_give, out_keep = weight_sum([dhr_0, dhr_1], [o])
    do, gate_got, out_keep = tie(do, gate_got, out_keep)
    s_gate = scatter(ctx_sum(g_gate, gate_got))
    if n_ctx == 2:
        out_theirs_got = swap_seq(jnp.concatenate([out_give[..., h_out:], out_keep[..., h_out:]], axis=0))
        out_mine = jnp.concatenate([out_give[..., :h_out], out_keep[..., :h_out]], axis=0)
    else:
        out_theirs_got, out_mine = swap_seq(out_keep[..., h_out:]), out_keep[..., :h_out]
    dq, dk, dv = attend_back(ids, q, k, v, o, do, lse, chunk, 1)
    dq, up_got, y_got, out_theirs_got = tie(dq, up_got, y_got, out_theirs_got)
    s_up = scatter(ctx_sum(g_up, up_got))
    g_out = added(out_mine, out_theirs_got)
    out_got = to_ctx(g_out[:n_dp], g_out)
    total = hidden + (y_0.astype(F32) + swap_core(y_1).astype(F32) + y_got.astype(F32))
    total = send_home(total.astype(BF))
    d_theirs, gains_theirs = turn_back(ids, z, dq, dk, dv, cos, sin, gain_q, gain_k, tb, chunk, 1)
    give_theirs, keep_theirs = weight_sum([normed], [d_theirs])
    do, keep_theirs, down_got, s_gate = tie(do, keep_theirs, down_got, s_gate)
    s_down = scatter(ctx_sum(g_down, down_got))
    qkv_got = swap_seq(jnp.concatenate([give_theirs, keep_theirs], axis=0) if n_ctx == 2 else keep_theirs)
    dq, dk, dv = attend_back(ids, q, k, v, o, do, lse, chunk, 0)
    dq, qkv_got, out_got, total = tie(dq, qkv_got, out_got, total)
    s_out = scatter(ctx_sum(g_out[n_dp:] if n_ctx == 2 else g_out, out_got))
    total_core, total_seq = swap_core(total), swap_seq(total)
    d_mine, gains_mine = turn_back(ids, z, dq, dk, dv, cos, sin, gain_q, gain_k, tb, chunk, 0)

    d_mine, s_up, s_down = tie(d_mine, s_up, s_down)
    parity = jnp.reshape(1 - core, (1,)).astype(jnp.int32)
    give = unproject(parity, d_mine, d_theirs, w_all, tb, chunk)
    got = swap_core(give)
    d_mine, give = tie(d_mine, give)
    give, keep = weight_sum([normed], [d_mine])
    d_mine, keep, s_out, got = tie(d_mine, keep, s_out, got)
    where = jnp.stack([core, id_here // 2]).astype(jnp.int32)
    dz = close(where, d_mine, d_theirs, w_all, got, xs, gain_a, dhidden, tb, chunk)
    dz = dz.reshape(n_ctx, chunk, width)

    fold = (gains_mine + gains_theirs)[:2]
    fold = (fold[:, :HD] + fold[:, HD:]).reshape(2, n_dp, h_part)
    fold = jnp.pad(fold, ((0, 0), (0, 0), (0, d_part - h_part))).reshape(2, width)
    fold = jnp.concatenate([fold, jnp.zeros((LANES - 2, width), F32)], axis=0).astype(BF).T
    if n_ctx == 2:
        fold = fold.reshape(n_dp, 2, -1, LANES)
        fold_give, fold_keep = [lax.dynamic_index_in_dim(fold, at, 1, keepdims=False) for at in (1 - ctx, ctx)]
        give = jnp.concatenate([added(give, qkv_got[:n_dp]), fold_give], axis=-1)
        keep = jnp.concatenate([added(keep, qkv_got[n_dp:]), fold_keep], axis=-1)
    else:
        keep = jnp.concatenate([added(keep, qkv_got), fold], axis=-1)
    qkv_got = to_ctx(give, keep)
    if n_ctx == 2:
        dx = swap_ctx(lax.dynamic_index_in_dim(dz, 1 - ctx, 0, keepdims=False))
        dx, qkv_got, total_seq = tie(dx, qkv_got, total_seq)
        dx = added(lax.dynamic_index_in_dim(dz, ctx, 0, keepdims=False), dx)
    else:
        dx = lax.psum_scatter(dz, "ctx", scatter_dimension=0, tiled=False)
    s_qkv = scatter(ctx_sum(keep, qkv_got))
    dx_core, dx_seq = swap_core(dx), swap_seq(dx)
    dx_core, s_qkv = tie(dx_core, s_qkv)

    def join(piece, p_core, p_seq, kind):
        out = put(blocks[:2], piece, p_core, None, kind)
        out = put(blocks[2:], p_seq, swap_core(p_seq), out, kind)
        return out.reshape(2, local_len, width)

    layer_output = join(total, total_core, total_seq, BF)
    input_grad = join(dx, dx_core, dx_seq, F32)

    gate_grad = gather_rows(s_gate).astype(F32)
    up_grad = gather_rows(s_up).astype(F32)
    down_grad = gather_rows(s_down).T.astype(F32)
    out_grad = gather_rows(s_out).T.astype(F32)
    g = gather_rows(s_qkv).astype(F32)
    query_grad, key_grad, value_grad = g[:, :nq], g[:, nq:nq + nk], g[:, nq + nk:n_qkv]

    attn_sum = jnp.sum(query_weight.astype(F32) * query_grad, axis=1) + jnp.sum(key_weight.astype(F32) * key_grad, axis=1)
    attn_sum += jnp.sum(value_weight.astype(F32) * value_grad, axis=1)
    ffn_sum = jnp.sum(gate_weight.astype(F32) * gate_grad, axis=1) + jnp.sum(up_weight.astype(F32) * up_grad, axis=1)
    small = jnp.concatenate([attn_sum / attn_gain.astype(F32), ffn_sum / ffn_gain.astype(F32), g[:h_part, n_qkv], g[:h_part, n_qkv + 1]])
    small = small + swap_core(small)
    small = small + swap_seq(small)
    attn_gain_grad, ffn_gain_grad = small[:d_part], small[d_part:2 * d_part]
    qgain_grad, kgain_grad = small[2 * d_part:2 * d_part + h_part], small[2 * d_part + h_part:]

    return (layer_output, input_grad, attn_gain_grad, query_grad, key_grad, value_grad, qgain_grad, kgain_grad,
            out_grad, ffn_gain_grad, gate_grad, up_grad, down_grad)


def solution(mesh):
    token = P("dp", "ctx", None)
    into, out_of, vector = P("dp", "tensor"), P("tensor", "dp"), P("dp")
    return jax.shard_map(
        on_device,
        mesh=mesh,
        in_specs=(token, token, vector, into, into, into, vector, vector, out_of, vector, into, into, out_of),
        out_specs=(token, token, vector, into, into, into, vector, vector, out_of, vector, into, into, out_of),
        check_vma=False,
    )
```

time: 635 us -> 534 us (0.84)
  Pallas kernels: 132 us -> 234 us
  blocking collectives: 89.3 us -> 0 us
  waiting for transfers between devices: 164 us -> 113 us
  matrix products: 54.9 us -> 9.03 us
  other arithmetic: 71.6 us -> 48.4 us
  starting transfers between devices: 25.2 us -> 48.1 us
  local copies, waits for them, and re-layouts: 76.4 us -> 57.4 us
    pallas_call x2 -> x14, Pallas kernels: 44.1 us -> 137 us  [the longest x6 50.8 us: weight_grad(): pl.pallas_call(functools.partial(weight_grad_kernel, n_left=len(lefts), n...]
    ppermute x9 -> x14, waiting for transfers between devices: 92.2 us -> 24.1 us  [swap_seq(): return lax.ppermute(x, 'tensor', [(i, i ^ 2) for i in range(n_tensor)])]
    psum x1 -> x0, blocking collectives: 54.4 us -> none  [on_device(): lax.psum(jnp.concatenate([attn_gain_part, ffn_gain_part, fold.reshape(-1)...]
    dot_general x11 -> x2, matrix products: 54.9 us -> 9.03 us  [mm(): return lax.dot_general(a, b, dims, preferred_element_type=F32)]
    ppermute x9 -> x14, waiting for transfers between devices: 71.8 us -> 36.9 us  [swap_ctx(): return lax.ppermute(x, 'ctx', [(0, 1), (1, 0)])]
    all_gather x1 -> x0, blocking collectives: 22.7 us -> none  [on_device(): lax.all_gather(out_weight, 'dp', axis=0, tiled=False).transpose(1, 0, 2)]
    reduce_scatter x4 -> x5, waiting for transfers between devices: 0.03 us -> 18.6 us  [scatter(): return lax.psum_scatter(half, 'dp', scatter_dimension=0, tiled=False)]
    ppermute x0 -> x3, waiting for transfers between devices: none -> 15.6 us  [on_device(): lax.ppermute(piece, 'dp', [(i, (i + 1) % n_dp) for i in range(n_dp)])]
  transfers between devices with their start and end apart: 43 -> 57, of which waited for: 9 -> 20; matrix products, arithmetic and copies ran while one was open for 28% -> 18% of each run, Pallas kernels for 17% -> 37%
where the time goes in v2:
time: 534 us; the launch traced here: 525 us
  Pallas kernels  234 us (44%)
  waiting for transfers between devices  113 us (21%)
  local copies, waits for them, and re-layouts  57.4 us (11%)
  other arithmetic  48.4 us (9%)
  starting transfers between devices  48.1 us (9%)
  between operations  15.5 us (3%)
  matrix products  9.03 us (2%)
    pallas_call x6, Pallas kernels, weight_grad(): pl.pallas_call(functools.partial(weight_grad_kernel, n_left=len(lefts), n...  50.8 us
    pallas_call x2, Pallas kernels, feed(): pl.pallas_call(functools.partial(feed_kernel, n_pieces=n_pieces), grid_sp...  50.5 us
    pallas_call x2, Pallas kernels, attend_back(): pl.pallas_call(attend_back_kernel, grid_spec=pltpu.PrefetchScalarGridSpec...  40.6 us
    ppermute x14, waiting for transfers between devices, swap_ctx(): return lax.ppermute(x, 'ctx', [(0, 1), (1, 0)])  36.9 us
    ppermute x14, waiting for transfers between devices, swap_seq(): return lax.ppermute(x, 'tensor', [(i, i ^ 2) for i in range(n_tensor)])  24.1 us
    pallas_call x2, Pallas kernels, turn_back(): pl.pallas_call(functools.partial(turn_back_kernel, per_chunk=chunk // tb)...  22.2 us
    ppermute x14, starting transfers between devices, swap_seq(): return lax.ppermute(x, 'tensor', [(i, i ^ 2) for i in range(n_tensor)])  20.2 us
    pallas_call x4, Pallas kernels, put(): pl.pallas_call(put_kernel, grid_spec=pltpu.PrefetchScalarGridSpec(num_sca...  20.2 us
  transfers between devices with their start and end apart: 57, of which 20 were waited for; matrix products, arithmetic and copies ran while one was open for 18% of the time, Pallas kernels for 37%

profile of v2, /device:TPU:0, one launch (start us, length us, event | category | flops | bytes accessed | tf_op | source)
XLA Modules:
  0.0 524.6 jit_solution(4288974484573452877)
XLA Ops:
  13.0 3.0 collective-permute-start.5
  18.4 2.4 dynamic-slice_bitcast_fusion.2
  28.5 3.7 fusion.11
  32.3 3.0 pad_maximum_fusion.1
  40.1 2.5 broadcast_in_dim.26
  46.9 10.8 %collective-permute-done.3 = bf16[256,640]{1,0:T(8,128)(2,1)} collective-permute-done((bf16[256,640]{1,0:T(8,128)(2,1)}, bf16[256,640]{1,0:T(8,128)(2,1)}, u32[]{:S(2)}, u32[]{:S(2)}) %collective-permute-start.3) | collective-permute-done | bytes 327712 | tf_op jit(solution)/shard_map/ppermute | solution.py:688
  60.9 2.8 collective-permute-start.4
  65.3 2.4 slice.166.refs_7_
  69.3 4.8 collective-permute-done.4
  84.2 3.0 constant_dynamic-update-slice_fusion.11.x_ref
  87.2 14.8 %project.1 = (bf16[2048,1024]{1,0:T(8,128)(2,1)}, f32[2048,1024]{1,0:T(8,128)}, bf16[2048,512]{1,0:T(8,128)(2,1)}, bf16[2048,512]{1,0:T(8,128)(2,1)}, bf16[2048,512]{1,0:T(8,128)(2,1)}) custom-call(bf16[2048,1024]{1,0:T(8,128)(2,1)} %constant_dynamic-update-slice_fusion.11.x_ref, f32[1,1024]{1,0:T(1,128)} %bitcast.134, bf16[1024,1024]{1,0:T(8,128)(2,1)} %copy-done.11, ...), custom_call_target="tpu_custom_call" | custom-call | flops 4294967 | bytes 28672 | tf_op jit(solution)/shard_map/project/pallas_call | solution.py:103
  108.8 19.1 %attend.1 = (bf16[1024,512]{1,0:T(8,128)(2,1)}, f32[32,1024]{1,0:T(8,128)}) custom-call(s32[2]{0:T(128)} %pad_add_fusion.2.ids, bf16[2048,512]{1,0:T(8,128)(2,1)} %get-tuple-element.105.q_ref, bf16[2048,512]{1,0:T(8,128)(2,1)} %get-tuple-element.106.k_ref, bf16[2048,512]{1,0:T(8,128)(2,1)} %get-tuple-element.107.v_ref), custom_call_target="tpu_custom_call" | custom-call | flops 5368709 | bytes 6291 | tf_op jit(solution)/shard_map/attend/pallas_call | solution.py:172
  128.1 5.2 fusion.9
  133.3 2.7 slice.210
  136.0 3.8 collective-permute-done.15.refs_2_.refs_8_.refs_9_.refs_10_.refs_11_
  147.5 3.1 slice_bitcast_fusion
  150.6 8.9 %all-gather.11.cloned.1.call-done = bf16[1024,1152]{1,0:T(8,128)(2,1)} async-done(((bf16[256,1152]{1,0:T(8,128)(2,1)}), bf16[1024,1152]{1,0:T(8,128)(2,1)}) %all-gather.11.cloned.1.call-update) | async-done | bytes 2359312 | tf_op jit(solution)/shard_map/all_gather | solution.py:700
  160.4 25.1 %feed.2 = (bf16[1024,1152]{1,0:T(8,128)(2,1)}, bf16[1024,1152]{1,0:T(8,128)(2,1)}, bf16[1024,1152]{1,0:T(8,128)(2,1)}, bf16[512,1024]{1,0:T(8,128)(2,1)}, bf16[5...) custom-call(s32[1]{0:T(128)} %bitcast.18.place, bf16[512,1024]{1,0:T(8,128)(2,1)} %copy-done.2, ...), custom_call_target="tpu_custom_call" | custom-call | flops 14495514 | bytes 22437 | tf_op jit(solution)/shard_map/feed/pallas_call | solution.py:420
  185.6 2.6 collective-permute-done.19.refs_1_.refs_12_.refs_13_.refs_14_.refs_15_
  189.2 25.4 %feed.3 = (bf16[1024,1152]{1,0:T(8,128)(2,1)}, bf16[1024,1152]{1,0:T(8,128)(2,1)}, bf16[1024,1152]{1,0:T(8,128)(2,1)}, bf16[512,1024]{1,0:T(8,128)(2,1)}, bf16[5...) custom-call(s32[1]{0:T(128)} %bitcast.18.place, bf16[512,1024]{1,0:T(8,128)(2,1)} %copy-done.4, ...), custom_call_target="tpu_custom_call" | custom-call | flops 14495514 | bytes 22437 | tf_op jit(solution)/shard_map/feed/pallas_call | solution.py:420
  215.3 2.5 collective-permute-done.21
  217.7 2.6 add_convert_fusion.4
  220.3 11.0 %weight_grad.6 = (bf16[4,128,1152]{2,1,0:T(8,128)(2,1)}, bf16[4,128,1152]{2,1,0:T(8,128)(2,1)}) custom-call(s32[1]{0:T(128)} %bitcast.18.place, bf16[512,1024]{1,0:T(8,128)(2,1)} %copy-done.2, bf16[512,1024]{1,0:T(8,128)(2,1)} %copy-done.2, bf16[512,1024]{1,0:T(8,128)(2,1)} %copy-done.2, bf16[512,1024]{1,0:T(8,128)(2,1)} %copy-done.2, ...), custom_call_target="tpu_custom_call" | custom-call | flops 4831838 | bytes 8912 | tf_op jit(solution)/shard_map/weight_grad/pallas_call | solution.py:472
  234.4 11.1 %weight_grad.7 = (bf16[4,128,1152]{2,1,0:T(8,128)(2,1)}, bf16[4,128,1152]{2,1,0:T(8,128)(2,1)}) custom-call(s32[1]{0:T(128)} %bitcast.18.place, bf16[512,1024]{1,0:T(8,128)(2,1)} %copy-done.2, bf16[512,1024]{1,0:T(8,128)(2,1)} %copy-done.2, bf16[512,1024]{1,0:T(8,128)(2,1)} %copy-done.2, bf16[512,1024]{1,0:T(8,128)(2,1)} %copy-done.2, ...), custom_call_target="tpu_custom_call" | custom-call | flops 4831838 | bytes 8912 | tf_op jit(solution)/shard_map/weight_grad/pallas_call | solution.py:472
  245.5 11.3 %weight_grad.8 = (bf16[4,128,1152]{2,1,0:T(8,128)(2,1)}, bf16[4,128,1152]{2,1,0:T(8,128)(2,1)}) custom-call(s32[1]{0:T(128)} %bitcast.18.place, bf16[512,1024]{1,0:T(8,128)(2,1)} %copy-done.8, bf16[512,1024]{1,0:T(8,128)(2,1)} %copy-done.8, bf16[512,1024]{1,0:T(8,128)(2,1)} %copy-done.8, bf16[512,1024]{1,0:T(8,128)(2,1)} %copy-done.8, ...), custom_call_target="tpu_custom_call" | custom-call | flops 4831838 | bytes 8912 | tf_op jit(solution)/shard_map/weight_grad/pallas_call | solution.py:472
  256.9 2.8 add_convert_fusion.5
  266.0 3.8 fusion.6.do_ref
  269.8 4.6 weight_grad.9
  282.8 20.4 %attend_back.2 = (f32[2048,256]{1,0:T(8,128)}, f32[2048,256]{1,0:T(8,128)}, f32[2048,256]{1,0:T(8,128)}) custom-call(s32[2]{0:T(128)} %pad_add_fusion.2.ids, bf16[2048,512]{1,0:T(8,128)(2,1)} %get-tuple-element.105.q_ref, bf16[2048,512]{1,0:T(8,128)(2,1)} %get-tuple-element.106.k_ref, bf16[2048,512]{1,0:T(8,128)(2,1)} %get-tuple-element.107.v_ref, ...), custom_call_target="tpu_custom_call" | custom-call | flops 6710886 | bytes 9437 | tf_op jit(solution)/shard_map/attend_back/pallas_call | solution.py:248
  304.3 9.3 %collective-permute-done.27 = bf16[8,128,256]{2,1,0:T(8,128)(2,1)} collective-permute-done((bf16[8,128,256]{2,1,0:T(8,128)(2,1)S(1)}, bf16[8,128,256]{2,1,0:T(8,128)(2,1)}, u32[]{:S(2)}, u32[]{:S(2)}) %collective-permute-start.27) | collective-permute-done | bytes 524320 | tf_op jit(solution)/shard_map/ppermute | solution.py:637
  316.0 11.2 %turn_back.2 = (bf16[2048,512]{1,0:T(8,128)(2,1)}, f32[8,128]{1,0:T(8,128)}) custom-call(s32[2]{0:T(128)} %pad_add_fusion.2.ids, f32[2048,1024]{1,0:T(8,128)} %get-tuple-element.103.z_ref, f32[2048,256]{1,0:T(8,128)} %get-tuple-element.148.dq_ref, f32[2048,256]{1,0:T(8,128)} %get-tuple-element.149.dk_ref, f32[2048,256]{1,0:T(8,128)} %get-tuple-element.150.dv_ref, ...), custom_call_target="tpu_custom_call" | custom-call | flops 409600 | bytes 24576 | tf_op jit(solution)/shard_map/turn_back/pallas_call | solution.py:317
  327.3 6.3 %weight_grad.10 = (bf16[4,128,512]{2,1,0:T(8,128)(2,1)}, bf16[4,128,512]{2,1,0:T(8,128)(2,1)}) custom-call(s32[1]{0:T(128)} %bitcast.18.place, bf16[2048,1024]{1,0:T(8,128)(2,1)} %get-tuple-element.141.refs_0_.refs_1_.refs_2_.refs_3_, bf16[2048,1024]{1,0:T(8,128)(2,1)} %get-tuple-element.141.refs_0_.refs_1_.refs_2_.refs_3_, ...), custom_call_target="tpu_custom_call" | custom-call | flops 2147483 | bytes 6291 | tf_op jit(solution)/shard_map/weight_grad/pallas_call | solution.py:472
  333.5 8.7 %collective-permute-done.28 = bf16[4,128,1152]{2,1,0:T(8,128)(2,1)} collective-permute-done((bf16[4,128,1152]{2,1,0:T(8,128)(2,1)}, bf16[4,128,1152]{2,1,0:T(8,128)(2,1)}, u32[]{:S(2)}, u32[]{:S(2)}) %collective-permute-start.28) | collective-permute-done | bytes 1179680 | tf_op jit(solution)/shard_map/ppermute | solution.py:640
  342.2 2.6 add_convert_fusion
  344.9 2.7 add_convert_fusion.3
  352.0 20.2 %attend_back.3 = (f32[2048,256]{1,0:T(8,128)}, f32[2048,256]{1,0:T(8,128)}, f32[2048,256]{1,0:T(8,128)}) custom-call(s32[2]{0:T(128)} %pad_add_fusion.2.ids, bf16[2048,512]{1,0:T(8,128)(2,1)} %get-tuple-element.105.q_ref, bf16[2048,512]{1,0:T(8,128)(2,1)} %get-tuple-element.106.k_ref, bf16[2048,512]{1,0:T(8,128)(2,1)} %get-tuple-element.107.v_ref, ...), custom_call_target="tpu_custom_call" | custom-call | flops 6710886 | bytes 9437 | tf_op jit(solution)/shard_map/attend_back/pallas_call | solution.py:248
  374.2 11.0 %turn_back.3 = (bf16[2048,512]{1,0:T(8,128)(2,1)}, f32[8,128]{1,0:T(8,128)}) custom-call(s32[2]{0:T(128)} %pad_add_fusion.2.ids, f32[2048,1024]{1,0:T(8,128)} %get-tuple-element.103.z_ref, f32[2048,256]{1,0:T(8,128)} %get-tuple-element.164.dq_ref, f32[2048,256]{1,0:T(8,128)} %get-tuple-element.165.dk_ref, f32[2048,256]{1,0:T(8,128)} %get-tuple-element.166.dv_ref, ...), custom_call_target="tpu_custom_call" | custom-call | flops 409600 | bytes 24576 | tf_op jit(solution)/shard_map/turn_back/pallas_call | solution.py:317
  385.2 6.2 %unproject.1 = bf16[1024,1024]{1,0:T(8,128)(2,1)} custom-call(s32[1]{0:T(128)} %bitcast.27.parity, bf16[2048,512]{1,0:T(8,128)(2,1)} %get-tuple-element.176.a_ref.refs_4_, bf16[2048,512]{1,0:T(8,128)(2,1)} %get-tuple-element.151.refs_4_.b_ref, bf16[1024,1024]{1,0:T(8,128)(2,1)} %copy-done.11), custom_call_target="tpu_custom_call" | custom-call | flops 2147483 | bytes 8388 | tf_op jit(solution)/shard_map/unproject/pallas_call | solution.py:535
  397.8 6.4 %weight_grad.11 = (bf16[4,128,512]{2,1,0:T(8,128)(2,1)}, bf16[4,128,512]{2,1,0:T(8,128)(2,1)}) custom-call(s32[1]{0:T(128)} %bitcast.18.place, bf16[2048,1024]{1,0:T(8,128)(2,1)} %get-tuple-element.141.refs_0_.refs_1_.refs_2_.refs_3_, bf16[2048,1024]{1,0:T(8,128)(2,1)} %get-tuple-element.141.refs_0_.refs_1_.refs_2_.refs_3_, ...), custom_call_target="tpu_custom_call" | custom-call | flops 2147483 | bytes 6291 | tf_op jit(solution)/shard_map/weight_grad/pallas_call | solution.py:472
  404.2 6.4 %reduce-scatter.12.cloned.1.call-done = bf16[1,128,256]{2,1,0:T(8,128)(2,1)} async-done(((bf16[4,128,256]{2,1,0:T(8,128)(2,1)}), bf16[1,128,256]{2,1,0:T(8,128)(2,1)}) %reduce-scatter.12.cloned.1.call-update) | async-done | bytes 65552 | tf_op jit(solution)/shard_map/reduce_scatter | solution.py:763
  411.9 9.3 %close.1 = bf16[1024,1024]{1,0:T(8,128)(2,1)} custom-call(s32[2]{0:T(128)} %pad_add_fusion.1.where, bf16[2048,512]{1,0:T(8,128)(2,1)} %get-tuple-element.176.a_ref.refs_4_, bf16[2048,512]{1,0:T(8,128)(2,1)} %get-tuple-element.151.refs_4_.b_ref, bf16[1024,1024]{1,0:T(8,128)(2,1)} %copy-done.11, bf16[1024,1024]{1,0:T(8,128)(2,1)} %copy-done.20, ...), custom_call_target="tpu_custom_call" | custom-call | flops 2147483 | bytes 10485 | tf_op jit(solution)/shard_map/close/pallas_call | solution.py:571
  427.6 4.9 put.4.refs_0_
  435.9 26.9 %collective-permute-done.35 = bf16[4,128,640]{2,1,0:T(8,128)(2,1)S(1)} collective-permute-done((bf16[4,128,640]{2,1,0:T(8,128)(2,1)S(1)}, bf16[4,128,640]{2,1,0:T(8,128)(2,1)S(1)}, u32[]{:S(2)}, u32[]{:S(2)}) %collective-permute-start.35) | collective-permute-done | bytes 655392 | tf_op jit(solution)/shard_map/ppermute | solution.py:640
  473.3 12.2 %reduce-scatter.14.cloned.1.call-done = bf16[1,128,640]{2,1,0:T(8,128)(2,1)} async-done(((bf16[4,128,640]{2,1,0:T(8,128)(2,1)}), bf16[1,128,640]{2,1,0:T(8,128)(2,1)}) %reduce-scatter.14.cloned.1.call-update) | async-done | bytes 163856 | tf_op jit(solution)/shard_map/reduce_scatter | solution.py:763
  487.5 4.8 collective-permute-done.39.a_ref
  499.9 4.8 put.5
  504.7 5.2 put.6.refs_0_
  512.0 5.3 %put.7 = f32[2048,1024]{1,0:T(8,128)} custom-call(s32[2]{0:T(128)} %pad_add_fusion.where, bf16[512,1024]{1,0:T(8,128)(2,1)} %collective-permute-done.39.a_ref, bf16[512,1024]{1,0:T(8,128)(2,1)} %copy-done.36, f32[2048,1024]{1,0:T(8,128)} %put.6.refs_0_), custom_call_target="tpu_custom_call", output_to_operand_aliasing={{}: (3, {})} | custom-call | bytes 6291 | tf_op jit(solution)/shard_map/put/pallas_call | solution.py:505
  (306 shorter events, 125.5 us)
Async XLA Ops:
  7.3 58.0 %all-gather.7.cloned.1.call-start = ((), (), s32[]{:S(2)}) async-start(), calls=%async_computation.10 | async-start | bytes 2129920 | tf_op jit(solution)/shard_map/all_gather | solution.py:700
  10.1 92.0 %all-gather.9.cloned.1.call-start = ((), (), s32[]{:S(2)}) async-start(), calls=%async_computation.11 | async-start | bytes 1474560 | tf_op jit(solution)/shard_map/all_gather | solution.py:700
  13.0 22.3 %collective-permute-start.5 = (bf16[256,512]{1,0:T(8,128)(2,1)}, bf16[256,512]{1,0:T(8,128)(2,1)}, u32[]{:S(2)}, u32[]{:S(2)}) collective-permute-start(bf16[256,512]{1,0:T(8,128)(2,1)} %constant_dynamic-update-slice_fusion), channel_id=1, source_target_pairs={{0,2},{1,3},{2,0},{3,1},{4,6},{5,7},{6,4},{7,5},{8,10},{9,11},{10,... | collective-permute-start | bytes 786440 | tf_op jit(solution)/shard_map/ppermute | solution.py:637
  16.8 19.5 %collective-permute-start.2 = (bf16[256,640]{1,0:T(8,128)(2,1)}, bf16[256,640]{1,0:T(8,128)(2,1)}, u32[]{:S(2)}, u32[]{:S(2)}) collective-permute-start(bf16[256,640]{1,0:T(8,128)(2,1)} %fusion.12), channel_id=1, source_target_pairs={{0,8},{8,16},{16,24},{24,0},{1,9},{9,17},{17,25},{25,1},{2,10},{10... | collective-permute-start | bytes 983048 | tf_op jit(solution)/shard_map/ppermute | solution.py:688
  20.8 44.4 %collective-permute-start = (bf16[512,1024]{1,0:T(8,128)(2,1)}, bf16[512,1024]{1,0:T(8,128)(2,1)}, u32[]{:S(2)}, u32[]{:S(2)}) collective-permute-start(bf16[512,1024]{1,0:T(8,128)(2,1)} %dynamic-slice_bitcast_fusion.2), channel_id=1, source_target_pairs={{0,4},{4,0},{1,5},{5,1},{2,6},{6,2},{3,7},{7,3},{8,12},{12,8},{9,1... | collective-permute-start | bytes 3145736 | tf_op jit(solution)/shard_map/ppermute | solution.py:640
  24.5 83.0 %collective-permute-start.11 = (bf16[512,1024]{1,0:T(8,128)(2,1)}, bf16[512,1024]{1,0:T(8,128)(2,1)S(1)}, u32[]{:S(2)}, u32[]{:S(2)}) collective-permute-start(bf16[512,1024]{1,0:T(8,128)(2,1)} %dynamic-slice_bitcast_fusion.1), channel_id=1, source_target_pairs={{0,0},{5,1},{2,2},{7,3},{4,4},{1,5},{6,6},{3,7},{8,8},{13,9},{10,1... | collective-permute-start | bytes 3145736 | tf_op jit(solution)/shard_map/ppermute | solution.py:652
  27.2 132.3 %all-gather.11.cloned.1.call-start = ((), (), s32[]{:S(2)}) async-start(), calls=%async_computation.12 | async-start | bytes 2949120 | tf_op jit(solution)/shard_map/all_gather | solution.py:700
  38.0 7.9 %collective-permute-start.6 = (bf16[256,512]{1,0:T(8,128)(2,1)}, bf16[256,512]{1,0:T(8,128)(2,1)}, u32[]{:S(2)}, u32[]{:S(2)}) collective-permute-start(bf16[256,512]{1,0:T(8,128)(2,1)} %get-tuple-element.223), channel_id=1, source_target_pairs={{0,2},{1,3},{2,0},{3,1},{4,6},{5,7},{6,4},{7,5},{8,10},{9,11},{10,... | collective-permute-start | bytes 786440 | tf_op jit(solution)/shard_map/ppermute | solution.py:637
  38.6 19.1 %collective-permute-start.3 = (bf16[256,640]{1,0:T(8,128)(2,1)}, bf16[256,640]{1,0:T(8,128)(2,1)}, u32[]{:S(2)}, u32[]{:S(2)}) collective-permute-start(bf16[256,640]{1,0:T(8,128)(2,1)} %collective-permute-done.2), channel_id=1, source_target_pairs={{0,8},{8,16},{16,24},{24,0},{1,9},{9,17},{17,25},{25,1},{2,10},{10... | collective-permute-start | bytes 983048 | tf_op jit(solution)/shard_map/ppermute | solution.py:688
  60.9 13.1 %collective-permute-start.4 = (bf16[256,640]{1,0:T(8,128)(2,1)}, bf16[256,640]{1,0:T(8,128)(2,1)}, u32[]{:S(2)}, u32[]{:S(2)}) collective-permute-start(bf16[256,640]{1,0:T(8,128)(2,1)} %collective-permute-done.3), channel_id=1, source_target_pairs={{0,8},{8,16},{16,24},{24,0},{1,9},{9,17},{17,25},{25,1},{2,10},{10... | collective-permute-start | bytes 983048 | tf_op jit(solution)/shard_map/ppermute | solution.py:688
  65.1 19.1 %collective-permute-start.1 = (bf16[512,1024]{1,0:T(8,128)(2,1)}, bf16[512,1024]{1,0:T(8,128)(2,1)}, u32[]{:S(2)}, u32[]{:S(2)}) collective-permute-start(bf16[512,1024]{1,0:T(8,128)(2,1)} %collective-permute-done), channel_id=1, source_target_pairs={{0,1},{1,0},{2,3},{3,2},{4,5},{5,4},{6,7},{7,6},{8,9},{9,8},{10,11... | collective-permute-start | bytes 3145736 | tf_op jit(solution)/shard_map/ppermute | solution.py:634
  67.6 34.5 %collective-permute-start.9 = (bf16[4,576,256]{2,1,0:T(8,128)(2,1)}, bf16[4,576,256]{2,1,0:T(8,128)(2,1)}, u32[]{:S(2)}, u32[]{:S(2)}) collective-permute-start(bf16[4,576,256]{2,1,0:T(8,128)(2,1)} %slice.166.refs_7_), channel_id=1, source_target_pairs={{0,4},{4,0},{1,5},{5,1},{2,6},{6,2},{3,7},{7,3},{8,12},{12,8},{9,1... | collective-permute-start | bytes 3538952 | tf_op jit(solution)/shard_map/ppermute | solution.py:640
  102.1 26.0 %collective-permute-start.10 = (bf16[4,128,1152]{2,1,0:T(8,128)(2,1)}, bf16[4,128,1152]{2,1,0:T(8,128)(2,1)S(1)}, u32[]{:S(2)}, u32[]{:S(2)}) collective-permute-start(bf16[4,128,1152]{2,1,0:T(8,128)(2,1)} %bitcast.115), channel_id=1, source_target_pairs={{0,4},{4,0},{1,5},{5,1},{2,6},{6,2},{3,7},{7,3},{8,12},{12,8},{9,1... | collective-permute-start | bytes 3538952 | tf_op jit(solution)/shard_map/ppermute | solution.py:640
  105.8 22.3 %collective-permute-start.12 = (bf16[256,1024]{0,1:T(8,128)(2,1)}, bf16[256,1024]{0,1:T(8,128)(2,1)}, u32[]{:S(2)}, u32[]{:S(2)}) collective-permute-start(bf16[256,1024]{0,1:T(8,128)(2,1)} %bitcast.17), channel_id=1, source_target_pairs={{0,2},{1,3},{2,0},{3,1},{4,6},{5,7},{6,4},{7,5},{8,10},{9,11},{10,... | collective-permute-start | bytes 1572872 | tf_op jit(solution)/shard_map/ppermute | solution.py:637
  107.5 32.3 %collective-permute-start.15 = (bf16[512,1024]{1,0:T(8,128)(2,1)S(1)}, bf16[512,1024]{1,0:T(8,128)(2,1)S(1)}, u32[]{:S(2)}, u32[]{:S(2)}) collective-permute-start(bf16[512,1024]{1,0:T(8,128)(2,1)S(1)} %collective-permute-done.11.refs_2_.refs_0_.refs_1_.refs_3_), channel_id=1, source_target_pairs={{0,2},{1,3},{2,0},{3,1},{4,6},{5,7},{6,4},{7,5},{8,10},{9,11},{10,... | collective-permute-start | bytes 3145736 | tf_op jit(solution)/shard_map/ppermute | solution.py:637
  107.8 234.4 %reduce-scatter.6.cloned.1.call-start = ((), (), s32[]{:S(2)}) async-start(), calls=%async_computation.5 | async-start | bytes 1474560 | tf_op jit(solution)/shard_map/reduce_scatter | solution.py:763
  145.3 14.2 %collective-permute-start.14 = (bf16[512,1024]{1,0:T(8,128)(2,1)S(1)}, bf16[512,1024]{1,0:T(8,128)(2,1)S(1)}, u32[]{:S(2)}, u32[]{:S(2)}) collective-permute-start(bf16[512,1024]{1,0:T(8,128)(2,1)S(1)} %multiply_convert_fusion.refs_0_.refs_1_.refs_2_.refs_3_), channel_id=1, source_target_pairs={{0,1},{1,0},{2,3},{3,2},{4,5},{5,4},{6,7},{7,6},{8,9},{9,8},{10,11... | collective-permute-start | bytes 3145736 | tf_op jit(solution)/shard_map/ppermute | solution.py:634
  145.8 39.7 %collective-permute-start.18 = (bf16[512,1024]{1,0:T(8,128)(2,1)S(1)}, bf16[512,1024]{1,0:T(8,128)(2,1)S(1)}, u32[]{:S(2)}, u32[]{:S(2)}) collective-permute-start(bf16[512,1024]{1,0:T(8,128)(2,1)S(1)} %multiply_convert_fusion.refs_0_.refs_1_.refs_2_.refs_3_), channel_id=1, source_target_pairs={{0,2},{1,3},{2,0},{3,1},{4,6},{5,7},{6,4},{7,5},{8,10},{9,11},{10,... | collective-permute-start | bytes 3145736 | tf_op jit(solution)/shard_map/ppermute | solution.py:637
  214.9 42.0 %collective-permute-start.20 = (bf16[512,1024]{1,0:T(8,128)(2,1)}, bf16[512,1024]{1,0:T(8,128)(2,1)}, u32[]{:S(2)}, u32[]{:S(2)}) collective-permute-start(bf16[512,1024]{1,0:T(8,128)(2,1)} %get-tuple-element.118), channel_id=1, source_target_pairs={{0,1},{1,0},{2,3},{3,2},{4,5},{5,4},{6,7},{7,6},{8,9},{9,8},{10,11... | collective-permute-start | bytes 3145736 | tf_op jit(solution)/shard_map/ppermute | solution.py:634
  231.4 28.3 %collective-permute-start.23 = (bf16[4,128,1152]{2,1,0:T(8,128)(2,1)}, bf16[4,128,1152]{2,1,0:T(8,128)(2,1)S(1)}, u32[]{:S(2)}, u32[]{:S(2)}) collective-permute-start(bf16[4,128,1152]{2,1,0:T(8,128)(2,1)} %get-tuple-element.135), channel_id=1, source_target_pairs={{0,4},{4,0},{1,5},{5,1},{2,6},{6,2},{3,7},{7,3},{8,12},{12,8},{9,1... | collective-permute-start | bytes 3538952 | tf_op jit(solution)/shard_map/ppermute | solution.py:640
  232.9 26.8 %collective-permute-start.22 = (bf16[512,1024]{1,0:T(8,128)(2,1)}, bf16[512,1024]{1,0:T(8,128)(2,1)S(1)}, u32[]{:S(2)}, u32[]{:S(2)}) collective-permute-start(bf16[512,1024]{1,0:T(8,128)(2,1)} %add_convert_fusion.4), channel_id=1, source_target_pairs={{0,2},{1,3},{2,0},{3,1},{4,6},{5,7},{6,4},{7,5},{8,10},{9,11},{10,... | collective-permute-start | bytes 3145736 | tf_op jit(solution)/shard_map/ppermute | solution.py:637
  234.4 25.3 %collective-permute-start.17 = (bf16[512,1024]{1,0:T(8,128)(2,1)}, bf16[512,1024]{1,0:T(8,128)(2,1)S(1)}, u32[]{:S(2)}, u32[]{:S(2)}) collective-permute-start(bf16[512,1024]{1,0:T(8,128)(2,1)} %get-tuple-element.114), channel_id=1, source_target_pairs={{0,1},{1,0},{2,3},{3,2},{4,5},{5,4},{6,7},{7,6},{8,9},{9,8},{10,11... | collective-permute-start | bytes 3145736 | tf_op jit(solution)/shard_map/ppermute | solution.py:634
  275.7 109.4 %reduce-scatter.8.cloned.1.call-start = ((), (), s32[]{:S(2)}) async-start(), calls=%async_computation.6 | async-start | bytes 1474560 | tf_op jit(solution)/shard_map/reduce_scatter | solution.py:763
  275.8 28.5 %collective-permute-start.25 = (bf16[4,128,1152]{2,1,0:T(8,128)(2,1)}, bf16[4,128,1152]{2,1,0:T(8,128)(2,1)S(1)}, u32[]{:S(2)}, u32[]{:S(2)}) collective-permute-start(bf16[4,128,1152]{2,1,0:T(8,128)(2,1)} %get-tuple-element.144), channel_id=1, source_target_pairs={{0,4},{4,0},{1,5},{5,1},{2,6},{6,2},{3,7},{7,3},{8,12},{12,8},{9,1... | collective-permute-start | bytes 3538952 | tf_op jit(solution)/shard_map/ppermute | solution.py:640
  277.1 27.2 %collective-permute-start.26 = (bf16[512,1024]{1,0:T(8,128)(2,1)}, bf16[512,1024]{1,0:T(8,128)(2,1)S(1)}, u32[]{:S(2)}, u32[]{:S(2)}) collective-permute-start(bf16[512,1024]{1,0:T(8,128)(2,1)} %add_convert_fusion.5), channel_id=1, source_target_pairs={{0,2},{1,3},{2,0},{3,1},{4,6},{5,7},{6,4},{7,5},{8,10},{9,11},{10,... | collective-permute-start | bytes 3145736 | tf_op jit(solution)/shard_map/ppermute | solution.py:637
  282.2 31.4 %collective-permute-start.27 = (bf16[8,128,256]{2,1,0:T(8,128)(2,1)S(1)}, bf16[8,128,256]{2,1,0:T(8,128)(2,1)}, u32[]{:S(2)}, u32[]{:S(2)}) collective-permute-start(bf16[8,128,256]{2,1,0:T(8,128)(2,1)S(1)} %pad_maximum_fusion.8), channel_id=1, source_target_pairs={{0,2},{1,3},{2,0},{3,1},{4,6},{5,7},{6,4},{7,5},{8,10},{9,11},{10,... | collective-permute-start | bytes 1572872 | tf_op jit(solution)/shard_map/ppermute | solution.py:637
  314.9 70.3 %reduce-scatter.10.cloned.1.call-start = ((), (), s32[]{:S(2)}) async-start(), calls=%async_computation.7 | async-start | bytes 1474560 | tf_op jit(solution)/shard_map/reduce_scatter | solution.py:763
  315.0 27.2 %collective-permute-start.28 = (bf16[4,128,1152]{2,1,0:T(8,128)(2,1)}, bf16[4,128,1152]{2,1,0:T(8,128)(2,1)}, u32[]{:S(2)}, u32[]{:S(2)}) collective-permute-start(bf16[4,128,1152]{2,1,0:T(8,128)(2,1)} %get-tuple-element.153), channel_id=1, source_target_pairs={{0,4},{4,0},{1,5},{5,1},{2,6},{6,2},{3,7},{7,3},{8,12},{12,8},{9,1... | collective-permute-start | bytes 3538952 | tf_op jit(solution)/shard_map/ppermute | solution.py:640
  316.0 28.8 %collective-permute-start.31 = (bf16[512,1024]{1,0:T(8,128)(2,1)}, bf16[512,1024]{1,0:T(8,128)(2,1)}, u32[]{:S(2)}, u32[]{:S(2)}) collective-permute-start(bf16[512,1024]{1,0:T(8,128)(2,1)} %get-tuple-element.162), channel_id=1, source_target_pairs={{0,1},{1,0},{2,3},{3,2},{4,5},{5,4},{6,7},{7,6},{8,9},{9,8},{10,11... | collective-permute-start | bytes 3145736 | tf_op jit(solution)/shard_map/ppermute | solution.py:634
  344.8 65.8 %reduce-scatter.12.cloned.1.call-start = ((), (), s32[]{:S(2)}) async-start(), calls=%async_computation.8 | async-start | bytes 327680 | tf_op jit(solution)/shard_map/reduce_scatter | solution.py:763
  347.6 24.7 %collective-permute-start.32 = (bf16[512,1024]{1,0:T(8,128)(2,1)S(1)}, bf16[512,1024]{1,0:T(8,128)(2,1)S(1)}, u32[]{:S(2)}, u32[]{:S(2)}) collective-permute-start(bf16[512,1024]{1,0:T(8,128)(2,1)S(1)} %add_convert_fusion.3), channel_id=1, source_target_pairs={{0,0},{1,5},{2,2},{3,7},{4,4},{5,1},{6,6},{7,3},{8,8},{9,13},{10,1... | collective-permute-start | bytes 3145736 | tf_op jit(solution)/shard_map/ppermute | solution.py:649
  348.6 25.6 %collective-permute-start.29 = (bf16[8,128,512]{2,1,0:T(8,128)(2,1)S(1)}, bf16[8,128,512]{2,1,0:T(8,128)(2,1)S(1)}, u32[]{:S(2)}, u32[]{:S(2)}) collective-permute-start(bf16[8,128,512]{2,1,0:T(8,128)(2,1)S(1)} %pad_maximum_fusion.4), channel_id=1, source_target_pairs={{0,2},{1,3},{2,0},{3,1},{4,6},{5,7},{6,4},{7,5},{8,10},{9,11},{10,... | collective-permute-start | bytes 3145736 | tf_op jit(solution)/shard_map/ppermute | solution.py:637
  351.3 21.0 %collective-permute-start.30 = (bf16[4,128,256]{2,1,0:T(8,128)(2,1)S(1)}, bf16[4,128,256]{2,1,0:T(8,128)(2,1)S(1)}, u32[]{:S(2)}, u32[]{:S(2)}) collective-permute-start(bf16[4,128,256]{2,1,0:T(8,128)(2,1)S(1)} %slice.173), channel_id=1, source_target_pairs={{0,4},{4,0},{1,5},{5,1},{2,6},{6,2},{3,7},{7,3},{8,12},{12,8},{9,1... | collective-permute-start | bytes 786440 | tf_op jit(solution)/shard_map/ppermute | solution.py:640
  391.4 19.2 %collective-permute-start.33 = (bf16[1024,1024]{1,0:T(8,128)(2,1)}, bf16[1024,1024]{1,0:T(8,128)(2,1)S(1)}, u32[]{:S(2)}, u32[]{:S(2)}) collective-permute-start(bf16[1024,1024]{1,0:T(8,128)(2,1)} %unproject.1), channel_id=1, source_target_pairs={{0,1},{1,0},{2,3},{3,2},{4,5},{5,4},{6,7},{7,6},{8,9},{9,8},{10,11... | collective-permute-start | bytes 6291464 | tf_op jit(solution)/shard_map/ppermute | solution.py:634
  392.8 92.6 %reduce-scatter.14.cloned.1.call-start = ((), (), s32[]{:S(2)}) async-start(), calls=%async_computation.9 | async-start | bytes 819200 | tf_op jit(solution)/shard_map/reduce_scatter | solution.py:763
  394.0 30.6 %collective-permute-start.43 = (bf16[128,1152]{1,0:T(8,128)(2,1)}, bf16[128,1152]{1,0:T(8,128)(2,1)S(1)}, u32[]{:S(2)}, u32[]{:S(2)}) collective-permute-start(bf16[128,1152]{1,0:T(8,128)(2,1)} %bitcast.24), channel_id=1, source_target_pairs={{0,4},{4,0},{1,5},{5,1},{2,6},{6,2},{3,7},{7,3},{8,12},{12,8},{9,1... | collective-permute-start | bytes 884744 | tf_op jit(solution)/shard_map/ppermute | solution.py:640
  394.5 33.1 %collective-permute-start.38 = (bf16[512,1024]{1,0:T(8,128)(2,1)}, bf16[512,1024]{1,0:T(8,128)(2,1)}, u32[]{:S(2)}, u32[]{:S(2)}) collective-permute-start(bf16[512,1024]{1,0:T(8,128)(2,1)} %copy-done.27), channel_id=1, source_target_pairs={{0,1},{1,0},{2,3},{3,2},{4,5},{5,4},{6,7},{7,6},{8,9},{9,8},{10,11... | collective-permute-start | bytes 3145736 | tf_op jit(solution)/shard_map/ppermute | solution.py:634
  394.7 41.2 %collective-permute-start.36 = (bf16[512,1024]{1,0:T(8,128)(2,1)}, bf16[512,1024]{1,0:T(8,128)(2,1)}, u32[]{:S(2)}, u32[]{:S(2)}) collective-permute-start(bf16[512,1024]{1,0:T(8,128)(2,1)} %copy-done.27), channel_id=1, source_target_pairs={{0,2},{1,3},{2,0},{3,1},{4,6},{5,7},{6,4},{7,5},{8,10},{9,11},{10,... | collective-permute-start | bytes 3145736 | tf_op jit(solution)/shard_map/ppermute | solution.py:637
  397.2 36.7 %collective-permute-start.48 = (bf16[128,1152]{1,0:T(8,128)(2,1)}, bf16[128,1152]{1,0:T(8,128)(2,1)}, u32[]{:S(2)}, u32[]{:S(2)}) collective-permute-start(bf16[128,1152]{1,0:T(8,128)(2,1)} %bitcast.123), channel_id=1, source_target_pairs={{0,4},{4,0},{1,5},{5,1},{2,6},{6,2},{3,7},{7,3},{8,12},{12,8},{9,1... | collective-permute-start | bytes 884744 | tf_op jit(solution)/shard_map/ppermute | solution.py:640
  422.7 40.2 %collective-permute-start.34 = (bf16[512,1024]{1,0:T(8,128)(2,1)S(1)}, bf16[512,1024]{1,0:T(8,128)(2,1)S(1)}, u32[]{:S(2)}, u32[]{:S(2)}) collective-permute-start(bf16[512,1024]{1,0:T(8,128)(2,1)S(1)} %dynamic-slice_bitcast_fusion), channel_id=1, source_target_pairs={{0,4},{4,0},{1,5},{5,1},{2,6},{6,2},{3,7},{7,3},{8,12},{12,8},{9,1... | collective-permute-start | bytes 3145736 | tf_op jit(solution)/shard_map/ppermute | solution.py:640
  424.6 38.3 %collective-permute-start.35 = (bf16[4,128,640]{2,1,0:T(8,128)(2,1)S(1)}, bf16[4,128,640]{2,1,0:T(8,128)(2,1)S(1)}, u32[]{:S(2)}, u32[]{:S(2)}) collective-permute-start(bf16[4,128,640]{2,1,0:T(8,128)(2,1)S(1)} %pad_maximum_fusion.7), channel_id=1, source_target_pairs={{0,4},{4,0},{1,5},{5,1},{2,6},{6,2},{3,7},{7,3},{8,12},{12,8},{9,1... | collective-permute-start | bytes 1966088 | tf_op jit(solution)/shard_map/ppermute | solution.py:640
  432.5 38.2 %collective-permute-start.44 = (bf16[128,1152]{1,0:T(8,128)(2,1)}, bf16[128,1152]{1,0:T(8,128)(2,1)}, u32[]{:S(2)}, u32[]{:S(2)}) collective-permute-start(bf16[128,1152]{1,0:T(8,128)(2,1)} %bitcast.25), channel_id=1, source_target_pairs={{0,4},{4,0},{1,5},{5,1},{2,6},{6,2},{3,7},{7,3},{8,12},{12,8},{9,1... | collective-permute-start | bytes 884744 | tf_op jit(solution)/shard_map/ppermute | solution.py:640
  466.6 25.7 %collective-permute-start.39 = (bf16[512,1024]{1,0:T(8,128)(2,1)S(1)}, bf16[512,1024]{1,0:T(8,128)(2,1)}, u32[]{:S(2)}, u32[]{:S(2)}) collective-permute-start(bf16[512,1024]{1,0:T(8,128)(2,1)S(1)} %fusion.5.a_ref), channel_id=1, source_target_pairs={{0,2},{1,3},{2,0},{3,1},{4,6},{5,7},{6,4},{7,5},{8,10},{9,11},{10,... | collective-permute-start | bytes 3145736 | tf_op jit(solution)/shard_map/ppermute | solution.py:637
  485.4 6.9 %collective-permute-start.42 = (bf16[128,640]{1,0:T(8,128)(2,1)}, bf16[128,640]{1,0:T(8,128)(2,1)S(1)}, u32[]{:S(2)}, u32[]{:S(2)}) collective-permute-start(bf16[128,640]{1,0:T(8,128)(2,1)} %bitcast.126), channel_id=1, source_target_pairs={{0,4},{4,0},{1,5},{5,1},{2,6},{6,2},{3,7},{7,3},{8,12},{12,8},{9,1... | collective-permute-start | bytes 491528 | tf_op jit(solution)/shard_map/ppermute | solution.py:640
  486.9 8.8 %collective-permute-start.47 = (bf16[128,256]{1,0:T(8,128)(2,1)S(1)}, bf16[128,256]{1,0:T(8,128)(2,1)S(1)}, u32[]{:S(2)}, u32[]{:S(2)}) collective-permute-start(bf16[128,256]{1,0:T(8,128)(2,1)S(1)} %bitcast.132), channel_id=1, source_target_pairs={{0,4},{4,0},{1,5},{5,1},{2,6},{6,2},{3,7},{7,3},{8,12},{12,8},{9,1... | collective-permute-start | bytes 196616 | tf_op jit(solution)/shard_map/ppermute | solution.py:640
  487.5 11.4 %collective-permute-start.37 = (bf16[512,1024]{1,0:T(8,128)(2,1)}, bf16[512,1024]{1,0:T(8,128)(2,1)S(1)}, u32[]{:S(2)}, u32[]{:S(2)}) collective-permute-start(bf16[512,1024]{1,0:T(8,128)(2,1)} %collective-permute-done.36.a_ref), channel_id=1, source_target_pairs={{0,1},{1,0},{2,3},{3,2},{4,5},{5,4},{6,7},{7,6},{8,9},{9,8},{10,11... | collective-permute-start | bytes 3145736 | tf_op jit(solution)/shard_map/ppermute | solution.py:634
  492.3 18.7 %collective-permute-start.40 = (bf16[512,1024]{1,0:T(8,128)(2,1)}, bf16[512,1024]{1,0:T(8,128)(2,1)S(1)}, u32[]{:S(2)}, u32[]{:S(2)}) collective-permute-start(bf16[512,1024]{1,0:T(8,128)(2,1)} %collective-permute-done.39.a_ref), channel_id=1, source_target_pairs={{0,1},{1,0},{2,3},{3,2},{4,5},{5,4},{6,7},{7,6},{8,9},{9,8},{10,11... | collective-permute-start | bytes 3145736 | tf_op jit(solution)/shard_map/ppermute | solution.py:634
  496.6 13.3 %collective-permute-start.46 = (f32[544]{0:T(1024)S(1)}, f32[544]{0:T(1024)S(1)}, u32[]{:S(2)}, u32[]{:S(2)}) collective-permute-start(f32[544]{0:T(1024)S(1)} %fusion.22), channel_id=1, source_target_pairs={{0,2},{1,3},{2,0},{3,1},{4,6},{5,7},{6,4},{7,5},{8,10},{9,11},{10,... | collective-permute-start | bytes 6536 | tf_op jit(solution)/shard_map/ppermute | solution.py:637
  (61 other events, 430.5 us)
Sparse Core Ops, SparseCore 0:
  10.2 52.8 all-gather.6
  64.7 28.4 all-gather.8
  107.9 51.4 all-gather.10
  275.8 27.7 reduce-scatter.5
  315.0 27.0 reduce-scatter.7
  344.9 27.8 reduce-scatter.9
  392.9 17.6 reduce-scatter.11
  465.0 20.3 reduce-scatter.13

commit v3 on v2

--- a/solution.py
+++ b/solution.py
@@ -716,9 +716,9 @@
     dy_13 = swap_core(dy_02)
     dy_own, dy_other = [dy_0, dy_13[0]], [dy_2, dy_13[1]]
 
-    tb = min(256, chunk)
+    tb, big = min(256, chunk), min(512, chunk)
     cos, sin = rope_tables(length)
-    normed, z, q, k, v = project(xs, gain_a, w_all, cos, sin, gain_q, gain_k, 2 * nq, 2 * nk, tb)
+    normed, z, q, k, v = project(xs, gain_a, w_all, cos, sin, gain_q, gain_k, 2 * nq, 2 * nk, big)
     if n_ctx == 2:
         q, down[1], gate[0] = tie(q, down[1], gate[0])
         gate.append(swap_ctx(gate[0]))
@@ -784,7 +784,8 @@
     dhidden = dy_0.astype(F32) + norm_back(hidden, h_scale, gain_f, dhn)
     dhr_0 = dhidden.astype(BF)
     dhr_1 = swap_core(dhr_0)
-    do = mm(jnp.concatenate([dhr_0, dhr_1], axis=0), w_out, NT).astype(BF)
+    dhr = jnp.concatenate([dhr_0, dhr_1], axis=0)
+    do = mm(dhr, w_out, NT).astype(BF)
 
     def ordinal(s, c):
         return 2 * s + c
@@ -792,43 +793,36 @@
     blocks = jnp.stack([ordinal(seq, core), ordinal(seq, 1 - core), ordinal(1 - seq, core), ordinal(1 - seq, 1 - core)])
     blocks = blocks.astype(jnp.int32)
 
-    out_give, out_keep = weight_sum([dhr_0, dhr_1], [o])
-    do, gate_got, out_keep = tie(do, gate_got, out_keep)
+    do, gate_got = tie(do, gate_got)
     s_gate = scatter(ctx_sum(g_gate, gate_got))
-    if n_ctx == 2:
-        out_theirs_got = swap_seq(jnp.concatenate([out_give[..., h_out:], out_keep[..., h_out:]], axis=0))
-        out_mine = jnp.concatenate([out_give[..., :h_out], out_keep[..., :h_out]], axis=0)
-    else:
-        out_theirs_got, out_mine = swap_seq(out_keep[..., h_out:]), out_keep[..., :h_out]
     dq, dk, dv = attend_back(ids, q, k, v, o, do, lse, chunk, 1)
-    dq, up_got, y_got, out_theirs_got = tie(dq, up_got, y_got, out_theirs_got)
+    dq, up_got, y_got = tie(dq, up_got, y_got)
     s_up = scatter(ctx_sum(g_up, up_got))
-    g_out = added(out_mine, out_theirs_got)
-    out_got = to_ctx(g_out[:n_dp], g_out)
     total = hidden + (y_0.astype(F32) + swap_core(y_1).astype(F32) + y_got.astype(F32))
     total = send_home(total.astype(BF))
-    d_theirs, gains_theirs = turn_back(ids, z, dq, dk, dv, cos, sin, gain_q, gain_k, tb, chunk, 1)
+    d_theirs, gains_theirs = turn_back(ids, z, dq, dk, dv, cos, sin, gain_q, gain_k, big, chunk, 1)
     give_theirs, keep_theirs = weight_sum([normed], [d_theirs])
-    do, keep_theirs, down_got, s_gate = tie(do, keep_theirs, down_got, s_gate)
+    dhr_0, keep_theirs = tie(dhr_0, keep_theirs)
+    out_give, out_keep = weight_sum([dhr_0, dhr_1], [o])
+    do, out_keep, down_got, s_gate = tie(do, out_keep, down_got, s_gate)
+    out_both = jnp.concatenate([out_give, out_keep], axis=0) if n_ctx == 2 else out_keep
+    out_got = swap_seq(out_both[..., h_out:])
     s_down = scatter(ctx_sum(g_down, down_got))
     qkv_got = swap_seq(jnp.concatenate([give_theirs, keep_theirs], axis=0) if n_ctx == 2 else keep_theirs)
     dq, dk, dv = attend_back(ids, q, k, v, o, do, lse, chunk, 0)
-    dq, qkv_got, out_got, total = tie(dq, qkv_got, out_got, total)
-    s_out = scatter(ctx_sum(g_out[n_dp:] if n_ctx == 2 else g_out, out_got))
+    dq, out_got, total = tie(dq, out_got, total)
+    g_out = added(out_both[..., :h_out], out_got)
+    out_got = to_ctx(g_out[:n_dp], g_out)
     total_core, total_seq = swap_core(total), swap_seq(total)
-    d_mine, gains_mine = turn_back(ids, z, dq, dk, dv, cos, sin, gain_q, gain_k, tb, chunk, 0)
-
-    d_mine, s_up, s_down = tie(d_mine, s_up, s_down)
+    d_mine, gains_mine = turn_back(ids, z, dq, dk, dv, cos, sin, gain_q, gain_k, big, chunk, 0)
+
+    d_mine, s_up, s_down, out_got, qkv_got = tie(d_mine, s_up, s_down, out_got, qkv_got)
+    s_out = scatter(ctx_sum(g_out[n_dp:], out_got) if n_ctx == 2 else g_out)
     parity = jnp.reshape(1 - core, (1,)).astype(jnp.int32)
-    give = unproject(parity, d_mine, d_theirs, w_all, tb, chunk)
+    give = unproject(parity, d_mine, d_theirs, w_all, big, chunk)
     got = swap_core(give)
     d_mine, give = tie(d_mine, give)
     give, keep = weight_sum([normed], [d_mine])
-    d_mine, keep, s_out, got = tie(d_mine, keep, s_out, got)
-    where = jnp.stack([core, id_here // 2]).astype(jnp.int32)
-    dz = close(where, d_mine, d_theirs, w_all, got, xs, gain_a, dhidden, tb, chunk)
-    dz = dz.reshape(n_ctx, chunk, width)
-
     fold = (gains_mine + gains_theirs)[:2]
     fold = (fold[:, :HD] + fold[:, HD:]).reshape(2, n_dp, h_part)
     fold = jnp.pad(fold, ((0, 0), (0, 0), (0, d_part - h_part))).reshape(2, width)
@@ -840,30 +834,35 @@
         keep = jnp.concatenate([added(keep, qkv_got[n_dp:]), fold_keep], axis=-1)
     else:
         keep = jnp.concatenate([added(keep, qkv_got), fold], axis=-1)
+    d_mine, give, got = tie(d_mine, give, got)
     qkv_got = to_ctx(give, keep)
+    where = jnp.stack([core, id_here // 2]).astype(jnp.int32)
+    dz = close(where, d_mine, d_theirs, w_all, got, xs, gain_a, dhidden, tb, chunk)
+    _, qkv_got = tie(dz, qkv_got)
+    s_qkv = scatter(ctx_sum(keep, qkv_got))
+    dz = dz.reshape(n_ctx, chunk, width)
     if n_ctx == 2:
-        dx = swap_ctx(lax.dynamic_index_in_dim(dz, 1 - ctx, 0, keepdims=False))
-        dx, qkv_got, total_seq = tie(dx, qkv_got, total_seq)
-        dx = added(lax.dynamic_index_in_dim(dz, ctx, 0, keepdims=False), dx)
+        dx_got = swap_ctx(lax.dynamic_index_in_dim(dz, 1 - ctx, 0, keepdims=False))
+        dx_kept = lax.dynamic_index_in_dim(dz, ctx, 0, keepdims=False)
     else:
-        dx = lax.psum_scatter(dz, "ctx", scatter_dimension=0, tiled=False)
-    s_qkv = scatter(ctx_sum(keep, qkv_got))
+        dx_got = lax.psum_scatter(dz, "ctx", scatter_dimension=0, tiled=False)
+
+    total, total_seq, _ = tie(total, total_seq, dz)
+    total_both = swap_core(total_seq)
+    out_low = put(blocks[:2], total, total_core, None, BF)
+    dx_got, s_qkv, s_out, out_low, total_both = tie(dx_got, s_qkv, s_out, out_low, total_both)
+    dx = added(dx_kept, dx_got) if n_ctx == 2 else dx_got
     dx_core, dx_seq = swap_core(dx), swap_seq(dx)
-    dx_core, s_qkv = tie(dx_core, s_qkv)
-
-    def join(piece, p_core, p_seq, kind):
-        out = put(blocks[:2], piece, p_core, None, kind)
-        out = put(blocks[2:], p_seq, swap_core(p_seq), out, kind)
-        return out.reshape(2, local_len, width)
-
-    layer_output = join(total, total_core, total_seq, BF)
-    input_grad = join(dx, dx_core, dx_seq, F32)
-
+    s_gate, s_up, s_down, s_qkv, s_out, dx = tie(s_gate, s_up, s_down, s_qkv, s_out, dx)
+    in_low = put(blocks[:2], dx, dx_core, None, F32)
+    layer_output = put(blocks[2:], total_seq, total_both, out_low, BF).reshape(2, local_len, width)
     gate_grad = gather_rows(s_gate).astype(F32)
     up_grad = gather_rows(s_up).astype(F32)
     down_grad = gather_rows(s_down).T.astype(F32)
+    g = gather_rows(s_qkv).astype(F32)
+    dx_seq, in_low, layer_output, gate_grad, up_grad, down_grad = tie(dx_seq, in_low, layer_output, gate_grad, up_grad, down_grad)
+    input_grad = put(blocks[2:], dx_seq, swap_core(dx_seq), in_low, F32).reshape(2, local_len, width)
     out_grad = gather_rows(s_out).T.astype(F32)
-    g = gather_rows(s_qkv).astype(F32)
     query_grad, key_grad, value_grad = g[:, :nq], g[:, nq:nq + nk], g[:, nq + nk:n_qkv]
 
     attn_sum = jnp.sum(query_weight.astype(F32) * query_grad, axis=1) + jnp.sum(key_weight.astype(F32) * key_grad, axis=1)

time: 534 us -> 505 us (0.946)
  waiting for transfers between devices: 113 us -> 96.6 us
  other arithmetic: 48.4 us -> 42.6 us
  local copies, waits for them, and re-layouts: 57.4 us -> 52 us
    reduce_scatter x5, waiting for transfers between devices: 18.6 us -> 0.02 us  [scatter(): return lax.psum_scatter(half, 'dp', scatter_dimension=0, tiled=False)]
    ppermute x14, waiting for transfers between devices: 36.9 us -> 45.4 us  [swap_ctx(): return lax.ppermute(x, 'ctx', [(0, 1), (1, 0)])]
    ppermute x14, waiting for transfers between devices: 24.1 us -> 18.1 us  [swap_seq(): return lax.ppermute(x, 'tensor', [(i, i ^ 2) for i in range(n_tensor)])]
    unnamed x110 -> x105, local copies, waits for them, and re-layouts: 12 us -> 10.6 us
  transfers between devices with their start and end apart: 57 -> 57, of which waited for: 20 -> 22; matrix products, arithmetic and copies ran while one was open for 18% -> 17% of each run, Pallas kernels for 37% -> 39%
where the time goes in v3:
time: 505 us; the launch traced here: 495 us
  Pallas kernels  229 us (45%)
  waiting for transfers between devices  96.6 us (19%)
  local copies, waits for them, and re-layouts  52 us (10%)
  starting transfers between devices  50.1 us (10%)
  other arithmetic  42.6 us (8%)
  between operations  15.5 us (3%)
  matrix products  9.1 us (2%)
    pallas_call x2, Pallas kernels, feed(): pl.pallas_call(functools.partial(feed_kernel, n_pieces=n_pieces), grid_sp...  50.5 us
    pallas_call x6, Pallas kernels, weight_grad(): pl.pallas_call(functools.partial(weight_grad_kernel, n_left=len(lefts), n...  50.4 us
    ppermute x14, waiting for transfers between devices, swap_ctx(): return lax.ppermute(x, 'ctx', [(0, 1), (1, 0)])  45.4 us
    pallas_call x2, Pallas kernels, attend_back(): pl.pallas_call(attend_back_kernel, grid_spec=pltpu.PrefetchScalarGridSpec...  40.8 us
    pallas_call x4, Pallas kernels, put(): pl.pallas_call(put_kernel, grid_spec=pltpu.PrefetchScalarGridSpec(num_sca...  20.3 us
    ppermute x14, starting transfers between devices, swap_seq(): return lax.ppermute(x, 'tensor', [(i, i ^ 2) for i in range(n_tensor)])  20 us
    pallas_call x1, Pallas kernels, attend(): pl.pallas_call(attend_kernel, grid_spec=pltpu.PrefetchScalarGridSpec(num_...  19.1 us
    pallas_call x2, Pallas kernels, turn_back(): pl.pallas_call(functools.partial(turn_back_kernel, per_chunk=chunk // tb)...  18.8 us
  transfers between devices with their start and end apart: 57, of which 22 were waited for; matrix products, arithmetic and copies ran while one was open for 17% of the time, Pallas kernels for 39%

profile of v3, /device:TPU:0, one launch (start us, length us, event | category | flops | bytes accessed | tf_op | source)
XLA Modules:
  0.0 495.1 jit_solution(10356830167659723088)
XLA Ops:
  13.0 3.0 collective-permute-start.5
  28.5 3.7 fusion.11
  32.3 3.0 pad_maximum_fusion.1
  40.1 2.5 broadcast_in_dim.26
  46.9 10.8 %collective-permute-done.3 = bf16[256,640]{1,0:T(8,128)(2,1)} collective-permute-done((bf16[256,640]{1,0:T(8,128)(2,1)}, bf16[256,640]{1,0:T(8,128)(2,1)}, u32[]{:S(2)}, u32[]{:S(2)}) %collective-permute-start.3) | collective-permute-done | bytes 327712 | tf_op jit(solution)/shard_map/ppermute | solution.py:688
  60.9 2.8 collective-permute-start.4
  69.3 4.8 collective-permute-done.4
  84.1 3.0 constant_dynamic-update-slice_fusion.13.x_ref
  87.2 14.1 %project.1 = (bf16[2048,1024]{1,0:T(8,128)(2,1)}, f32[2048,1024]{1,0:T(8,128)}, bf16[2048,512]{1,0:T(8,128)(2,1)}, bf16[2048,512]{1,0:T(8,128)(2,1)}, bf16[2048,512]{1,0:T(8,128)(2,1)}) custom-call(bf16[2048,1024]{1,0:T(8,128)(2,1)} %constant_dynamic-update-slice_fusion.13.x_ref, f32[1,1024]{1,0:T(1,128)} %bitcast.133, bf16[1024,1024]{1,0:T(8,128)(2,1)} %copy-done.11, ...), custom_call_target="tpu_custom_call" | custom-call | flops 4294967 | bytes 28672 | tf_op jit(solution)/shard_map/project/pallas_call | solution.py:103
  107.9 19.1 %attend.1 = (bf16[1024,512]{1,0:T(8,128)(2,1)}, f32[32,1024]{1,0:T(8,128)}) custom-call(s32[2]{0:T(128)} %get-tuple-element.260.ids, bf16[2048,512]{1,0:T(8,128)(2,1)} %get-tuple-element.120.q_ref, bf16[2048,512]{1,0:T(8,128)(2,1)} %get-tuple-element.121.k_ref, bf16[2048,512]{1,0:T(8,128)(2,1)} %get-tuple-element.122.v_ref), custom_call_target="tpu_custom_call" | custom-call | flops 5368709 | bytes 6291 | tf_op jit(solution)/shard_map/attend/pallas_call | solution.py:172
  127.2 5.2 %fusion.9 = f32[1024,1024]{1,0:T(8,128)} fusion(bf16[1024,512]{1,0:T(8,128)(2,1)} %get-tuple-element.125.o_ref.refs_8_, bf16[256,1024]{0,1:T(8,128)(2,1)} %collective-permute-done.12, bf16[256,1024]{0,1:T(8,128)(2,1)} %bitcast.15), kind=kOutput, calls=%fused_computation.40 | convolution fusion | flops 1075838976 | bytes 6291456 | tf_op jit(solution)/shard_map/dot_general | solution.py:32
  132.4 2.7 slice.205
  135.2 3.7 collective-permute-done.15.refs_2_.refs_8_.refs_9_.refs_10_.refs_11_
  146.6 3.0 slice_bitcast_fusion
  149.6 8.9 %all-gather.11.cloned.1.call-done = bf16[1024,1152]{1,0:T(8,128)(2,1)} async-done(((bf16[256,1152]{1,0:T(8,128)(2,1)}), bf16[1024,1152]{1,0:T(8,128)(2,1)}) %all-gather.11.cloned.1.call-update) | async-done | bytes 2359312 | tf_op jit(solution)/shard_map/all_gather | solution.py:700
  159.5 25.0 %feed.2 = (bf16[1024,1152]{1,0:T(8,128)(2,1)}, bf16[1024,1152]{1,0:T(8,128)(2,1)}, bf16[1024,1152]{1,0:T(8,128)(2,1)}, bf16[512,1024]{1,0:T(8,128)(2,1)}, bf16[5...) custom-call(s32[1]{0:T(128)} %bitcast.16.place, bf16[512,1024]{1,0:T(8,128)(2,1)} %copy-done.2, ...), custom_call_target="tpu_custom_call" | custom-call | flops 14495514 | bytes 22437 | tf_op jit(solution)/shard_map/feed/pallas_call | solution.py:420
  184.6 2.6 collective-permute-done.19.refs_1_.refs_12_.refs_13_.refs_14_.refs_15_
  188.2 25.5 %feed.3 = (bf16[1024,1152]{1,0:T(8,128)(2,1)}, bf16[1024,1152]{1,0:T(8,128)(2,1)}, bf16[1024,1152]{1,0:T(8,128)(2,1)}, bf16[512,1024]{1,0:T(8,128)(2,1)}, bf16[5...) custom-call(s32[1]{0:T(128)} %bitcast.16.place, bf16[512,1024]{1,0:T(8,128)(2,1)} %copy-done.4, ...), custom_call_target="tpu_custom_call" | custom-call | flops 14495514 | bytes 22437 | tf_op jit(solution)/shard_map/feed/pallas_call | solution.py:420
  216.6 2.6 add_convert_fusion.4
  219.3 11.0 %weight_grad.6 = (bf16[4,128,1152]{2,1,0:T(8,128)(2,1)}, bf16[4,128,1152]{2,1,0:T(8,128)(2,1)}) custom-call(s32[1]{0:T(128)} %bitcast.16.place, bf16[512,1024]{1,0:T(8,128)(2,1)} %copy-done.2, bf16[512,1024]{1,0:T(8,128)(2,1)} %copy-done.2, bf16[512,1024]{1,0:T(8,128)(2,1)} %copy-done.2, bf16[512,1024]{1,0:T(8,128)(2,1)} %copy-done.2, ...), custom_call_target="tpu_custom_call" | custom-call | flops 4831838 | bytes 8912 | tf_op jit(solution)/shard_map/weight_grad/pallas_call | solution.py:472
  233.3 11.1 %weight_grad.7 = (bf16[4,128,1152]{2,1,0:T(8,128)(2,1)}, bf16[4,128,1152]{2,1,0:T(8,128)(2,1)}) custom-call(s32[1]{0:T(128)} %bitcast.16.place, bf16[512,1024]{1,0:T(8,128)(2,1)} %copy-done.2, bf16[512,1024]{1,0:T(8,128)(2,1)} %copy-done.2, bf16[512,1024]{1,0:T(8,128)(2,1)} %copy-done.2, bf16[512,1024]{1,0:T(8,128)(2,1)} %copy-done.2, ...), custom_call_target="tpu_custom_call" | custom-call | flops 4831838 | bytes 8912 | tf_op jit(solution)/shard_map/weight_grad/pallas_call | solution.py:472
  244.4 11.3 %weight_grad.8 = (bf16[4,128,1152]{2,1,0:T(8,128)(2,1)}, bf16[4,128,1152]{2,1,0:T(8,128)(2,1)}) custom-call(s32[1]{0:T(128)} %bitcast.16.place, bf16[512,1024]{1,0:T(8,128)(2,1)} %copy-done.8, bf16[512,1024]{1,0:T(8,128)(2,1)} %copy-done.8, bf16[512,1024]{1,0:T(8,128)(2,1)} %copy-done.8, bf16[512,1024]{1,0:T(8,128)(2,1)} %copy-done.8, ...), custom_call_target="tpu_custom_call" | custom-call | flops 4831838 | bytes 8912 | tf_op jit(solution)/shard_map/weight_grad/pallas_call | solution.py:472
  262.1 2.7 collective-permute-done.24.refs_4_.refs_5_.refs_6_.refs_7_
  264.8 3.9 fusion.6.do_ref
  273.0 20.5 %attend_back.2 = (f32[2048,256]{1,0:T(8,128)}, f32[2048,256]{1,0:T(8,128)}, f32[2048,256]{1,0:T(8,128)}) custom-call(s32[2]{0:T(128)} %get-tuple-element.260.ids, bf16[2048,512]{1,0:T(8,128)(2,1)} %get-tuple-element.120.q_ref, bf16[2048,512]{1,0:T(8,128)(2,1)} %get-tuple-element.121.k_ref, bf16[2048,512]{1,0:T(8,128)(2,1)} %get-tuple-element.122.v_ref, ...), custom_call_target="tpu_custom_call" | custom-call | flops 6710886 | bytes 9437 | tf_op jit(solution)/shard_map/attend_back/pallas_call | solution.py:248
  293.6 4.7 collective-permute-done.25
  301.3 9.5 %turn_back.2 = (bf16[2048,512]{1,0:T(8,128)(2,1)}, f32[8,128]{1,0:T(8,128)}) custom-call(s32[2]{0:T(128)} %get-tuple-element.260.ids, f32[2048,1024]{1,0:T(8,128)} %get-tuple-element.118.z_ref, f32[2048,256]{1,0:T(8,128)} %get-tuple-element.160.dq_ref, f32[2048,256]{1,0:T(8,128)} %get-tuple-element.161.dk_ref, f32[2048,256]{1,0:T(8,128)} %get-tuple-element.162.dv_ref, ...), custom_call_target="tpu_custom_call" | custom-call | flops 409600 | bytes 24576 | tf_op jit(solution)/shard_map/turn_back/pallas_call | solution.py:317
  310.8 6.2 %weight_grad.9 = (bf16[4,128,512]{2,1,0:T(8,128)(2,1)}, bf16[4,128,512]{2,1,0:T(8,128)(2,1)}) custom-call(s32[1]{0:T(128)} %bitcast.16.place, bf16[2048,1024]{1,0:T(8,128)(2,1)} %get-tuple-element.155.refs_0_.refs_1_.refs_2_.refs_3_, bf16[2048,1024]{1,0:T(8,128)(2,1)} %get-tuple-element.155.refs_0_.refs_1_.refs_2_.refs_3_, ...), custom_call_target="tpu_custom_call" | custom-call | flops 2147483 | bytes 6291 | tf_op jit(solution)/shard_map/weight_grad/pallas_call | solution.py:472
  317.0 4.6 weight_grad.10
  321.7 5.7 %collective-permute-done.27 = bf16[4,128,1152]{2,1,0:T(8,128)(2,1)} collective-permute-done((bf16[4,128,1152]{2,1,0:T(8,128)(2,1)}, bf16[4,128,1152]{2,1,0:T(8,128)(2,1)}, u32[]{:S(2)}, u32[]{:S(2)}) %collective-permute-start.27) | collective-permute-done | bytes 1179680 | tf_op jit(solution)/shard_map/ppermute | solution.py:640
  327.3 2.6 add_convert_fusion
  330.0 2.7 add_convert_fusion.3
  336.9 20.2 %attend_back.3 = (f32[2048,256]{1,0:T(8,128)}, f32[2048,256]{1,0:T(8,128)}, f32[2048,256]{1,0:T(8,128)}) custom-call(s32[2]{0:T(128)} %get-tuple-element.260.ids, bf16[2048,512]{1,0:T(8,128)(2,1)} %get-tuple-element.120.q_ref, bf16[2048,512]{1,0:T(8,128)(2,1)} %get-tuple-element.121.k_ref, bf16[2048,512]{1,0:T(8,128)(2,1)} %get-tuple-element.122.v_ref, ...), custom_call_target="tpu_custom_call" | custom-call | flops 6710886 | bytes 9437 | tf_op jit(solution)/shard_map/attend_back/pallas_call | solution.py:248
  358.9 9.3 %turn_back.3 = (bf16[2048,512]{1,0:T(8,128)(2,1)}, f32[8,128]{1,0:T(8,128)}) custom-call(s32[2]{0:T(128)} %get-tuple-element.260.ids, f32[2048,1024]{1,0:T(8,128)} %get-tuple-element.118.z_ref, f32[2048,256]{1,0:T(8,128)} %get-tuple-element.177.dq_ref, f32[2048,256]{1,0:T(8,128)} %get-tuple-element.178.dk_ref, f32[2048,256]{1,0:T(8,128)} %get-tuple-element.179.dv_ref, ...), custom_call_target="tpu_custom_call" | custom-call | flops 409600 | bytes 24576 | tf_op jit(solution)/shard_map/turn_back/pallas_call | solution.py:317
  368.1 2.7 collective-permute-done.32
  370.9 5.6 %unproject.1 = bf16[1024,1024]{1,0:T(8,128)(2,1)} custom-call(s32[1]{0:T(128)} %bitcast.25.parity, bf16[2048,512]{1,0:T(8,128)(2,1)} %get-tuple-element.194.a_ref.refs_4_, bf16[2048,512]{1,0:T(8,128)(2,1)} %get-tuple-element.163.refs_4_.b_ref, bf16[1024,1024]{1,0:T(8,128)(2,1)} %copy-done.11), custom_call_target="tpu_custom_call" | custom-call | flops 2147483 | bytes 8388 | tf_op jit(solution)/shard_map/unproject/pallas_call | solution.py:535
  377.5 6.2 %weight_grad.11 = (bf16[4,128,512]{2,1,0:T(8,128)(2,1)}, bf16[4,128,512]{2,1,0:T(8,128)(2,1)}) custom-call(s32[1]{0:T(128)} %bitcast.16.place, bf16[2048,1024]{1,0:T(8,128)(2,1)} %get-tuple-element.155.refs_0_.refs_1_.refs_2_.refs_3_, bf16[2048,1024]{1,0:T(8,128)(2,1)} %get-tuple-element.155.refs_0_.refs_1_.refs_2_.refs_3_, ...), custom_call_target="tpu_custom_call" | custom-call | flops 2147483 | bytes 6291 | tf_op jit(solution)/shard_map/weight_grad/pallas_call | solution.py:472
  388.8 9.7 %close.1 = bf16[1024,1024]{1,0:T(8,128)(2,1)} custom-call(s32[2]{0:T(128)} %pad_add_fusion.where, bf16[2048,512]{1,0:T(8,128)(2,1)} %get-tuple-element.194.a_ref.refs_4_, bf16[2048,512]{1,0:T(8,128)(2,1)} %get-tuple-element.163.refs_4_.b_ref, bf16[1024,1024]{1,0:T(8,128)(2,1)} %copy-done.11, bf16[1024,1024]{1,0:T(8,128)(2,1)} %collective-permute-done.33.got_ref, ...), custom_call_target="tpu_custom_call" | custom-call | flops 2147483 | bytes 10485 | tf_op jit(solution)/shard_map/close/pallas_call | solution.py:571
  398.5 4.1 collective-permute-done.35
  405.8 5.7 %collective-permute-done.36.a_ref = bf16[512,1024]{1,0:T(8,128)(2,1)} collective-permute-done((bf16[512,1024]{1,0:T(8,128)(2,1)}, bf16[512,1024]{1,0:T(8,128)(2,1)}, u32[]{:S(2)}, u32[]{:S(2)}) %collective-permute-start.36) | collective-permute-done | bytes 1048608 | tf_op jit(solution)/shard_map/ppermute | solution.py:637
  414.5 4.8 put.4.refs_0_
  419.3 16.9 %collective-permute-done.34 = bf16[512,1024]{1,0:T(8,128)(2,1)} collective-permute-done((bf16[512,1024]{1,0:T(8,128)(2,1)}, bf16[512,1024]{1,0:T(8,128)(2,1)}, u32[]{:S(2)}, u32[]{:S(2)}) %collective-permute-start.34) | collective-permute-done | bytes 1048608 | tf_op jit(solution)/shard_map/ppermute | solution.py:640
  436.2 2.6 fusion.5.a_ref
  443.8 4.9 put.6
  452.2 6.7 %collective-permute-done.43 = bf16[128,1152]{1,0:T(8,128)(2,1)S(1)} collective-permute-done((bf16[128,1152]{1,0:T(8,128)(2,1)S(1)}, bf16[128,1152]{1,0:T(8,128)(2,1)S(1)}, u32[]{:S(2)}, u32[]{:S(2)}) %collective-permute-start.43) | collective-permute-done | bytes 294944 | tf_op jit(solution)/shard_map/ppermute | solution.py:640
  461.6 5.7 %collective-permute-done.42 = bf16[128,1152]{1,0:T(8,128)(2,1)S(1)} collective-permute-done((bf16[128,1152]{1,0:T(8,128)(2,1)S(1)}, bf16[128,1152]{1,0:T(8,128)(2,1)S(1)}, u32[]{:S(2)}, u32[]{:S(2)}) %collective-permute-start.42) | collective-permute-done | bytes 294944 | tf_op jit(solution)/shard_map/ppermute | solution.py:640
  467.7 5.3 %put.5.refs_0_ = f32[2048,1024]{1,0:T(8,128)} custom-call(s32[2]{0:T(128)} %pad_add_fusion.2.where, bf16[512,1024]{1,0:T(8,128)(2,1)} %fusion.5.a_ref, bf16[512,1024]{1,0:T(8,128)(2,1)} %collective-permute-done.40.b_ref), custom_call_target="tpu_custom_call" | custom-call | bytes 6291 | tf_op jit(solution)/shard_map/put/pallas_call | solution.py:505
  482.5 5.3 %put.7 = f32[2048,1024]{1,0:T(8,128)} custom-call(s32[2]{0:T(128)} %get-tuple-element.261.where, bf16[512,1024]{1,0:T(8,128)(2,1)} %collective-permute-done.39.a_ref, bf16[512,1024]{1,0:T(8,128)(2,1)} %copy-done.30, f32[2048,1024]{1,0:T(8,128)} %put.5.refs_0_), custom_call_target="tpu_custom_call", output_to_operand_aliasing={{}: (3, {})} | custom-call | bytes 6291 | tf_op jit(solution)/shard_map/put/pallas_call | solution.py:505
  (301 shorter events, 121.2 us)
Async XLA Ops:
  7.3 58.0 %all-gather.7.cloned.1.call-start = ((), (), s32[]{:S(2)}) async-start(), calls=%async_computation.10 | async-start | bytes 2129920 | tf_op jit(solution)/shard_map/all_gather | solution.py:700
  10.1 91.1 %all-gather.9.cloned.1.call-start = ((), (), s32[]{:S(2)}) async-start(), calls=%async_computation.11 | async-start | bytes 1474560 | tf_op jit(solution)/shard_map/all_gather | solution.py:700
  13.0 22.3 %collective-permute-start.5 = (bf16[256,512]{1,0:T(8,128)(2,1)}, bf16[256,512]{1,0:T(8,128)(2,1)}, u32[]{:S(2)}, u32[]{:S(2)}) collective-permute-start(bf16[256,512]{1,0:T(8,128)(2,1)} %constant_dynamic-update-slice_fusion), channel_id=1, source_target_pairs={{0,2},{1,3},{2,0},{3,1},{4,6},{5,7},{6,4},{7,5},{8,10},{9,11},{10,... | collective-permute-start | bytes 786440 | tf_op jit(solution)/shard_map/ppermute | solution.py:637
  16.8 19.5 %collective-permute-start.2 = (bf16[256,640]{1,0:T(8,128)(2,1)}, bf16[256,640]{1,0:T(8,128)(2,1)}, u32[]{:S(2)}, u32[]{:S(2)}) collective-permute-start(bf16[256,640]{1,0:T(8,128)(2,1)} %fusion.12), channel_id=1, source_target_pairs={{0,8},{8,16},{16,24},{24,0},{1,9},{9,17},{17,25},{25,1},{2,10},{10... | collective-permute-start | bytes 983048 | tf_op jit(solution)/shard_map/ppermute | solution.py:688
  20.8 44.4 %collective-permute-start = (bf16[512,1024]{1,0:T(8,128)(2,1)}, bf16[512,1024]{1,0:T(8,128)(2,1)}, u32[]{:S(2)}, u32[]{:S(2)}) collective-permute-start(bf16[512,1024]{1,0:T(8,128)(2,1)} %dynamic-slice_bitcast_fusion.2), channel_id=1, source_target_pairs={{0,4},{4,0},{1,5},{5,1},{2,6},{6,2},{3,7},{7,3},{8,12},{12,8},{9,1... | collective-permute-start | bytes 3145736 | tf_op jit(solution)/shard_map/ppermute | solution.py:640
  24.5 82.1 %collective-permute-start.11 = (bf16[512,1024]{1,0:T(8,128)(2,1)}, bf16[512,1024]{1,0:T(8,128)(2,1)S(1)}, u32[]{:S(2)}, u32[]{:S(2)}) collective-permute-start(bf16[512,1024]{1,0:T(8,128)(2,1)} %dynamic-slice_bitcast_fusion.1), channel_id=1, source_target_pairs={{0,0},{5,1},{2,2},{7,3},{4,4},{1,5},{6,6},{3,7},{8,8},{13,9},{10,1... | collective-permute-start | bytes 3145736 | tf_op jit(solution)/shard_map/ppermute | solution.py:652
  27.2 131.3 %all-gather.11.cloned.1.call-start = ((), (), s32[]{:S(2)}) async-start(), calls=%async_computation.12 | async-start | bytes 2949120 | tf_op jit(solution)/shard_map/all_gather | solution.py:700
  38.0 7.9 %collective-permute-start.6 = (bf16[256,512]{1,0:T(8,128)(2,1)}, bf16[256,512]{1,0:T(8,128)(2,1)}, u32[]{:S(2)}, u32[]{:S(2)}) collective-permute-start(bf16[256,512]{1,0:T(8,128)(2,1)} %get-tuple-element.245), channel_id=1, source_target_pairs={{0,2},{1,3},{2,0},{3,1},{4,6},{5,7},{6,4},{7,5},{8,10},{9,11},{10,... | collective-permute-start | bytes 786440 | tf_op jit(solution)/shard_map/ppermute | solution.py:637
  38.6 19.1 %collective-permute-start.3 = (bf16[256,640]{1,0:T(8,128)(2,1)}, bf16[256,640]{1,0:T(8,128)(2,1)}, u32[]{:S(2)}, u32[]{:S(2)}) collective-permute-start(bf16[256,640]{1,0:T(8,128)(2,1)} %collective-permute-done.2), channel_id=1, source_target_pairs={{0,8},{8,16},{16,24},{24,0},{1,9},{9,17},{17,25},{25,1},{2,10},{10... | collective-permute-start | bytes 983048 | tf_op jit(solution)/shard_map/ppermute | solution.py:688
  60.9 13.1 %collective-permute-start.4 = (bf16[256,640]{1,0:T(8,128)(2,1)}, bf16[256,640]{1,0:T(8,128)(2,1)}, u32[]{:S(2)}, u32[]{:S(2)}) collective-permute-start(bf16[256,640]{1,0:T(8,128)(2,1)} %collective-permute-done.3), channel_id=1, source_target_pairs={{0,8},{8,16},{16,24},{24,0},{1,9},{9,17},{17,25},{25,1},{2,10},{10... | collective-permute-start | bytes 983048 | tf_op jit(solution)/shard_map/ppermute | solution.py:688
  65.1 19.0 %collective-permute-start.1 = (bf16[512,1024]{1,0:T(8,128)(2,1)}, bf16[512,1024]{1,0:T(8,128)(2,1)}, u32[]{:S(2)}, u32[]{:S(2)}) collective-permute-start(bf16[512,1024]{1,0:T(8,128)(2,1)} %collective-permute-done), channel_id=1, source_target_pairs={{0,1},{1,0},{2,3},{3,2},{4,5},{5,4},{6,7},{7,6},{8,9},{9,8},{10,11... | collective-permute-start | bytes 3145736 | tf_op jit(solution)/shard_map/ppermute | solution.py:634
  67.6 33.6 %collective-permute-start.9 = (bf16[4,576,256]{2,1,0:T(8,128)(2,1)}, bf16[4,576,256]{2,1,0:T(8,128)(2,1)}, u32[]{:S(2)}, u32[]{:S(2)}) collective-permute-start(bf16[4,576,256]{2,1,0:T(8,128)(2,1)} %slice.158.refs_7_), channel_id=1, source_target_pairs={{0,4},{4,0},{1,5},{5,1},{2,6},{6,2},{3,7},{7,3},{8,12},{12,8},{9,1... | collective-permute-start | bytes 3538952 | tf_op jit(solution)/shard_map/ppermute | solution.py:640
  101.3 26.0 %collective-permute-start.10 = (bf16[4,128,1152]{2,1,0:T(8,128)(2,1)}, bf16[4,128,1152]{2,1,0:T(8,128)(2,1)S(1)}, u32[]{:S(2)}, u32[]{:S(2)}) collective-permute-start(bf16[4,128,1152]{2,1,0:T(8,128)(2,1)} %bitcast.113), channel_id=1, source_target_pairs={{0,4},{4,0},{1,5},{5,1},{2,6},{6,2},{3,7},{7,3},{8,12},{12,8},{9,1... | collective-permute-start | bytes 3538952 | tf_op jit(solution)/shard_map/ppermute | solution.py:640
  104.9 22.3 %collective-permute-start.12 = (bf16[256,1024]{0,1:T(8,128)(2,1)}, bf16[256,1024]{0,1:T(8,128)(2,1)}, u32[]{:S(2)}, u32[]{:S(2)}) collective-permute-start(bf16[256,1024]{0,1:T(8,128)(2,1)} %bitcast.15), channel_id=1, source_target_pairs={{0,2},{1,3},{2,0},{3,1},{4,6},{5,7},{6,4},{7,5},{8,10},{9,11},{10,... | collective-permute-start | bytes 1572872 | tf_op jit(solution)/shard_map/ppermute | solution.py:637
  106.6 32.3 %collective-permute-start.15 = (bf16[512,1024]{1,0:T(8,128)(2,1)S(1)}, bf16[512,1024]{1,0:T(8,128)(2,1)S(1)}, u32[]{:S(2)}, u32[]{:S(2)}) collective-permute-start(bf16[512,1024]{1,0:T(8,128)(2,1)S(1)} %collective-permute-done.11.refs_2_.refs_0_.refs_1_.refs_3_), channel_id=1, source_target_pairs={{0,2},{1,3},{2,0},{3,1},{4,6},{5,7},{6,4},{7,5},{8,10},{9,11},{10,... | collective-permute-start | bytes 3145736 | tf_op jit(solution)/shard_map/ppermute | solution.py:637
  106.9 220.4 %reduce-scatter.6.cloned.1.call-start = ((), (), s32[]{:S(2)}) async-start(), calls=%async_computation.5 | async-start | bytes 1474560 | tf_op jit(solution)/shard_map/reduce_scatter | solution.py:763
  144.4 14.1 %collective-permute-start.14 = (bf16[512,1024]{1,0:T(8,128)(2,1)S(1)}, bf16[512,1024]{1,0:T(8,128)(2,1)S(1)}, u32[]{:S(2)}, u32[]{:S(2)}) collective-permute-start(bf16[512,1024]{1,0:T(8,128)(2,1)S(1)} %multiply_convert_fusion.refs_0_.refs_1_.refs_2_.refs_3_), channel_id=1, source_target_pairs={{0,1},{1,0},{2,3},{3,2},{4,5},{5,4},{6,7},{7,6},{8,9},{9,8},{10,11... | collective-permute-start | bytes 3145736 | tf_op jit(solution)/shard_map/ppermute | solution.py:634
  144.8 39.7 %collective-permute-start.18 = (bf16[512,1024]{1,0:T(8,128)(2,1)S(1)}, bf16[512,1024]{1,0:T(8,128)(2,1)S(1)}, u32[]{:S(2)}, u32[]{:S(2)}) collective-permute-start(bf16[512,1024]{1,0:T(8,128)(2,1)S(1)} %multiply_convert_fusion.refs_0_.refs_1_.refs_2_.refs_3_), channel_id=1, source_target_pairs={{0,2},{1,3},{2,0},{3,1},{4,6},{5,7},{6,4},{7,5},{8,10},{9,11},{10,... | collective-permute-start | bytes 3145736 | tf_op jit(solution)/shard_map/ppermute | solution.py:637
  213.9 41.8 %collective-permute-start.20 = (bf16[512,1024]{1,0:T(8,128)(2,1)}, bf16[512,1024]{1,0:T(8,128)(2,1)S(1)}, u32[]{:S(2)}, u32[]{:S(2)}) collective-permute-start(bf16[512,1024]{1,0:T(8,128)(2,1)} %get-tuple-element.133), channel_id=1, source_target_pairs={{0,1},{1,0},{2,3},{3,2},{4,5},{5,4},{6,7},{7,6},{8,9},{9,8},{10,11... | collective-permute-start | bytes 3145736 | tf_op jit(solution)/shard_map/ppermute | solution.py:634
  230.3 28.3 %collective-permute-start.23 = (bf16[4,128,1152]{2,1,0:T(8,128)(2,1)}, bf16[4,128,1152]{2,1,0:T(8,128)(2,1)S(1)}, u32[]{:S(2)}, u32[]{:S(2)}) collective-permute-start(bf16[4,128,1152]{2,1,0:T(8,128)(2,1)} %get-tuple-element.150), channel_id=1, source_target_pairs={{0,4},{4,0},{1,5},{5,1},{2,6},{6,2},{3,7},{7,3},{8,12},{12,8},{9,1... | collective-permute-start | bytes 3538952 | tf_op jit(solution)/shard_map/ppermute | solution.py:640
  231.9 25.3 %collective-permute-start.22 = (bf16[512,1024]{1,0:T(8,128)(2,1)}, bf16[512,1024]{1,0:T(8,128)(2,1)S(1)}, u32[]{:S(2)}, u32[]{:S(2)}) collective-permute-start(bf16[512,1024]{1,0:T(8,128)(2,1)} %add_convert_fusion.4), channel_id=1, source_target_pairs={{0,2},{1,3},{2,0},{3,1},{4,6},{5,7},{6,4},{7,5},{8,10},{9,11},{10,... | collective-permute-start | bytes 3145736 | tf_op jit(solution)/shard_map/ppermute | solution.py:637
  233.3 25.3 %collective-permute-start.17 = (bf16[512,1024]{1,0:T(8,128)(2,1)}, bf16[512,1024]{1,0:T(8,128)(2,1)S(1)}, u32[]{:S(2)}, u32[]{:S(2)}) collective-permute-start(bf16[512,1024]{1,0:T(8,128)(2,1)} %get-tuple-element.129), channel_id=1, source_target_pairs={{0,1},{1,0},{2,3},{3,2},{4,5},{5,4},{6,7},{7,6},{8,9},{9,8},{10,11... | collective-permute-start | bytes 3145736 | tf_op jit(solution)/shard_map/ppermute | solution.py:634
  270.0 100.9 %reduce-scatter.8.cloned.1.call-start = ((), (), s32[]{:S(2)}) async-start(), calls=%async_computation.6 | async-start | bytes 1474560 | tf_op jit(solution)/shard_map/reduce_scatter | solution.py:763
  270.0 28.3 %collective-permute-start.25 = (bf16[4,128,1152]{2,1,0:T(8,128)(2,1)}, bf16[4,128,1152]{2,1,0:T(8,128)(2,1)S(1)}, u32[]{:S(2)}, u32[]{:S(2)}) collective-permute-start(bf16[4,128,1152]{2,1,0:T(8,128)(2,1)} %get-tuple-element.158), channel_id=1, source_target_pairs={{0,4},{4,0},{1,5},{5,1},{2,6},{6,2},{3,7},{7,3},{8,12},{12,8},{9,1... | collective-permute-start | bytes 3538952 | tf_op jit(solution)/shard_map/ppermute | solution.py:640
  271.6 26.8 %collective-permute-start.26 = (bf16[512,1024]{1,0:T(8,128)(2,1)}, bf16[512,1024]{1,0:T(8,128)(2,1)S(1)}, u32[]{:S(2)}, u32[]{:S(2)}) collective-permute-start(bf16[512,1024]{1,0:T(8,128)(2,1)} %add_convert_fusion.5), channel_id=1, source_target_pairs={{0,2},{1,3},{2,0},{3,1},{4,6},{5,7},{6,4},{7,5},{8,10},{9,11},{10,... | collective-permute-start | bytes 3145736 | tf_op jit(solution)/shard_map/ppermute | solution.py:637
  299.7 71.2 %reduce-scatter.10.cloned.1.call-start = ((), (), s32[]{:S(2)}) async-start(), calls=%async_computation.7 | async-start | bytes 1474560 | tf_op jit(solution)/shard_map/reduce_scatter | solution.py:763
  299.8 27.6 %collective-permute-start.27 = (bf16[4,128,1152]{2,1,0:T(8,128)(2,1)}, bf16[4,128,1152]{2,1,0:T(8,128)(2,1)}, u32[]{:S(2)}, u32[]{:S(2)}) collective-permute-start(bf16[4,128,1152]{2,1,0:T(8,128)(2,1)} %get-tuple-element.167), channel_id=1, source_target_pairs={{0,4},{4,0},{1,5},{5,1},{2,6},{6,2},{3,7},{7,3},{8,12},{12,8},{9,1... | collective-permute-start | bytes 3538952 | tf_op jit(solution)/shard_map/ppermute | solution.py:640
  301.3 28.7 %collective-permute-start.29 = (bf16[512,1024]{1,0:T(8,128)(2,1)}, bf16[512,1024]{1,0:T(8,128)(2,1)}, u32[]{:S(2)}, u32[]{:S(2)}) collective-permute-start(bf16[512,1024]{1,0:T(8,128)(2,1)} %get-tuple-element.175), channel_id=1, source_target_pairs={{0,1},{1,0},{2,3},{3,2},{4,5},{5,4},{6,7},{7,6},{8,9},{9,8},{10,11... | collective-permute-start | bytes 3145736 | tf_op jit(solution)/shard_map/ppermute | solution.py:634
  329.9 89.4 %reduce-scatter.14.cloned.1.call-start = ((), (), s32[]{:S(2)}) async-start(), calls=%async_computation.9 | async-start | bytes 327680 | tf_op jit(solution)/shard_map/reduce_scatter | solution.py:763
  332.7 24.5 %collective-permute-start.30 = (bf16[512,1024]{1,0:T(8,128)(2,1)S(1)}, bf16[512,1024]{1,0:T(8,128)(2,1)}, u32[]{:S(2)}, u32[]{:S(2)}) collective-permute-start(bf16[512,1024]{1,0:T(8,128)(2,1)S(1)} %add_convert_fusion.3), channel_id=1, source_target_pairs={{0,0},{1,5},{2,2},{3,7},{4,4},{5,1},{6,6},{7,3},{8,8},{9,13},{10,1... | collective-permute-start | bytes 3145736 | tf_op jit(solution)/shard_map/ppermute | solution.py:649
  334.6 22.5 %collective-permute-start.28 = (bf16[8,128,256]{2,1,0:T(8,128)(2,1)S(1)}, bf16[8,128,256]{2,1,0:T(8,128)(2,1)S(1)}, u32[]{:S(2)}, u32[]{:S(2)}) collective-permute-start(bf16[8,128,256]{2,1,0:T(8,128)(2,1)S(1)} %slice.165), channel_id=1, source_target_pairs={{0,2},{1,3},{2,0},{3,1},{4,6},{5,7},{6,4},{7,5},{8,10},{9,11},{10,... | collective-permute-start | bytes 1572872 | tf_op jit(solution)/shard_map/ppermute | solution.py:637
  336.3 34.5 %collective-permute-start.32 = (bf16[8,128,512]{2,1,0:T(8,128)(2,1)S(1)}, bf16[8,128,512]{2,1,0:T(8,128)(2,1)S(1)}, u32[]{:S(2)}, u32[]{:S(2)}) collective-permute-start(bf16[8,128,512]{2,1,0:T(8,128)(2,1)S(1)} %pad_maximum_fusion.4), channel_id=1, source_target_pairs={{0,2},{1,3},{2,0},{3,1},{4,6},{5,7},{6,4},{7,5},{8,10},{9,11},{10,... | collective-permute-start | bytes 3145736 | tf_op jit(solution)/shard_map/ppermute | solution.py:637
  357.3 13.5 %collective-permute-start.31 = (bf16[4,128,256]{2,1,0:T(8,128)(2,1)S(1)}, bf16[4,128,256]{2,1,0:T(8,128)(2,1)S(1)}, u32[]{:S(2)}, u32[]{:S(2)}) collective-permute-start(bf16[4,128,256]{2,1,0:T(8,128)(2,1)S(1)} %slice.167), channel_id=1, source_target_pairs={{0,4},{4,0},{1,5},{5,1},{2,6},{6,2},{3,7},{7,3},{8,12},{12,8},{9,1... | collective-permute-start | bytes 786440 | tf_op jit(solution)/shard_map/ppermute | solution.py:640
  376.5 8.8 %collective-permute-start.33 = (bf16[1024,1024]{1,0:T(8,128)(2,1)}, bf16[1024,1024]{1,0:T(8,128)(2,1)}, u32[]{:S(2)}, u32[]{:S(2)}) collective-permute-start(bf16[1024,1024]{1,0:T(8,128)(2,1)} %unproject.1), channel_id=1, source_target_pairs={{0,1},{1,0},{2,3},{3,2},{4,5},{5,4},{6,7},{7,6},{8,9},{9,8},{10,11... | collective-permute-start | bytes 6291464 | tf_op jit(solution)/shard_map/ppermute | solution.py:634
  385.3 17.3 %collective-permute-start.35 = (bf16[4,128,640]{2,1,0:T(8,128)(2,1)S(1)}, bf16[4,128,640]{2,1,0:T(8,128)(2,1)}, u32[]{:S(2)}, u32[]{:S(2)}) collective-permute-start(bf16[4,128,640]{2,1,0:T(8,128)(2,1)S(1)} %pad_maximum_fusion.7), channel_id=1, source_target_pairs={{0,4},{4,0},{1,5},{5,1},{2,6},{6,2},{3,7},{7,3},{8,12},{12,8},{9,1... | collective-permute-start | bytes 1966088 | tf_op jit(solution)/shard_map/ppermute | solution.py:640
  385.9 25.6 %collective-permute-start.36 = (bf16[512,1024]{1,0:T(8,128)(2,1)}, bf16[512,1024]{1,0:T(8,128)(2,1)}, u32[]{:S(2)}, u32[]{:S(2)}) collective-permute-start(bf16[512,1024]{1,0:T(8,128)(2,1)} %collective-permute-done.30.a_ref), channel_id=1, source_target_pairs={{0,2},{1,3},{2,0},{3,1},{4,6},{5,7},{6,4},{7,5},{8,10},{9,11},{10,... | collective-permute-start | bytes 3145736 | tf_op jit(solution)/shard_map/ppermute | solution.py:637
  388.1 48.1 %reduce-scatter.12.cloned.1.call-start = ((), (), s32[]{:S(2)}) async-start(), calls=%async_computation.8 | async-start | bytes 819200 | tf_op jit(solution)/shard_map/reduce_scatter | solution.py:763
  404.7 8.9 %collective-permute-start.37 = (bf16[512,1024]{1,0:T(8,128)(2,1)}, bf16[512,1024]{1,0:T(8,128)(2,1)S(1)}, u32[]{:S(2)}, u32[]{:S(2)}) collective-permute-start(bf16[512,1024]{1,0:T(8,128)(2,1)} %collective-permute-done.30.a_ref), channel_id=1, source_target_pairs={{0,1},{1,0},{2,3},{3,2},{4,5},{5,4},{6,7},{7,6},{8,9},{9,8},{10,11... | collective-permute-start | bytes 3145736 | tf_op jit(solution)/shard_map/ppermute | solution.py:634
  411.5 24.8 %collective-permute-start.34 = (bf16[512,1024]{1,0:T(8,128)(2,1)}, bf16[512,1024]{1,0:T(8,128)(2,1)}, u32[]{:S(2)}, u32[]{:S(2)}) collective-permute-start(bf16[512,1024]{1,0:T(8,128)(2,1)} %dynamic-slice_bitcast_fusion), channel_id=1, source_target_pairs={{0,4},{4,0},{1,5},{5,1},{2,6},{6,2},{3,7},{7,3},{8,12},{12,8},{9,1... | collective-permute-start | bytes 3145736 | tf_op jit(solution)/shard_map/ppermute | solution.py:640
  412.9 23.3 %collective-permute-start.38 = (bf16[512,1024]{1,0:T(8,128)(2,1)}, bf16[512,1024]{1,0:T(8,128)(2,1)}, u32[]{:S(2)}, u32[]{:S(2)}) collective-permute-start(bf16[512,1024]{1,0:T(8,128)(2,1)} %collective-permute-done.36.a_ref), channel_id=1, source_target_pairs={{0,1},{1,0},{2,3},{3,2},{4,5},{5,4},{6,7},{7,6},{8,9},{9,8},{10,11... | collective-permute-start | bytes 3145736 | tf_op jit(solution)/shard_map/ppermute | solution.py:634
  438.8 9.9 %collective-permute-start.45 = (bf16[128,640]{1,0:T(8,128)(2,1)}, bf16[128,640]{1,0:T(8,128)(2,1)S(1)}, u32[]{:S(2)}, u32[]{:S(2)}) collective-permute-start(bf16[128,640]{1,0:T(8,128)(2,1)} %bitcast.35), channel_id=1, source_target_pairs={{0,4},{4,0},{1,5},{5,1},{2,6},{6,2},{3,7},{7,3},{8,12},{12,8},{9,1... | collective-permute-start | bytes 491528 | tf_op jit(solution)/shard_map/ppermute | solution.py:640
  440.3 27.4 %collective-permute-start.40 = (bf16[512,1024]{1,0:T(8,128)(2,1)}, bf16[512,1024]{1,0:T(8,128)(2,1)}, u32[]{:S(2)}, u32[]{:S(2)}) collective-permute-start(bf16[512,1024]{1,0:T(8,128)(2,1)} %fusion.5.a_ref), channel_id=1, source_target_pairs={{0,1},{1,0},{2,3},{3,2},{4,5},{5,4},{6,7},{7,6},{8,9},{9,8},{10,11... | collective-permute-start | bytes 3145736 | tf_op jit(solution)/shard_map/ppermute | solution.py:634
  440.3 32.7 %collective-permute-start.39 = (bf16[512,1024]{1,0:T(8,128)(2,1)}, bf16[512,1024]{1,0:T(8,128)(2,1)}, u32[]{:S(2)}, u32[]{:S(2)}) collective-permute-start(bf16[512,1024]{1,0:T(8,128)(2,1)} %fusion.5.a_ref), channel_id=1, source_target_pairs={{0,2},{1,3},{2,0},{3,1},{4,6},{5,7},{6,4},{7,5},{8,10},{9,11},{10,... | collective-permute-start | bytes 3145736 | tf_op jit(solution)/shard_map/ppermute | solution.py:637
  441.8 33.2 %collective-permute-start.48 = (bf16[128,256]{1,0:T(8,128)(2,1)}, bf16[128,256]{1,0:T(8,128)(2,1)}, u32[]{:S(2)}, u32[]{:S(2)}) collective-permute-start(bf16[128,256]{1,0:T(8,128)(2,1)} %bitcast.36), channel_id=1, source_target_pairs={{0,4},{4,0},{1,5},{5,1},{2,6},{6,2},{3,7},{7,3},{8,12},{12,8},{9,1... | collective-permute-start | bytes 196616 | tf_op jit(solution)/shard_map/ppermute | solution.py:640
  442.3 19.2 %collective-permute-start.41 = (bf16[128,1152]{1,0:T(8,128)(2,1)S(1)}, bf16[128,1152]{1,0:T(8,128)(2,1)S(1)}, u32[]{:S(2)}, u32[]{:S(2)}) collective-permute-start(bf16[128,1152]{1,0:T(8,128)(2,1)S(1)} %bitcast.121), channel_id=1, source_target_pairs={{0,4},{4,0},{1,5},{5,1},{2,6},{6,2},{3,7},{7,3},{8,12},{12,8},{9,1... | collective-permute-start | bytes 884744 | tf_op jit(solution)/shard_map/ppermute | solution.py:640
  448.7 10.1 %collective-permute-start.43 = (bf16[128,1152]{1,0:T(8,128)(2,1)S(1)}, bf16[128,1152]{1,0:T(8,128)(2,1)S(1)}, u32[]{:S(2)}, u32[]{:S(2)}) collective-permute-start(bf16[128,1152]{1,0:T(8,128)(2,1)S(1)} %bitcast.123), channel_id=1, source_target_pairs={{0,4},{4,0},{1,5},{5,1},{2,6},{6,2},{3,7},{7,3},{8,12},{12,8},{9,1... | collective-permute-start | bytes 884744 | tf_op jit(solution)/shard_map/ppermute | solution.py:640
  458.9 8.4 %collective-permute-start.42 = (bf16[128,1152]{1,0:T(8,128)(2,1)S(1)}, bf16[128,1152]{1,0:T(8,128)(2,1)S(1)}, u32[]{:S(2)}, u32[]{:S(2)}) collective-permute-start(bf16[128,1152]{1,0:T(8,128)(2,1)S(1)} %bitcast.122), channel_id=1, source_target_pairs={{0,4},{4,0},{1,5},{5,1},{2,6},{6,2},{3,7},{7,3},{8,12},{12,8},{9,1... | collective-permute-start | bytes 884744 | tf_op jit(solution)/shard_map/ppermute | solution.py:640
  474.3 7.2 %collective-permute-start.44 = (bf16[512,1024]{1,0:T(8,128)(2,1)}, bf16[512,1024]{1,0:T(8,128)(2,1)S(1)}, u32[]{:S(2)}, u32[]{:S(2)}) collective-permute-start(bf16[512,1024]{1,0:T(8,128)(2,1)} %collective-permute-done.39.a_ref), channel_id=1, source_target_pairs={{0,1},{1,0},{2,3},{3,2},{4,5},{5,4},{6,7},{7,6},{8,9},{9,8},{10,11... | collective-permute-start | bytes 3145736 | tf_op jit(solution)/shard_map/ppermute | solution.py:634
  (58 other events, 351.8 us)
Sparse Core Ops, SparseCore 0:
  10.2 52.8 all-gather.6
  64.7 28.4 all-gather.8
  107.1 51.3 all-gather.10
  270.1 27.9 reduce-scatter.5
  300.9 27.8 reduce-scatter.7
  331.5 27.8 reduce-scatter.9
  388.3 17.5 reduce-scatter.13
  408.8 20.3 reduce-scatter.11
